TPU v7x, 256 devices: a whole 4x4x8 slice. The times are simulated.
256 devices in a mesh: gx: 64 (over x, z, core), af: 4 (over y).
Axes of the slice: x: 4, y: 4, z: 8, core: 2. Of those that a mesh axis runs over, the one named last changes fastest.
Arguments:
- scalar_field: float32 [128, 512, 512], P('gx', 'af'), may hold values from -256 to 256
- plane_sketch: float32 [128, 2, 256], P('gx'), may hold values from -0.5 to 0.5
- second_sketch: float32 [512, 256], P('af'), may hold values from -0.25 to 0.25
- third_sketch: float32 [512, 256], replicated, may hold values from -0.25 to 0.25
- mixing: float32 [2, 256, 128], replicated, may hold values from -0.375 to 0.375
- plane_targets: int32 [128, 2], replicated, may hold values from 0 to 7
- plane_signs: int32 [128, 2], replicated, may hold values from 0 to 1
Outputs:
- factor_second: float32 [512, 128], P(('af', 'gx'))
- factor_third: float32 [512, 128], P(('gx', 'af'))
- core_sketch: float32 [128, 128, 128], P('gx', 'af')
Inputs may be any that keep to these rules, and one draw needn't show every extreme that they name: `plane_targets`: block id of each of a plane's two entries in the core sketch; the two may coincide. `plane_signs`: 1 stands for a plus sign, 0 for a minus sign.
All inputs are finite; a program needn't handle non-finite values.
Results may differ from a plain program's by a relative error of at most 0.0003.
Values sent between devices are 32-bit elements; how exact they have to be, the bound alone decides.
A program may use at most 64 MiB of HBM per device.

v0:
```python
import jax
import jax.numpy as jnp
from jax import lax
from jax.sharding import PartitionSpec as P

BLOCK = 16
BLOCKS = 8


precise = lax.Precision.HIGHEST


def gram_of(ranged):
    return jnp.dot(ranged.T, ranged, precision=precise)


def orthonormal_rows(ranged, gram_matrix):
    lower_factor = jnp.linalg.cholesky(gram_matrix)
    return jax.scipy.linalg.solve_triangular(lower_factor, ranged.T, lower=True).T


def selector(targets, sign_values, row_count):
    row_ids = jnp.arange(row_count, dtype=jnp.int32)
    return jnp.sum(
        jnp.where(targets[None, :, :] == row_ids[:, None, None], sign_values[None, :, :], 0.0),
        axis=2,
    )


def body(
    scalar_field, plane_sketch, second_sketch, third_sketch, mixing, plane_targets, plane_signs
):
    planes = scalar_field.shape[0]
    rank_cols = mixing.shape[2]
    along_second = jnp.einsum("pjl,lk->pjk", scalar_field, third_sketch, precision=precise)
    partial_second = jnp.einsum(
        "pjk,pk->jk", along_second, plane_sketch[:, 0, :], precision=precise
    )
    along_third = jnp.einsum("pjl,jk->plk", scalar_field, second_sketch, precision=precise)
    partial_third = jnp.einsum("plk,pk->lk", along_third, plane_sketch[:, 1, :], precision=precise)

    def finish(sketched, mode_index):
        return jnp.dot(sketched, mixing[mode_index], precision=precise)

    rows_second = finish(lax.psum_scatter(partial_second, "gx", scatter_dimension=0, tiled=True), 0)
    rows_third = finish(
        lax.psum_scatter(partial_third, ("gx", "af"), scatter_dimension=0, tiled=True), 1
    )
    gram_second, gram_third = lax.psum((gram_of(rows_second), gram_of(rows_third)), ("gx", "af"))
    factor_second = orthonormal_rows(rows_second, gram_second)
    factor_third = orthonormal_rows(rows_third, gram_third)
    basis_second = lax.all_gather(factor_second, "gx", axis=0, tiled=True)
    basis_third = lax.all_gather(factor_third, ("gx", "af"), axis=0, tiled=True)
    left_side = jnp.einsum("jr,pjl->prl", basis_second, scalar_field, precision=precise)
    projected = jnp.einsum("prl,ls->prs", left_side, basis_third, precision=precise)
    out_rows = BLOCKS * BLOCK // lax.axis_size("gx")
    plane_ids = jnp.arange(plane_targets.shape[0], dtype=jnp.int32)
    all_targets = plane_targets * BLOCK + (plane_ids % BLOCK)[:, None]
    all_signs = (2 * plane_signs - 1).astype(jnp.float32)
    first_plane = lax.axis_index("gx") * planes
    own_targets = lax.dynamic_slice_in_dim(all_targets, first_plane, planes, 0)
    own_signs = lax.dynamic_slice_in_dim(all_signs, first_plane, planes, 0)
    flattened = projected.reshape(planes, -1)
    select = selector(own_targets, own_signs, lax.axis_size("gx") * out_rows)
    partial_core = lax.psum_scatter(
        jnp.dot(select, flattened, precision=precise).reshape(
            lax.axis_size("gx") * out_rows, rank_cols, rank_cols
        ),
        "gx",
        scatter_dimension=0,
        tiled=True,
    )
    core_sketch = lax.psum_scatter(partial_core, "af", scatter_dimension=1, tiled=True)
    return (factor_second, factor_third, core_sketch)


def solution(mesh):
    in_specs = (P("gx", "af", None), P("gx", None, None), P("af", None), P(), P(), P(), P())
    out_specs = (P(("af", "gx"), None), P(("gx", "af"), None), P("gx", "af", None))
    return jax.shard_map(body, mesh=mesh, in_specs=in_specs, out_specs=out_specs, check_vma=False)
```

profile of v0, /device:TPU:32, one launch (start us, length us, event | category | flops | bytes accessed | tf_op | source)
XLA Modules:
  0.0 1100.2 jit_solution(13940723075682379421)
XLA Ops:
  7.2 0.0 copy-start
  7.2 0.0 all-reduce.9.cloned.1.call-start
  7.2 0.8 fusion.30
  8.0 0.2 copy-done
  8.2 1.6 fusion.3
  9.9 0.8 copy.63
  10.6 0.0 all-reduce.9.cloned.1.call-update
  10.7 0.0 all-reduce.11.cloned.1.call-start
  10.7 2.0 fusion.1
  12.7 1.0 copy.72
  13.7 0.0 all-reduce.11.cloned.1.call-update
  13.7 0.0 all-reduce.15.cloned.1.call-start
  13.8 1.3 dynamic-slice
  15.7 0.7 multiply_add_fusion
  16.4 0.1 constant_dynamic-slice_fusion.2
  16.5 0.1 copy.51
  16.6 0.7 add_convert_fusion
  17.3 0.1 constant_dynamic-slice_fusion.1
  17.4 0.1 copy.52
  17.5 167.8 %all-reduce.9.cloned.1.call-done = f32[128,256]{0,1:T(8,128)} async-done(((f32[128,256]{0,1:T(8,128)}), f32[128,256]{0,1:T(8,128)}) %all-reduce.9.cloned.1.call-update) | async-done | bytes 131088
  185.2 1.4 fusion.9
  186.6 0.9 fusion.31
  187.5 252.6 %all-reduce.11.cloned.1.call-done = f32[512,256]{0,1:T(8,128)} async-done(((f32[512,256]{0,1:T(8,128)}), f32[512,256]{0,1:T(8,128)}) %all-reduce.11.cloned.1.call-update) | async-done | bytes 524304
  440.1 1.4 fusion.7
  441.5 0.9 fusion.32
  442.5 0.0 all-reduce.15.cloned.1.call-update
  442.5 0.0 reduce-scatter.4.cloned.1.call-start
  442.5 0.1 fusion.24
  442.6 244.5 %all-reduce.15.cloned.1.call-done = (f32[128,128]{0,1:T(8,128)}, f32[128,128]{0,1:T(8,128)}) async-done(((f32[128,128]{0,1:T(8,128)}, f32[128,128]{0,1:T(8,128)}), (f32[128,128]{0,1:T(8,128)}, f32[128,128]{0,1:T(8,128)})) %all-reduce.15.cloned.1.call-update) | async-done | bytes 131088 | tf_op jit(solution)/shard_map/psum | solution.py:49
  687.2 0.9 copy.47
  688.1 0.9 fusion.23
  689.0 11.7 %cholesky.44 = f32[128,128]{1,0:T(8,128)S(1)} custom-call(f32[128,128]{1,0:T(8,128)S(1)} %fusion.23), custom_call_target="Cholesky" | custom-call | tf_op jit(solution)/shard_map/jit(cholesky)/cholesky | solution.py:18
  700.7 0.6 compare_reduce_fusion.1
  701.3 0.7 fusion.16
  702.0 9.8 custom-call.6
  711.8 0.2 fusion.21
  712.0 0.0 copy-start.1
  712.0 42.7 %all-gather = f32[64,2,128]{2,1,0:T(2,128)S(1)} all-gather(f32[1,2,128]{2,1,0:T(2,128)S(1)} %bitcast.107), channel_id=1, replica_groups=mesh['gx'=64,'af'=4] {'gx'}, dimensions={0}, use_global_device_ids=true | all-gather | bytes 66560 | tf_op jit(solution)/shard_map/all_gather | solution.py:52
  754.7 0.9 copy.50
  755.7 0.9 fusion.20
  756.5 11.7 %cholesky.55 = f32[128,128]{1,0:T(8,128)S(1)} custom-call(f32[128,128]{1,0:T(8,128)S(1)} %fusion.20), custom_call_target="Cholesky" | custom-call | tf_op jit(solution)/shard_map/jit(cholesky)/cholesky | solution.py:18
  768.3 0.6 compare_reduce_fusion
  768.9 0.7 fusion.17
  769.6 9.8 custom-call.7
  779.4 0.2 fusion.18
  779.6 0.0 copy-start.2
  779.6 99.2 %all-gather.1 = f32[256,2,128]{2,1,0:T(2,128)S(1)} all-gather(f32[1,2,128]{2,1,0:T(2,128)S(1)} %bitcast.109), channel_id=1, replica_groups=mesh['gx'=64,'af'=4] {'gx','af'}, dimensions={0}, use_global_device_ids=true | all-gather | bytes 263168 | tf_op jit(solution)/shard_map/all_gather | solution.py:53
  878.8 0.6 convolution_bitcast_fusion.1
  879.4 0.6 convolution_bitcast_fusion.3
  880.0 6.8 fusion.5
  886.8 8.1 copy.54
  894.8 0.0 copy-done.1
  894.8 0.0 copy-done.2
  894.8 0.0 copy-start.3
  894.8 0.0 reduce-scatter.4.cloned.1.call-update
  894.9 0.0 all-reduce.13.cloned.1.call-start
  894.9 149.6 %reduce-scatter.4.cloned.1.call-done = f32[2,128,128]{2,1,0:T(8,128)} async-done(((f32[128,128,128]{2,1,0:T(8,128)}), f32[2,128,128]{2,1,0:T(8,128)}) %reduce-scatter.4.cloned.1.call-update) | async-done | bytes 131088 | tf_op jit(solution)/shard_map/reduce_scatter | solution.py:65
  1044.5 1.6 copy.55
  1046.2 0.0 all-reduce.13.cloned.1.call-update
  1046.2 0.0 copy-done.3
  1046.2 0.6 dynamic-slice.3
  1047.4 44.8 %all-reduce.13.cloned.1.call-done = f32[2,128,128]{2,0,1:T(2,128)} async-done(((f32[2,128,128]{2,0,1:T(2,128)}), f32[2,128,128]{2,0,1:T(2,128)}) %all-reduce.13.cloned.1.call-update) | async-done | bytes 131088
  1092.3 0.8 constant_dynamic-slice_fusion
  1093.0 0.6 copy.56
  (4 shorter events, 0.1 us)
Async XLA Ops:
  7.2 1.1 copy-start
  7.2 178.0 %all-reduce.9.cloned.1.call-start = ((), (), s32[]{:S(2)}) async-start(), calls=%async_computation.2 | async-start | bytes 262144
  10.7 429.5 %all-reduce.11.cloned.1.call-start = ((), (), s32[]{:S(2)}) async-start(), calls=%async_computation.3 | async-start | bytes 1048576
  13.7 673.4 %all-reduce.15.cloned.1.call-start = ((), (), s32[]{:S(2)}) async-start(), calls=%async_computation.5 | async-start | bytes 262144 | tf_op jit(solution)/shard_map/psum | solution.py:49
  442.5 602.0 %reduce-scatter.4.cloned.1.call-start = ((), (), s32[]{:S(2)}) async-start(), calls=%async_computation.1 | async-start | bytes 8519680 | tf_op jit(solution)/shard_map/reduce_scatter | solution.py:65
  712.0 182.8 %copy-start.1 = (f32[128,2]{0,1:T(2,128)}, f32[128,2]{0,1:T(2,128)S(1)}, u32[]{:S(2)}) copy-start(f32[128,2]{0,1:T(2,128)S(1)} %fusion.21) | copy-start | bytes 3076
  779.6 115.3 %copy-start.2 = (f32[128,2]{0,1:T(2,128)}, f32[128,2]{0,1:T(2,128)S(1)}, u32[]{:S(2)}) copy-start(f32[128,2]{0,1:T(2,128)S(1)} %fusion.18) | copy-start | bytes 3076
  894.8 151.4 %copy-start.3 = (u32[256]{0:T(256)S(1)}, u32[256]{0:T(256)}, u32[]{:S(2)}) copy-start(u32[256]{0:T(256)} %constant.78) | copy-start | bytes 3076
  894.9 197.4 %all-reduce.13.cloned.1.call-start = ((), (), s32[]{:S(2)}) async-start(), calls=%async_computation.4 | async-start | bytes 262144
Sparse Core Ops, SparseCore 0:
  11.5 173.6 all-reduce.8
  190.7 249.4 all-reduce.10
  445.7 241.3 all-reduce.14
  895.0 149.4 reduce-scatter.3
  1046.8 45.4 all-reduce.12
where the time goes:
time: 1100 us
  waiting for transfers between devices  859 us (78%)
  blocking collectives  142 us (13%)
  other arithmetic  48.9 us (4%)
  local copies, waits for them, and re-layouts  17.9 us (2%)
  matrix products  16.6 us (2%)
  between operations  15.2 us (1%)
    unnamed x8, waiting for transfers between devices  465 us
    psum x1, waiting for transfers between devices, body(): lax.psum((gram_of(rows_second), gram_of(rows_third)), ('gx', 'af'))  245 us
    reduce_scatter x1, waiting for transfers between devices, body(): lax.psum_scatter(jnp.dot(select, flattened, precision=precise).reshape(la...  150 us
    all_gather x1, blocking collectives, body(): basis_third = lax.all_gather(factor_third, ('gx', 'af'), axis=0, tiled=True)  99.2 us
    all_gather x1, blocking collectives, body(): basis_second = lax.all_gather(factor_second, 'gx', axis=0, tiled=True)  42.7 us
    another operation x6, other arithmetic, orthonormal_rows(): lower_factor = jnp.linalg.cholesky(gram_matrix)  24.8 us
  transfers between devices with their start and end apart: 5, of which 5 were waited for; matrix products, arithmetic and copies ran while one was open for 1% of the time, Pallas kernels for 0%

commit v1 on v0

v1 whole, which is shorter than its diff:
```python
import jax
import jax.numpy as jnp
from jax import lax
from jax.sharding import PartitionSpec as P

BLOCK = 16
BLOCKS = 8


precise = lax.Precision.HIGHEST


def gram_of(ranged):
    return jnp.dot(ranged.T, ranged, precision=precise)


def orthonormal_rows(ranged, gram_matrix):
    lower_factor = jnp.linalg.cholesky(gram_matrix)
    return jax.scipy.linalg.solve_triangular(lower_factor, ranged.T, lower=True).T


def selector(targets, sign_values, row_count):
    row_ids = jnp.arange(row_count, dtype=jnp.int32)
    return jnp.sum(
        jnp.where(targets[None, :, :] == row_ids[:, None, None], sign_values[None, :, :], 0.0),
        axis=2,
    )


def body(
    scalar_field, plane_sketch, second_sketch, third_sketch, mixing, plane_targets, plane_signs
):
    planes, rows, cells = scalar_field.shape
    rank_cols = mixing.shape[2]
    gx_index = lax.axis_index("gx")
    af_index = lax.axis_index("af")
    gx_size = lax.axis_size("gx")
    af_size = lax.axis_size("af")

    along_second = jnp.einsum("pjl,lk->pjk", scalar_field, third_sketch, precision=precise)
    partial_second = jnp.einsum(
        "pjk,pk->jk", along_second, plane_sketch[:, 0, :], precision=precise
    )
    along_third = jnp.einsum("pjl,jk->plk", scalar_field, second_sketch, precision=precise)
    partial_third = jnp.einsum("plk,pk->lk", along_third, plane_sketch[:, 1, :], precision=precise)

    range_second_block = jnp.dot(partial_second, mixing[0], precision=precise)
    range_third = jnp.dot(partial_third, mixing[1], precision=precise)
    full_rows = rows * af_size
    range_second = lax.dynamic_update_slice_in_dim(
        jnp.zeros((full_rows, rank_cols), jnp.float32), range_second_block, af_index * rows, 0
    )
    both = lax.psum(jnp.stack([range_second, range_third]), ("gx", "af"))
    rows_second, rows_third = both[0], both[1]

    factor_second_all = orthonormal_rows(rows_second, gram_of(rows_second))
    factor_third_all = orthonormal_rows(rows_third, gram_of(rows_third))

    out_second = full_rows // (gx_size * af_size)
    factor_second = lax.dynamic_slice_in_dim(
        factor_second_all, (af_index * gx_size + gx_index) * out_second, out_second, 0
    )
    factor_third = lax.dynamic_slice_in_dim(
        factor_third_all, (gx_index * af_size + af_index) * out_second, out_second, 0
    )
    basis_second = lax.dynamic_slice_in_dim(factor_second_all, af_index * rows, rows, 0)
    left_side = jnp.einsum("jr,pjl->prl", basis_second, scalar_field, precision=precise)
    projected = jnp.einsum("prl,ls->prs", left_side, factor_third_all, precision=precise)
    out_rows = BLOCKS * BLOCK // gx_size
    plane_ids = jnp.arange(plane_targets.shape[0], dtype=jnp.int32)
    all_targets = plane_targets * BLOCK + (plane_ids % BLOCK)[:, None]
    all_signs = (2 * plane_signs - 1).astype(jnp.float32)
    first_plane = gx_index * planes
    own_targets = lax.dynamic_slice_in_dim(all_targets, first_plane, planes, 0)
    own_signs = lax.dynamic_slice_in_dim(all_signs, first_plane, planes, 0)
    flattened = projected.reshape(planes, -1)
    select = selector(own_targets, own_signs, gx_size * out_rows)
    partial_core = lax.psum_scatter(
        jnp.dot(select, flattened, precision=precise).reshape(
            gx_size * out_rows, rank_cols, rank_cols
        ),
        "gx",
        scatter_dimension=0,
        tiled=True,
    )
    core_sketch = lax.psum_scatter(partial_core, "af", scatter_dimension=1, tiled=True)
    return (factor_second, factor_third, core_sketch)


def solution(mesh):
    in_specs = (P("gx", "af", None), P("gx", None, None), P("af", None), P(), P(), P(), P())
    out_specs = (P(("af", "gx"), None), P(("gx", "af"), None), P("gx", "af", None))
    return jax.shard_map(body, mesh=mesh, in_specs=in_specs, out_specs=out_specs, check_vma=False)
```

time: 1100 us -> 545 us (0.50)
  waiting for transfers between devices: 859 us -> 445 us
  blocking collectives: 142 us -> 0 us
    unnamed x8 -> x4, waiting for transfers between devices: 465 us -> 44.8 us
    all_gather x2 -> x0, blocking collectives: 142 us -> none  [the longest x1 99.2 us: body(): basis_third = lax.all_gather(factor_third, ('gx', 'af'), axis=0, tiled=True)]
  transfers between devices with their start and end apart: 5 -> 3, of which waited for: 5 -> 3; matrix products, arithmetic and copies ran while one was open for 1% -> 1% of each run, Pallas kernels for 0% -> 0%
where the time goes in v1:
time: 545 us; the launch traced here: 544 us
  waiting for transfers between devices  445 us (82%)
  other arithmetic  48.2 us (9%)
  matrix products  20.2 us (4%)
  local copies, waits for them, and re-layouts  15.5 us (3%)
  between operations  14.6 us (3%)
    psum x1, waiting for transfers between devices, body(): both = lax.psum(jnp.stack([range_second, range_third]), ('gx', 'af'))  250 us
    reduce_scatter x1, waiting for transfers between devices, body(): lax.psum_scatter(jnp.dot(select, flattened, precision=precise).reshape(gx...  150 us
    unnamed x4, waiting for transfers between devices  44.8 us
    another operation x6, other arithmetic, orthonormal_rows(): lower_factor = jnp.linalg.cholesky(gram_matrix)  24.8 us
    another operation x4, other arithmetic, orthonormal_rows(): jax.scipy.linalg.solve_triangular(lower_factor, ranged.T, lower=True)  21.1 us
  transfers between devices with their start and end apart: 3, of which 3 were waited for; matrix products, arithmetic and copies ran while one was open for 1% of the time, Pallas kernels for 0%

profile of v1, /device:TPU:32, one launch (start us, length us, event | category | flops | bytes accessed | tf_op | source)
XLA Modules:
  0.0 544.0 jit_solution(9497696338969925887)
XLA Ops:
  7.2 0.0 copy-start
  7.2 0.0 all-reduce.4.cloned.1.call-start
  7.2 0.8 fusion.37
  8.0 0.2 copy-done
  8.2 2.0 fusion.1
  10.2 1.5 convolution_bitcast_fusion.2
  11.7 1.6 fusion.3
  13.4 1.2 fusion.4
  14.6 0.8 pad_maximum_fusion
  15.4 0.0 all-reduce.4.cloned.1.call-update
  15.4 0.2 reduce-scatter.2.cloned.1.call-start
  15.7 0.7 add_convert_fusion
  16.4 0.7 multiply_add_fusion
  17.1 0.1 constant_dynamic-slice_fusion
  17.1 0.1 copy.38
  17.2 0.1 constant_dynamic-slice_fusion.1
  17.3 0.1 copy.37
  17.4 0.1 fusion.34
  17.5 250.5 %all-reduce.4.cloned.1.call-done = f32[2,512,128]{2,1,0:T(8,128)} async-done(((f32[2,512,128]{2,1,0:T(8,128)}), f32[2,512,128]{2,1,0:T(8,128)}) %all-reduce.4.cloned.1.call-update) | async-done | bytes 524304 | tf_op jit(solution)/shard_map/psum | solution.py:53
  268.0 1.6 fusion.13
  269.6 0.1 copy.35
  269.7 11.7 %cholesky.44 = f32[128,128]{1,0:T(8,128)S(1)} custom-call(f32[128,128]{1,0:T(8,128)S(1)} %fusion.32), custom_call_target="Cholesky" | custom-call | tf_op jit(solution)/shard_map/jit(cholesky)/cholesky | solution.py:18
  281.5 0.6 compare_reduce_fusion.1
  282.1 0.7 fusion.26
  282.8 9.8 %custom-call.6 = f32[1,128,128]{1,2,0:T(8,128)S(1)} custom-call(f32[1,128,128]{2,1,0:T(8,128)S(1)} %fusion.26), custom_call_target="InvertDiagBlocksLowerTriangular" | custom-call | tf_op jit(solution)/shard_map/jit(_solve_triangular)/triangular_solve | solution.py:19
  292.6 1.6 fusion.11
  294.2 0.1 copy.36
  294.3 11.7 %cholesky.55 = f32[128,128]{1,0:T(8,128)S(1)} custom-call(f32[128,128]{1,0:T(8,128)S(1)} %fusion.30), custom_call_target="Cholesky" | custom-call | tf_op jit(solution)/shard_map/jit(cholesky)/cholesky | solution.py:18
  306.1 0.6 compare_reduce_fusion
  306.7 0.7 fusion.27
  307.4 10.0 %custom-call.7 = f32[1,128,128]{1,2,0:T(8,128)S(1)} custom-call(f32[1,128,128]{2,1,0:T(8,128)S(1)} %fusion.27), custom_call_target="InvertDiagBlocksLowerTriangular" | custom-call | tf_op jit(solution)/shard_map/jit(_solve_triangular)/triangular_solve | solution.py:19
  317.4 1.4 fusion.8
  318.8 0.6 convolution_bitcast_fusion.1
  319.4 1.4 fusion.6
  320.7 0.6 convolution_bitcast_fusion.4
  321.3 6.8 %fusion.19 = f32[128,128,128]{2,0,1:T(8,128)S(1)} fusion(f32[1,2,128,128]{3,2,1,0:T(8,128)S(1)} %convolution_bitcast_fusion.4, f32[128,2]{0,1:T(2,128)S(1)} %fusion.34), kind=kOutput, calls=%fused_computation.27 | convolution fusion | flops 50331648 | bytes 8520704 | tf_op jit(solution)/shard_map/dot_general | solution.py:79
  328.1 8.3 %copy.39 = f32[128,128,128]{2,1,0:T(8,128)} copy(f32[128,128,128]{2,0,1:T(8,128)S(1)} %fusion.19) | data formatting | bytes 16777216 | tf_op jit(solution)/shard_map/dot_general | solution.py:79
  336.4 0.0 copy-start.1
  336.4 0.0 reduce-scatter.2.cloned.1.call-update
  336.5 0.0 all-reduce.6.cloned.1.call-start
  336.5 0.6 copy-done.1
  337.1 0.6 dynamic-slice.12
  338.3 149.8 %reduce-scatter.2.cloned.1.call-done = f32[2,128,128]{2,1,0:T(8,128)} async-done(((f32[128,128,128]{2,1,0:T(8,128)}), f32[2,128,128]{2,1,0:T(8,128)}) %reduce-scatter.2.cloned.1.call-update) | async-done | bytes 131088 | tf_op jit(solution)/shard_map/reduce_scatter | solution.py:78
  488.1 1.6 copy.40
  489.8 0.0 all-reduce.6.cloned.1.call-update
  489.8 0.1 dynamic-slice_bitcast_fusion.1
  489.9 0.6 copy.41
  490.5 0.1 dynamic-slice_bitcast_fusion
  490.6 0.6 copy.42
  491.3 44.8 %all-reduce.6.cloned.1.call-done = f32[2,128,128]{2,0,1:T(2,128)} async-done(((f32[2,128,128]{2,0,1:T(2,128)}), f32[2,128,128]{2,0,1:T(2,128)}) %all-reduce.6.cloned.1.call-update) | async-done | bytes 131088
  536.0 0.8 constant_dynamic-slice_fusion.2
  536.8 0.6 copy.43
  (7 shorter events, 0.1 us)
Async XLA Ops:
  7.2 1.1 copy-start
  7.2 260.8 %all-reduce.4.cloned.1.call-start = ((), (), s32[]{:S(2)}) async-start(), calls=%async_computation.1 | async-start | bytes 1048576 | tf_op jit(solution)/shard_map/psum | solution.py:53
  15.4 472.7 %reduce-scatter.2.cloned.1.call-start = ((), (), s32[]{:S(2)}) async-start(), calls=%async_computation.2 | async-start | bytes 8519680 | tf_op jit(solution)/shard_map/reduce_scatter | solution.py:78
  336.4 0.7 copy-start.1
  336.5 199.6 %all-reduce.6.cloned.1.call-start = ((), (), s32[]{:S(2)}) async-start(), calls=%async_computation.3 | async-start | bytes 262144
Sparse Core Ops, SparseCore 0:
  15.6 252.3 all-reduce.3
  336.6 151.5 reduce-scatter.1
  490.5 45.4 all-reduce.5

commit v2 on v1

--- a/solution.py
+++ b/solution.py
@@ -1,7 +1,13 @@
+import functools
+
 import jax
 import jax.numpy as jnp
 from jax import lax
+from jax.experimental import pallas as pl
+from jax.experimental.pallas import tpu as pltpu
 from jax.sharding import PartitionSpec as P
+
+MESH = pl.DeviceIdType.MESH
 
 BLOCK = 16
 BLOCKS = 8
@@ -17,6 +23,64 @@
 def orthonormal_rows(ranged, gram_matrix):
     lower_factor = jnp.linalg.cholesky(gram_matrix)
     return jax.scipy.linalg.solve_triangular(lower_factor, ranged.T, lower=True).T
+
+
+def partner_list(gx_size, af_size):
+    steps = []
+    bit = 1
+    while bit < gx_size:
+        steps.append(("gx", bit))
+        bit *= 2
+    bit = 1
+    while bit < af_size:
+        steps.append(("af", bit))
+        bit *= 2
+    return steps
+
+
+def allreduce_kernel(steps, x_ref, o_ref, recv, send_sem, recv_sem):
+    g = lax.axis_index("gx")
+    a = lax.axis_index("af")
+
+    def partner(axis, bit):
+        if axis == "gx":
+            return (lax.bitwise_xor(g, bit), a)
+        return (g, lax.bitwise_xor(a, bit))
+
+    barrier = pltpu.get_barrier_semaphore()
+    for axis, bit in steps:
+        pl.semaphore_signal(barrier, inc=1, device_id=partner(axis, bit), device_id_type=MESH)
+    pl.semaphore_wait(barrier, len(steps))
+
+    o_ref[...] = x_ref[...]
+    for s, (axis, bit) in enumerate(steps):
+        copy = pltpu.make_async_remote_copy(
+            src_ref=o_ref,
+            dst_ref=recv.at[s],
+            send_sem=send_sem.at[s],
+            recv_sem=recv_sem.at[s],
+            device_id=partner(axis, bit),
+            device_id_type=MESH,
+        )
+        copy.start()
+        copy.wait()
+        o_ref[...] = o_ref[...] + recv[s]
+
+
+def allreduce_all(x):
+    steps = partner_list(lax.axis_size("gx"), lax.axis_size("af"))
+    return pl.pallas_call(
+        functools.partial(allreduce_kernel, steps),
+        out_shape=jax.ShapeDtypeStruct(x.shape, x.dtype),
+        in_specs=[pl.BlockSpec(memory_space=pltpu.VMEM)],
+        out_specs=pl.BlockSpec(memory_space=pltpu.VMEM),
+        scratch_shapes=[
+            pltpu.VMEM((len(steps),) + x.shape, x.dtype),
+            pltpu.SemaphoreType.DMA((len(steps),)),
+            pltpu.SemaphoreType.DMA((len(steps),)),
+        ],
+        compiler_params=pltpu.CompilerParams(collective_id=0, has_side_effects=True),
+    )(x)
 
 
 def selector(targets, sign_values, row_count):
@@ -50,8 +114,8 @@
     range_second = lax.dynamic_update_slice_in_dim(
         jnp.zeros((full_rows, rank_cols), jnp.float32), range_second_block, af_index * rows, 0
     )
-    both = lax.psum(jnp.stack([range_second, range_third]), ("gx", "af"))
-    rows_second, rows_third = both[0], both[1]
+    both = allreduce_all(jnp.concatenate([range_second, range_third], axis=0))
+    rows_second, rows_third = both[:full_rows], both[full_rows:]
 
     factor_second_all = orthonormal_rows(rows_second, gram_of(rows_second))
     factor_third_all = orthonormal_rows(rows_third, gram_of(rows_third))

time: 545 us -> 413 us (0.76)
  waiting for transfers between devices: 445 us -> 200 us
  Pallas kernels: 0 us -> 116 us
    psum x1 -> x0, waiting for transfers between devices: 250 us -> none  [body(): both = lax.psum(jnp.stack([range_second, range_third]), ('gx', 'af'))]
    pallas_call x0 -> x1, Pallas kernels: none -> 116 us  [allreduce_all(): pl.pallas_call(functools.partial(allreduce_kernel, steps), out_shape=jax....]
    reduce_scatter x1, waiting for transfers between devices: 150 us -> 156 us  [body(): lax.psum_scatter(jnp.dot(select, flattened, precision=precise).reshape(gx...]
    unnamed x4 -> x3, waiting for transfers between devices: 44.8 us -> 43.5 us
  transfers between devices with their start and end apart: 3 -> 2, of which waited for: 3 -> 2; matrix products, arithmetic and copies ran while one was open for 1% -> 0% of each run, Pallas kernels for 0% -> 0%
where the time goes in v2:
time: 413 us
  waiting for transfers between devices  200 us (48%)
  Pallas kernels  116 us (28%)
  other arithmetic  46.8 us (11%)
  matrix products  20.4 us (5%)
  between operations  14.9 us (4%)
  local copies, waits for them, and re-layouts  14.7 us (4%)
    reduce_scatter x1, waiting for transfers between devices, body(): lax.psum_scatter(jnp.dot(select, flattened, precision=precise).reshape(gx...  156 us
    pallas_call x1, Pallas kernels, allreduce_all(): pl.pallas_call(functools.partial(allreduce_kernel, steps), out_shape=jax....  116 us
    unnamed x3, waiting for transfers between devices  43.5 us
    another operation x6, other arithmetic, orthonormal_rows(): lower_factor = jnp.linalg.cholesky(gram_matrix)  24.9 us
    another operation x4, other arithmetic, orthonormal_rows(): jax.scipy.linalg.solve_triangular(lower_factor, ranged.T, lower=True)  20.9 us
  transfers between devices with their start and end apart: 2, of which 2 were waited for; matrix products, arithmetic and copies ran while one was open for 0% of the time, Pallas kernels for 0%

profile of v2, /device:TPU:32, one launch (start us, length us, event | category | flops | bytes accessed | tf_op | source)
XLA Modules:
  0.0 412.6 jit_solution(14986173758069673982)
XLA Ops:
  7.2 0.0 copy-start
  7.2 0.0 copy-start.1
  7.2 0.0 copy-start.2
  7.2 0.0 reduce-scatter.2.cloned.1.call-start
  7.2 0.8 fusion.35
  8.0 0.2 copy-done
  8.2 2.0 fusion.1
  10.2 1.5 fusion.18
  11.7 1.6 fusion.3
  13.4 1.2 convolution_dynamic-update-slice_fusion
  14.6 0.8 pad_maximum_fusion.x_ref
  15.4 116.0 %shard_map.94 = f32[1024,128]{1,0:T(8,128)} custom-call(f32[1024,128]{1,0:T(8,128)} %pad_maximum_fusion.x_ref), custom_call_target="tpu_custom_call" | custom-call | tf_op jit(solution)/shard_map/pallas_call | solution.py:72
  131.4 1.6 fusion.14
  133.0 1.6 fusion.11
  134.6 0.1 copy.35
  134.8 11.7 %cholesky.44 = f32[128,128]{1,0:T(8,128)S(1)} custom-call(f32[128,128]{1,0:T(8,128)S(1)} %fusion.30), custom_call_target="Cholesky" | custom-call | tf_op jit(solution)/shard_map/jit(cholesky)/cholesky | solution.py:24
  146.5 0.6 compare_reduce_fusion.1
  147.1 0.7 fusion.24
  147.8 9.8 %custom-call.6 = f32[1,128,128]{1,2,0:T(8,128)S(1)} custom-call(f32[1,128,128]{2,1,0:T(8,128)S(1)} %fusion.24), custom_call_target="InvertDiagBlocksLowerTriangular" | custom-call | tf_op jit(solution)/shard_map/jit(_solve_triangular)/triangular_solve | solution.py:25
  157.6 1.4 fusion.8
  159.0 0.1 copy.36
  159.1 11.9 %cholesky.55 = f32[128,128]{1,0:T(8,128)S(1)} custom-call(f32[128,128]{1,0:T(8,128)S(1)} %fusion.28), custom_call_target="Cholesky" | custom-call | tf_op jit(solution)/shard_map/jit(cholesky)/cholesky | solution.py:24
  171.0 0.6 compare_reduce_fusion
  171.7 0.7 fusion.25
  172.3 9.8 %custom-call.7 = f32[1,128,128]{1,2,0:T(8,128)S(1)} custom-call(f32[1,128,128]{2,1,0:T(8,128)S(1)} %fusion.25), custom_call_target="InvertDiagBlocksLowerTriangular" | custom-call | tf_op jit(solution)/shard_map/jit(_solve_triangular)/triangular_solve | solution.py:25
  182.1 1.4 fusion.6
  183.5 0.6 convolution_bitcast_fusion.1
  184.1 0.0 copy-done.1
  184.1 0.1 constant_dynamic-slice_fusion
  184.2 0.1 copy.38
  184.3 0.0 copy-done.2
  184.3 0.1 constant_dynamic-slice_fusion.1
  184.4 0.1 copy.37
  184.5 0.6 convolution_bitcast_fusion.3
  185.1 0.1 fusion.32
  185.2 7.0 %fusion.16 = f32[128,128,128]{2,0,1:T(8,128)S(1)} fusion(f32[1,2,128,128]{3,2,1,0:T(8,128)S(1)} %convolution_bitcast_fusion.3, f32[128,2]{0,1:T(2,128)S(1)} %fusion.32), kind=kOutput, calls=%fused_computation.23 | convolution fusion | flops 50331648 | bytes 8520704 | tf_op jit(solution)/shard_map/dot_general | solution.py:143
  192.2 8.1 %copy.39 = f32[128,128,128]{2,1,0:T(8,128)} copy(f32[128,128,128]{2,0,1:T(8,128)S(1)} %fusion.16) | data formatting | bytes 16777216 | tf_op jit(solution)/shard_map/dot_general | solution.py:143
  200.3 0.0 copy-start.3
  200.3 0.0 reduce-scatter.2.cloned.1.call-update
  200.3 0.0 all-reduce.3.cloned.1.call-start
  200.3 156.1 %reduce-scatter.2.cloned.1.call-done = f32[2,128,128]{2,1,0:T(8,128)} async-done(((f32[128,128,128]{2,1,0:T(8,128)}), f32[2,128,128]{2,1,0:T(8,128)}) %reduce-scatter.2.cloned.1.call-update) | async-done | bytes 131088 | tf_op jit(solution)/shard_map/reduce_scatter | solution.py:142
  356.5 1.6 copy.40
  358.1 0.0 all-reduce.3.cloned.1.call-update
  358.1 0.1 dynamic-slice_bitcast_fusion.1
  358.2 0.6 copy.41
  358.9 0.1 dynamic-slice_bitcast_fusion
  359.0 0.6 copy.42
  359.6 0.0 copy-done.3
  359.6 0.6 dynamic-slice.12
  360.8 43.5 %all-reduce.3.cloned.1.call-done = f32[2,128,128]{2,0,1:T(2,128)} async-done(((f32[2,128,128]{2,0,1:T(2,128)}), f32[2,128,128]{2,0,1:T(2,128)}) %all-reduce.3.cloned.1.call-update) | async-done | bytes 131088
  404.3 0.8 constant_dynamic-slice_fusion.2
  405.1 0.6 copy.43
  (9 shorter events, 0.1 us)
Async XLA Ops:
  7.2 1.1 copy-start
  7.2 176.9 %copy-start.1 = (s32[128,2]{0,1:T(2,128)S(1)}, s32[128,2]{0,1:T(2,128)}, u32[]{:S(2)}) copy-start(s32[128,2]{0,1:T(2,128)} %param.16) | copy-start | bytes 3076
  7.2 177.1 %copy-start.2 = (s32[128,2]{0,1:T(2,128)S(1)}, s32[128,2]{0,1:T(2,128)}, u32[]{:S(2)}) copy-start(s32[128,2]{0,1:T(2,128)} %param.15) | copy-start | bytes 3076
  7.2 349.3 %reduce-scatter.2.cloned.1.call-start = ((), (), s32[]{:S(2)}) async-start(), calls=%async_computation.1 | async-start | bytes 8519680 | tf_op jit(solution)/shard_map/reduce_scatter | solution.py:142
  200.3 159.4 %copy-start.3 = (u32[256]{0:T(256)S(1)}, u32[256]{0:T(256)}, u32[]{:S(2)}) copy-start(u32[256]{0:T(256)} %constant.81) | copy-start | bytes 3076
  200.3 204.1 %all-reduce.3.cloned.1.call-start = ((), (), s32[]{:S(2)}) async-start(), calls=%async_computation.2 | async-start | bytes 262144
Sparse Core Ops, SparseCore 0:
  200.4 156.0 reduce-scatter.1
  358.9 45.4 all-reduce.2

commit v3 on v2

--- a/solution.py
+++ b/solution.py
@@ -83,12 +83,60 @@
     )(x)
 
 
-def selector(targets, sign_values, row_count):
-    row_ids = jnp.arange(row_count, dtype=jnp.int32)
-    return jnp.sum(
-        jnp.where(targets[None, :, :] == row_ids[:, None, None], sign_values[None, :, :], 0.0),
-        axis=2,
-    )
+def core_kernel(cycle, send_ref, o_ref, recv, send_sem, recv_sem):
+    g = lax.axis_index("gx")
+    a = lax.axis_index("af")
+    groups, af_size = send_ref.shape[0], send_ref.shape[1]
+    k = g // cycle
+    c = g % cycle
+    offsets = [(db, da) for db in range(groups) for da in range(af_size) if (db, da) != (0, 0)]
+
+    def target(db, da):
+        return ((k + db) % groups, (a + da) % af_size)
+
+    barrier = pltpu.get_barrier_semaphore()
+    for db, da in offsets:
+        tb, ta = target(db, da)
+        pl.semaphore_signal(barrier, inc=1, device_id=(tb * cycle + c, ta), device_id_type=MESH)
+    pl.semaphore_wait(barrier, len(offsets))
+
+    copies = []
+    for n, (db, da) in enumerate(offsets):
+        tb, ta = target(db, da)
+        copy = pltpu.make_async_remote_copy(
+            src_ref=send_ref.at[tb, ta],
+            dst_ref=recv.at[n],
+            send_sem=send_sem.at[n],
+            recv_sem=recv_sem.at[n],
+            device_id=(tb * cycle + c, ta),
+            device_id_type=MESH,
+        )
+        copy.start()
+        copies.append(copy)
+    for copy in copies:
+        copy.wait()
+    total = send_ref[k, a]
+    for n in range(len(offsets)):
+        total = total + recv[n]
+    o_ref[...] = total
+
+
+def core_exchange(contributions, cycle):
+    groups, af_size = contributions.shape[:2]
+    piece = contributions.shape[2:]
+    slots = groups * af_size - 1
+    return pl.pallas_call(
+        functools.partial(core_kernel, cycle),
+        out_shape=jax.ShapeDtypeStruct(piece, contributions.dtype),
+        in_specs=[pl.BlockSpec(memory_space=pltpu.VMEM)],
+        out_specs=pl.BlockSpec(memory_space=pltpu.VMEM),
+        scratch_shapes=[
+            pltpu.VMEM((slots,) + piece, contributions.dtype),
+            pltpu.SemaphoreType.DMA((slots,)),
+            pltpu.SemaphoreType.DMA((slots,)),
+        ],
+        compiler_params=pltpu.CompilerParams(collective_id=1, has_side_effects=True),
+    )(contributions)
 
 
 def body(
@@ -130,24 +178,21 @@
     basis_second = lax.dynamic_slice_in_dim(factor_second_all, af_index * rows, rows, 0)
     left_side = jnp.einsum("jr,pjl->prl", basis_second, scalar_field, precision=precise)
     projected = jnp.einsum("prl,ls->prs", left_side, factor_third_all, precision=precise)
-    out_rows = BLOCKS * BLOCK // gx_size
-    plane_ids = jnp.arange(plane_targets.shape[0], dtype=jnp.int32)
-    all_targets = plane_targets * BLOCK + (plane_ids % BLOCK)[:, None]
-    all_signs = (2 * plane_signs - 1).astype(jnp.float32)
-    first_plane = gx_index * planes
-    own_targets = lax.dynamic_slice_in_dim(all_targets, first_plane, planes, 0)
-    own_signs = lax.dynamic_slice_in_dim(all_signs, first_plane, planes, 0)
-    flattened = projected.reshape(planes, -1)
-    select = selector(own_targets, own_signs, gx_size * out_rows)
-    partial_core = lax.psum_scatter(
-        jnp.dot(select, flattened, precision=precise).reshape(
-            gx_size * out_rows, rank_cols, rank_cols
-        ),
-        "gx",
-        scatter_dimension=0,
-        tiled=True,
-    )
-    core_sketch = lax.psum_scatter(partial_core, "af", scatter_dimension=1, tiled=True)
+    cycle = BLOCK // planes
+    groups = gx_size // cycle
+    assert planes * gx_size == BLOCKS * BLOCK and groups == BLOCKS
+    own_targets = lax.dynamic_slice_in_dim(plane_targets, gx_index * planes, planes, 0)
+    own_signs = lax.dynamic_slice_in_dim(plane_signs, gx_index * planes, planes, 0)
+    sign_values = (2 * own_signs - 1).astype(jnp.float32)
+    block_ids = jnp.arange(groups, dtype=jnp.int32)
+    weights = jnp.sum(
+        jnp.where(own_targets[None, :, :] == block_ids[:, None, None], sign_values[None, :, :], 0.0),
+        axis=2,
+    )
+    slab = rank_cols // af_size
+    pieces = projected.reshape(planes, af_size, slab, rank_cols).transpose(1, 0, 2, 3)
+    contributions = weights[:, None, :, None, None] * pieces[None]
+    core_sketch = core_exchange(contributions, cycle)
     return (factor_second, factor_third, core_sketch)
 
 

time: 413 us -> 215 us (0.52)
  the two profiles are of different devices: /device:TPU:32 before, /device:TPU:4 now
where the time goes in v3:
time: 215 us
  Pallas kernels  151 us (70%)
  other arithmetic  48 us (22%)
  matrix products  8.72 us (4%)
  local copies, waits for them, and re-layouts  6.12 us (3%)
    pallas_call x1, Pallas kernels, allreduce_all(): pl.pallas_call(functools.partial(allreduce_kernel, steps), out_shape=jax....  124 us
    pallas_call x1, Pallas kernels, core_exchange(): pl.pallas_call(functools.partial(core_kernel, cycle), out_shape=jax.Shape...  26.8 us
    another operation x6, other arithmetic, orthonormal_rows(): lower_factor = jnp.linalg.cholesky(gram_matrix)  24.9 us
    another operation x4, other arithmetic, orthonormal_rows(): jax.scipy.linalg.solve_triangular(lower_factor, ranged.T, lower=True)  20.9 us
    unnamed x18, local copies, waits for them, and re-layouts  5.46 us

profile of v3, /device:TPU:4, one launch (start us, length us, event | category | flops | bytes accessed | tf_op | source)
XLA Modules:
  0.0 214.8 jit_solution(10386636492559817070)
XLA Ops:
  0.6 0.0 copy-start
  0.7 0.0 copy-start.5
  0.7 0.0 copy-start.6
  0.7 0.7 copy-done.5
  1.4 0.0 copy-done.6
  1.4 0.1 constant_dynamic-slice_fusion.1
  1.5 0.1 copy.27
  1.6 0.1 copy.28
  1.7 0.0 copy-start.4
  1.7 0.1 fusion.31
  1.8 0.1 copy.29
  1.8 0.5 copy-done.4
  2.4 0.0 copy-done
  2.4 1.6 fusion.3
  4.0 0.0 copy-start.2
  4.1 0.9 copy-done.2
  5.0 0.0 copy-start.3
  5.0 0.3 convolution_dynamic-update-slice_fusion
  5.3 0.6 copy-done.3
  5.9 1.0 fusion.1
  6.9 0.6 fusion.17
  7.5 0.8 pad_maximum_fusion.x_ref
  8.3 124.2 %shard_map.94 = f32[1024,128]{1,0:T(8,128)} custom-call(f32[1024,128]{1,0:T(8,128)} %pad_maximum_fusion.x_ref), custom_call_target="tpu_custom_call" | custom-call | tf_op jit(solution)/shard_map/pallas_call | solution.py:72
  132.5 1.6 fusion.12
  134.2 1.6 fusion.15
  135.8 0.0 copy-start.1
  135.8 0.1 copy.25
  135.9 11.7 %cholesky.44 = f32[128,128]{1,0:T(8,128)S(1)} custom-call(f32[128,128]{1,0:T(8,128)S(1)} %fusion.29), custom_call_target="Cholesky" | custom-call | tf_op jit(solution)/shard_map/jit(cholesky)/cholesky | solution.py:24
  147.6 0.6 compare_reduce_fusion.1
  148.3 0.7 fusion.23
  149.0 9.8 %custom-call.6 = f32[1,128,128]{1,2,0:T(8,128)S(1)} custom-call(f32[1,128,128]{2,1,0:T(8,128)S(1)} %fusion.23), custom_call_target="InvertDiagBlocksLowerTriangular" | custom-call | tf_op jit(solution)/shard_map/jit(_solve_triangular)/triangular_solve | solution.py:25
  158.8 0.1 copy.26
  158.9 11.9 %cholesky.55 = f32[128,128]{1,0:T(8,128)S(1)} custom-call(f32[128,128]{1,0:T(8,128)S(1)} %fusion.27), custom_call_target="Cholesky" | custom-call | tf_op jit(solution)/shard_map/jit(cholesky)/cholesky | solution.py:24
  170.8 0.6 compare_reduce_fusion
  171.4 0.7 fusion.24
  172.1 9.8 %custom-call.7 = f32[1,128,128]{1,2,0:T(8,128)S(1)} custom-call(f32[1,128,128]{2,1,0:T(8,128)S(1)} %fusion.24), custom_call_target="InvertDiagBlocksLowerTriangular" | custom-call | tf_op jit(solution)/shard_map/jit(_solve_triangular)/triangular_solve | solution.py:25
  181.9 0.0 copy-done.1
  181.9 0.4 fusion.7
  182.4 0.4 fusion.9
  182.8 0.1 dynamic-slice_bitcast_fusion.1
  182.9 0.6 copy.31
  183.5 0.1 dynamic-slice_bitcast_fusion
  183.6 0.6 copy.32
  184.2 0.6 convolution_bitcast_fusion.1
  184.8 0.6 fusion.5
  185.4 1.1 broadcast_multiply_fusion.send_ref
  186.5 26.8 %shard_map.95 = f32[2,32,128]{2,1,0:T(8,128)} custom-call(f32[8,4,2,32,128]{4,3,2,1,0:T(8,128)} %broadcast_multiply_fusion.send_ref), custom_call_target="tpu_custom_call" | custom-call | tf_op jit(solution)/shard_map/pallas_call | solution.py:128
  213.4 1.4 copy.62
  (8 shorter events, 0.1 us)
Async XLA Ops:
  0.6 1.7 copy-start
  0.7 0.7 copy-start.5
  0.7 0.7 copy-start.6
  1.7 0.7 copy-start.4
  4.0 1.0 copy-start.2
  5.0 0.9 copy-start.3
  135.8 46.2 %copy-start.1 = (f32[1024,128]{1,0:T(8,128)S(1)}, f32[1024,128]{1,0:T(8,128)}, u32[]{:S(2)}) copy-start(f32[1024,128]{1,0:T(8,128)} %shard_map.94) | copy-start | bytes 1572868

commit v4 on v3

--- a/solution.py
+++ b/solution.py
@@ -14,15 +14,6 @@
 
 
 precise = lax.Precision.HIGHEST
-
-
-def gram_of(ranged):
-    return jnp.dot(ranged.T, ranged, precision=precise)
-
-
-def orthonormal_rows(ranged, gram_matrix):
-    lower_factor = jnp.linalg.cholesky(gram_matrix)
-    return jax.scipy.linalg.solve_triangular(lower_factor, ranged.T, lower=True).T
 
 
 def partner_list(gx_size, af_size):
@@ -163,10 +154,14 @@
         jnp.zeros((full_rows, rank_cols), jnp.float32), range_second_block, af_index * rows, 0
     )
     both = allreduce_all(jnp.concatenate([range_second, range_third], axis=0))
-    rows_second, rows_third = both[:full_rows], both[full_rows:]
 
-    factor_second_all = orthonormal_rows(rows_second, gram_of(rows_second))
-    factor_third_all = orthonormal_rows(rows_third, gram_of(rows_third))
+    ranges = both.reshape(2, full_rows, rank_cols)
+    grams = jnp.einsum("nji,njk->nik", ranges, ranges, precision=precise)
+    lower_factors = jnp.linalg.cholesky(grams)
+    factors = jax.scipy.linalg.solve_triangular(
+        lower_factors, ranges.transpose(0, 2, 1), lower=True
+    ).transpose(0, 2, 1)
+    factor_second_all, factor_third_all = factors[0], factors[1]
 
     out_second = full_rows // (gx_size * af_size)
     factor_second = lax.dynamic_slice_in_dim(

time: 215 us -> 211 us (0.981)
  other arithmetic: 48 us -> 45.7 us
    another operation x10 -> x7, other arithmetic: 45.9 us -> 43.6 us  [the longest x4 23.8 us: body(): lower_factors = jnp.linalg.cholesky(grams)]
    unnamed x18 -> x16, local copies, waits for them, and re-layouts: 5.46 us -> 4.19 us
where the time goes in v4:
time: 211 us; the launch traced here: 210 us
  Pallas kernels  150 us (71%)
  other arithmetic  45.7 us (22%)
  matrix products  7.52 us (4%)
  local copies, waits for them, and re-layouts  5.76 us (3%)
    pallas_call x1, Pallas kernels, allreduce_all(): pl.pallas_call(functools.partial(allreduce_kernel, steps), out_shape=jax....  124 us
    pallas_call x1, Pallas kernels, core_exchange(): pl.pallas_call(functools.partial(core_kernel, cycle), out_shape=jax.Shape...  26.2 us
    another operation x4, other arithmetic, body(): lower_factors = jnp.linalg.cholesky(grams)  23.8 us
    another operation x3, other arithmetic, body(): jax.scipy.linalg.solve_triangular(lower_factors, ranges.transpose(0, 2, 1...  19.8 us

profile of v4, /device:TPU:4, one launch (start us, length us, event | category | flops | bytes accessed | tf_op | source)
XLA Modules:
  0.0 210.2 jit_solution(11273631656131219264)
XLA Ops:
  0.6 0.0 copy-start
  0.7 0.0 copy-start.5
  0.7 0.0 copy-start.6
  0.7 0.7 copy-done.5
  1.4 0.0 copy-done.6
  1.4 0.1 constant_dynamic-slice_fusion.1
  1.5 0.1 copy.27
  1.6 0.1 copy.28
  1.7 0.0 copy-start.4
  1.7 0.1 fusion.18
  1.8 0.1 copy.29
  1.8 0.5 copy-done.4
  2.4 0.0 copy-done
  2.4 1.6 fusion.3
  4.1 0.0 copy-start.2
  4.1 0.9 copy-done.2
  5.0 0.0 copy-start.3
  5.0 0.3 convolution_dynamic-update-slice_fusion
  5.3 0.6 copy-done.3
  5.9 1.0 fusion.1
  7.0 0.6 fusion.9
  7.5 0.8 pad_maximum_fusion.x_ref
  8.4 124.2 %shard_map.94 = f32[1024,128]{1,0:T(8,128)} custom-call(f32[1024,128]{1,0:T(8,128)} %pad_maximum_fusion.x_ref), custom_call_target="tpu_custom_call" | custom-call | tf_op jit(solution)/shard_map/pallas_call | solution.py:63
  132.6 2.2 %fusion.28 = f32[2,128,128]{2,1,0:T(8,128)S(1)} fusion(f32[2,512,128]{2,1,0:T(8,128)} %bitcast.74), kind=kOutput, calls=%fused_computation.47 | convolution fusion | flops 201326592 | bytes 655360 | tf_op jit(solution)/shard_map/nji,njk->nik/dot_general | solution.py:159
  134.8 0.0 copy-start.1
  134.8 0.1 copy.25
  134.9 23.6 %custom-call.8 = f32[2,128,128]{2,1,0:T(8,128)S(1)} custom-call(f32[2,128,128]{2,1,0:T(8,128)S(1)} %fusion.8), custom_call_target="Cholesky" | custom-call | tf_op jit(solution)/shard_map/jit(cholesky)/cholesky | solution.py:160
  158.6 0.1 compare_reduce_fusion
  158.7 0.1 select_bitcast_fusion
  158.8 19.7 %custom-call.9 = f32[2,1,128,128]{2,3,1,0:T(8,128)S(1)} custom-call(f32[2,1,128,128]{3,2,1,0:T(8,128)S(1)} %select_bitcast_fusion), custom_call_target="InvertDiagBlocksLowerTriangular" | custom-call | tf_op jit(solution)/shard_map/jit(_solve_triangular)/vmap()/triangular_solve | solution.py:161
  178.5 0.0 copy-done.1
  178.5 0.6 fusion.6
  179.2 0.6 fusion.21
  179.7 0.6 fusion.20
  180.3 0.6 fusion.15
  180.9 0.6 convolution_bitcast_fusion.2
  181.5 1.1 broadcast_multiply_fusion.send_ref
  182.7 26.2 %shard_map.95 = f32[2,32,128]{2,1,0:T(8,128)} custom-call(f32[8,4,2,32,128]{4,3,2,1,0:T(8,128)} %broadcast_multiply_fusion.send_ref), custom_call_target="tpu_custom_call" | custom-call | tf_op jit(solution)/shard_map/pallas_call | solution.py:119
  208.9 1.4 copy.66
  (8 shorter events, 0.2 us)
Async XLA Ops:
  0.6 1.8 copy-start
  0.7 0.7 copy-start.5
  0.7 0.7 copy-start.6
  1.7 0.7 copy-start.4
  4.1 1.0 copy-start.2
  5.0 0.9 copy-start.3
  134.8 43.7 %copy-start.1 = (f32[1024,128]{1,0:T(8,128)S(1)}, f32[1024,128]{1,0:T(8,128)}, u32[]{:S(2)}) copy-start(f32[1024,128]{1,0:T(8,128)} %shard_map.94) | copy-start | bytes 1572868

commit v5 on v4

--- a/solution.py
+++ b/solution.py
@@ -17,58 +17,85 @@
 
 
 def partner_list(gx_size, af_size):
-    steps = []
-    bit = 1
-    while bit < gx_size:
-        steps.append(("gx", bit))
-        bit *= 2
-    bit = 1
-    while bit < af_size:
-        steps.append(("af", bit))
-        bit *= 2
+    preferred = [("gx", 1), ("gx", 2), ("gx", 16), ("af", 1), ("gx", 4), ("gx", 32), ("af", 2), ("gx", 8)]
+    sizes = {"gx": gx_size, "af": af_size}
+    steps = [(axis, bit) for axis, bit in preferred if bit < sizes[axis]]
+    for axis in ("gx", "af"):
+        bit = 1
+        while bit < sizes[axis]:
+            if (axis, bit) not in steps:
+                steps.append((axis, bit))
+            bit *= 2
     return steps
 
 
-def allreduce_kernel(steps, x_ref, o_ref, recv, send_sem, recv_sem):
-    g = lax.axis_index("gx")
-    a = lax.axis_index("af")
+def allreduce_kernel(steps, x_ref, o_ref, acc, recv, gathered, send_sem, recv_sem):
+    index = {"gx": lax.axis_index("gx"), "af": lax.axis_index("af")}
 
     def partner(axis, bit):
-        if axis == "gx":
-            return (lax.bitwise_xor(g, bit), a)
-        return (g, lax.bitwise_xor(a, bit))
+        own = index[axis]
+        side = (own // bit) % 2
+        other = own + bit - 2 * bit * side
+        device = (other, index["af"]) if axis == "gx" else (index["gx"], other)
+        return device, side
 
     barrier = pltpu.get_barrier_semaphore()
     for axis, bit in steps:
-        pl.semaphore_signal(barrier, inc=1, device_id=partner(axis, bit), device_id_type=MESH)
+        pl.semaphore_signal(barrier, inc=1, device_id=partner(axis, bit)[0], device_id_type=MESH)
     pl.semaphore_wait(barrier, len(steps))
 
-    o_ref[...] = x_ref[...]
-    for s, (axis, bit) in enumerate(steps):
+    def send(n, device, source, target):
         copy = pltpu.make_async_remote_copy(
-            src_ref=o_ref,
-            dst_ref=recv.at[s],
-            send_sem=send_sem.at[s],
-            recv_sem=recv_sem.at[s],
-            device_id=partner(axis, bit),
+            src_ref=source,
+            dst_ref=target,
+            send_sem=send_sem.at[n],
+            recv_sem=recv_sem.at[n],
+            device_id=device,
             device_id_type=MESH,
         )
         copy.start()
         copy.wait()
-        o_ref[...] = o_ref[...] + recv[s]
+
+    acc[...] = x_ref[...]
+    offset, length, slot = 0, acc.shape[0], 0
+    parents = []
+    for n, (axis, bit) in enumerate(steps[:-1]):
+        device, side = partner(axis, bit)
+        half = length // 2
+        give = pl.multiple_of(offset + half * (1 - side), 8)
+        keep = pl.multiple_of(offset + half * side, 8)
+        send(n, device, acc.at[pl.ds(give, half)], recv.at[pl.ds(slot, half)])
+        acc[pl.ds(keep, half), :] = acc[pl.ds(keep, half), :] + recv[pl.ds(slot, half), :]
+        parents.append((offset, length))
+        offset, length, slot = keep, half, slot + half
+    n = len(steps) - 1
+    device, side = partner(*steps[-1])
+    send(n, device, acc.at[pl.ds(offset, length)], recv.at[pl.ds(slot, length)])
+    gathered[pl.ds(offset, length), :] = (
+        acc[pl.ds(offset, length), :] + recv[pl.ds(slot, length), :]
+    )
+    for (axis, bit), (parent_offset, parent_length) in zip(reversed(steps[:-1]), reversed(parents)):
+        n += 1
+        device, side = partner(axis, bit)
+        send(n, device, gathered.at[pl.ds(offset, length)], gathered.at[pl.ds(offset, length)])
+        offset, length = parent_offset, parent_length
+    o_ref[...] = gathered[...]
 
 
 def allreduce_all(x):
     steps = partner_list(lax.axis_size("gx"), lax.axis_size("af"))
+    assert x.shape[0] % (8 << (len(steps) - 1)) == 0
     return pl.pallas_call(
         functools.partial(allreduce_kernel, steps),
         out_shape=jax.ShapeDtypeStruct(x.shape, x.dtype),
         in_specs=[pl.BlockSpec(memory_space=pltpu.VMEM)],
         out_specs=pl.BlockSpec(memory_space=pltpu.VMEM),
         scratch_shapes=[
-            pltpu.VMEM((len(steps),) + x.shape, x.dtype),
-            pltpu.SemaphoreType.DMA((len(steps),)),
-            pltpu.SemaphoreType.DMA((len(steps),)),
+            pltpu.VMEM(x.shape, x.dtype),
+            pltpu.VMEM(x.shape, x.dtype),
+            pltpu.VMEM(x.shape, x.dtype),
+            pltpu.SemaphoreType.DMA((2 * len(steps) - 1,)),
+            pltpu.SemaphoreType.DMA((2 * len(steps) - 1,)),
         ],
         compiler_params=pltpu.CompilerParams(collective_id=0, has_side_effects=True),
     )(x)

time: 211 us -> 154 us (0.73)
  the two profiles are of different devices: /device:TPU:4 before, /device:TPU:32 now
where the time goes in v5:
time: 154 us; the launch traced here: 153 us
  Pallas kernels  93.3 us (61%)
  other arithmetic  45.7 us (30%)
  matrix products  7.52 us (5%)
  local copies, waits for them, and re-layouts  5.76 us (4%)
    pallas_call x1, Pallas kernels, allreduce_all(): pl.pallas_call(functools.partial(allreduce_kernel, steps), out_shape=jax....  56.9 us
    pallas_call x1, Pallas kernels, core_exchange(): pl.pallas_call(functools.partial(core_kernel, cycle), out_shape=jax.Shape...  36.4 us
    another operation x4, other arithmetic, body(): lower_factors = jnp.linalg.cholesky(grams)  23.8 us
    another operation x3, other arithmetic, body(): jax.scipy.linalg.solve_triangular(lower_factors, ranges.transpose(0, 2, 1...  19.8 us
    unnamed x16, local copies, waits for them, and re-layouts  4.19 us

profile of v5, /device:TPU:32, one launch (start us, length us, event | category | flops | bytes accessed | tf_op | source)
XLA Modules:
  0.0 153.1 jit_solution(1606951861628536631)
XLA Ops:
  0.6 0.0 copy-start
  0.7 0.0 copy-start.5
  0.7 0.0 copy-start.6
  0.7 0.7 copy-done.5
  1.4 0.0 copy-done.6
  1.4 0.1 constant_dynamic-slice_fusion.1
  1.5 0.1 copy.27
  1.6 0.1 copy.28
  1.7 0.0 copy-start.4
  1.7 0.1 fusion.18
  1.8 0.1 copy.29
  1.8 0.5 copy-done.4
  2.4 0.0 copy-done
  2.4 1.6 %fusion.3 = f32[256,128]{0,1:T(8,128)S(1)} fusion(f32[2,128,512]{2,1,0:T(8,128)S(1)} %copy-done, f32[512,256]{1,0:T(8,128)} %param.10, f32[256,2]{0,1:T(2,128)S(1)} %get-tuple-element.8), kind=kOutput, calls=%fused_computation.5 | convolution fusion | flops 402751488 | bytes 1181696 | tf_op jit(solution)/shard_map/pjl,lk->pjk/dot_general | solution.py:170
  4.1 0.0 copy-start.2
  4.1 0.9 copy-done.2
  5.0 0.0 copy-start.3
  5.0 0.3 convolution_dynamic-update-slice_fusion
  5.3 0.6 copy-done.3
  5.9 1.0 fusion.1
  7.0 0.6 fusion.9
  7.5 0.8 pad_maximum_fusion.x_ref
  8.4 56.9 %shard_map.94 = f32[1024,128]{1,0:T(8,128)} custom-call(f32[1024,128]{1,0:T(8,128)} %pad_maximum_fusion.x_ref), custom_call_target="tpu_custom_call" | custom-call | tf_op jit(solution)/shard_map/pallas_call | solution.py:88
  65.3 2.2 %fusion.28 = f32[2,128,128]{2,1,0:T(8,128)S(1)} fusion(f32[2,512,128]{2,1,0:T(8,128)} %bitcast.74), kind=kOutput, calls=%fused_computation.47 | convolution fusion | flops 201326592 | bytes 655360 | tf_op jit(solution)/shard_map/nji,njk->nik/dot_general | solution.py:186
  67.5 0.0 copy-start.1
  67.5 0.1 copy.25
  67.6 23.6 %custom-call.8 = f32[2,128,128]{2,1,0:T(8,128)S(1)} custom-call(f32[2,128,128]{2,1,0:T(8,128)S(1)} %fusion.8), custom_call_target="Cholesky" | custom-call | tf_op jit(solution)/shard_map/jit(cholesky)/cholesky | solution.py:187
  91.3 0.1 compare_reduce_fusion
  91.4 0.1 select_bitcast_fusion
  91.5 19.7 %custom-call.9 = f32[2,1,128,128]{2,3,1,0:T(8,128)S(1)} custom-call(f32[2,1,128,128]{3,2,1,0:T(8,128)S(1)} %select_bitcast_fusion), custom_call_target="InvertDiagBlocksLowerTriangular" | custom-call | tf_op jit(solution)/shard_map/jit(_solve_triangular)/vmap()/triangular_solve | solution.py:188
  111.2 0.0 copy-done.1
  111.2 0.6 fusion.6
  111.8 0.6 fusion.21
  112.4 0.6 fusion.20
  113.0 0.6 fusion.15
  113.6 0.6 convolution_bitcast_fusion.2
  114.2 1.1 broadcast_multiply_fusion.send_ref
  115.3 36.4 %shard_map.95 = f32[2,32,128]{2,1,0:T(8,128)} custom-call(f32[8,4,2,32,128]{4,3,2,1,0:T(8,128)} %broadcast_multiply_fusion.send_ref), custom_call_target="tpu_custom_call" | custom-call | tf_op jit(solution)/shard_map/pallas_call | solution.py:146
  151.8 1.4 copy.66
  (8 shorter events, 0.2 us)
Async XLA Ops:
  0.6 1.8 %copy-start = (f32[2,128,512]{2,1,0:T(8,128)S(1)}, f32[2,128,512]{2,1,0:T(8,128)}, u32[]{:S(2)}) copy-start(f32[2,128,512]{2,1,0:T(8,128)} %param.7) | copy-start | bytes 1572868
  0.7 0.7 copy-start.5
  0.7 0.7 copy-start.6
  1.7 0.7 copy-start.4
  4.1 1.0 copy-start.2
  5.0 0.9 copy-start.3
  67.5 43.7 %copy-start.1 = (f32[1024,128]{1,0:T(8,128)S(1)}, f32[1024,128]{1,0:T(8,128)}, u32[]{:S(2)}) copy-start(f32[1024,128]{1,0:T(8,128)} %shard_map.94) | copy-start | bytes 1572868

commit v6 on v5

--- a/solution.py
+++ b/solution.py
@@ -101,60 +101,62 @@
     )(x)
 
 
-def core_kernel(cycle, send_ref, o_ref, recv, send_sem, recv_sem):
+def group_kernel(kind, cycle, send_ref, o_ref, recv, send_sem, recv_sem):
     g = lax.axis_index("gx")
     a = lax.axis_index("af")
-    groups, af_size = send_ref.shape[0], send_ref.shape[1]
-    k = g // cycle
-    c = g % cycle
-    offsets = [(db, da) for db in range(groups) for da in range(af_size) if (db, da) != (0, 0)]
-
-    def target(db, da):
-        return ((k + db) % groups, (a + da) % af_size)
-
+    size = send_ref.shape[0]
+    if kind == "af":
+        me = a
+
+        def device(j):
+            return (g, j)
+    else:
+        me = g // cycle
+
+        def device(j):
+            return (j * cycle + g % cycle, a)
+
+    members = [(me + d) % size for d in range(1, size)]
     barrier = pltpu.get_barrier_semaphore()
-    for db, da in offsets:
-        tb, ta = target(db, da)
-        pl.semaphore_signal(barrier, inc=1, device_id=(tb * cycle + c, ta), device_id_type=MESH)
-    pl.semaphore_wait(barrier, len(offsets))
+    for j in members:
+        pl.semaphore_signal(barrier, inc=1, device_id=device(j), device_id_type=MESH)
+    pl.semaphore_wait(barrier, len(members))
 
     copies = []
-    for n, (db, da) in enumerate(offsets):
-        tb, ta = target(db, da)
+    for n, j in enumerate(members):
         copy = pltpu.make_async_remote_copy(
-            src_ref=send_ref.at[tb, ta],
+            src_ref=send_ref.at[j],
             dst_ref=recv.at[n],
             send_sem=send_sem.at[n],
             recv_sem=recv_sem.at[n],
-            device_id=(tb * cycle + c, ta),
+            device_id=device(j),
             device_id_type=MESH,
         )
         copy.start()
         copies.append(copy)
     for copy in copies:
         copy.wait()
-    total = send_ref[k, a]
-    for n in range(len(offsets)):
+    total = send_ref[me]
+    for n in range(len(members)):
         total = total + recv[n]
     o_ref[...] = total
 
 
-def core_exchange(contributions, cycle):
-    groups, af_size = contributions.shape[:2]
-    piece = contributions.shape[2:]
-    slots = groups * af_size - 1
+def group_sum(pieces, kind, cycle, collective_id):
+    size = pieces.shape[0]
+    piece = pieces.shape[1:]
     return pl.pallas_call(
-        functools.partial(core_kernel, cycle),
-        out_shape=jax.ShapeDtypeStruct(piece, contributions.dtype),
+        functools.partial(group_kernel, kind, cycle),
+        out_shape=jax.ShapeDtypeStruct(piece, pieces.dtype),
         in_specs=[pl.BlockSpec(memory_space=pltpu.VMEM)],
         out_specs=pl.BlockSpec(memory_space=pltpu.VMEM),
         scratch_shapes=[
-            pltpu.VMEM((slots,) + piece, contributions.dtype),
-            pltpu.SemaphoreType.DMA((slots,)),
-            pltpu.SemaphoreType.DMA((slots,)),
+            pltpu.VMEM((size - 1,) + piece, pieces.dtype),
+            pltpu.SemaphoreType.DMA((size - 1,)),
+            pltpu.SemaphoreType.DMA((size - 1,)),
         ],
-        compiler_params=pltpu.CompilerParams(collective_id=1, has_side_effects=True),
-    )(contributions)
+        compiler_params=pltpu.CompilerParams(collective_id=collective_id, has_side_effects=True),
+    )(pieces)
 
 
 def body(
@@ -213,8 +215,9 @@
     )
     slab = rank_cols // af_size
     pieces = projected.reshape(planes, af_size, slab, rank_cols).transpose(1, 0, 2, 3)
-    contributions = weights[:, None, :, None, None] * pieces[None]
-    core_sketch = core_exchange(contributions, cycle)
+    summed = group_sum(pieces, "af", cycle, 1)
+    contributions = weights[:, :, None, None] * summed[None]
+    core_sketch = group_sum(contributions, "gx", cycle, 2)
     return (factor_second, factor_third, core_sketch)
 
 

time: 154 us -> 141 us (0.916)
  Pallas kernels: 93.3 us -> 79.9 us
    pallas_call x1 -> x2, Pallas kernels: 36.4 us -> 23.1 us  [group_sum(): pl.pallas_call(functools.partial(group_kernel, kind, cycle), out_shape=ja...]
    unnamed x16 -> x14, local copies, waits for them, and re-layouts: 4.19 us -> 2.81 us
where the time goes in v6:
time: 141 us; the launch traced here: 140 us
  Pallas kernels  79.9 us (57%)
  other arithmetic  46.1 us (33%)
  matrix products  8.08 us (6%)
  local copies, waits for them, and re-layouts  5.14 us (4%)
    pallas_call x1, Pallas kernels, allreduce_all(): pl.pallas_call(functools.partial(allreduce_kernel, steps), out_shape=jax....  56.9 us
    another operation x4, other arithmetic, body(): lower_factors = jnp.linalg.cholesky(grams)  23.8 us
    pallas_call x2, Pallas kernels, group_sum(): pl.pallas_call(functools.partial(group_kernel, kind, cycle), out_shape=ja...  23.1 us
    another operation x3, other arithmetic, body(): jax.scipy.linalg.solve_triangular(lower_factors, ranges.transpose(0, 2, 1...  19.8 us

profile of v6, /device:TPU:32, one launch (start us, length us, event | category | flops | bytes accessed | tf_op | source)
XLA Modules:
  0.0 140.1 jit_solution(2871532924350299131)
XLA Ops:
  0.6 0.0 copy-start
  0.6 0.8 fusion.28
  1.4 0.3 copy-done
  1.7 0.0 copy-start.3
  1.7 2.0 %fusion.1 = f32[256,512]{0,1:T(8,128)S(1)} fusion(f32[2,128,512]{2,1,0:T(8,128)S(1)} %copy-done, f32[256,2]{0,1:T(2,128)S(1)} %get-tuple-element.7, f32[128,256]{1,0:T(8,128)} %param.9), kind=kOutput, calls=%fused_computation.2 | convolution fusion | flops 403046400 | bytes 1181696 | tf_op jit(solution)/shard_map/pjl,jk->plk/dot_general | solution.py:176
  3.7 0.0 copy-done.3
  3.7 0.0 copy-start.2
  3.7 0.6 fusion.10
  4.3 0.4 copy-done.2
  4.8 0.6 fusion.3
  5.4 0.3 convolution_dynamic-update-slice_fusion
  5.7 0.8 pad_maximum_fusion.x_ref
  6.5 56.9 %shard_map.94 = f32[1024,128]{1,0:T(8,128)} custom-call(f32[1024,128]{1,0:T(8,128)} %pad_maximum_fusion.x_ref), custom_call_target="tpu_custom_call" | custom-call | tf_op jit(solution)/shard_map/pallas_call | solution.py:88
  63.4 2.2 %fusion.29 = f32[2,128,128]{2,1,0:T(8,128)S(1)} fusion(f32[2,512,128]{2,1,0:T(8,128)} %bitcast.71), kind=kOutput, calls=%fused_computation.48 | convolution fusion | flops 201326592 | bytes 655360 | tf_op jit(solution)/shard_map/nji,njk->nik/dot_general | solution.py:188
  65.6 0.0 copy-start.1
  65.6 0.1 copy.25
  65.7 23.6 %custom-call.8 = f32[2,128,128]{2,1,0:T(8,128)S(1)} custom-call(f32[2,128,128]{2,1,0:T(8,128)S(1)} %fusion.9), custom_call_target="Cholesky" | custom-call | tf_op jit(solution)/shard_map/jit(cholesky)/cholesky | solution.py:189
  89.4 0.1 compare_reduce_fusion
  89.6 0.1 select_bitcast_fusion
  89.7 19.7 %custom-call.9 = f32[2,1,128,128]{2,3,1,0:T(8,128)S(1)} custom-call(f32[2,1,128,128]{3,2,1,0:T(8,128)S(1)} %select_bitcast_fusion), custom_call_target="InvertDiagBlocksLowerTriangular" | custom-call | tf_op jit(solution)/shard_map/jit(_solve_triangular)/vmap()/triangular_solve | solution.py:190
  109.3 0.0 copy-done.1
  109.4 0.6 fusion.7
  110.0 0.6 fusion.21
  110.6 0.6 fusion.22
  111.1 0.6 fusion.16
  111.8 1.2 convolution_bitcast_fusion.2.send_ref
  113.0 8.1 %shard_map.95 = f32[2,32,128]{2,1,0:T(8,128)} custom-call(f32[4,2,32,128]{3,2,1,0:T(8,128)} %convolution_bitcast_fusion.2.send_ref), custom_call_target="tpu_custom_call" | custom-call | tf_op jit(solution)/shard_map/pallas_call | solution.py:148
  121.1 0.0 copy-start.4
  121.1 0.0 copy-start.5
  121.1 0.7 copy-done.4
  121.8 0.0 copy-done.5
  121.8 0.1 constant_dynamic-slice_fusion.1
  121.9 0.1 copy.28
  122.0 0.1 copy.27
  122.1 0.1 fusion.19
  122.2 0.1 copy.29
  122.3 1.5 %broadcast_multiply_fusion.send_ref = f32[8,2,32,128]{3,2,1,0:T(8,128)} fusion(f32[2,32,128]{2,1,0:T(8,128)} %shard_map.95, f32[8,2]{1,0:T(8,128)S(1)} %copy.29), kind=kLoop, calls=%fused_computation.20 | loop fusion | flops 65536 | bytes 294976 | tf_op jit(solution)/shard_map/mul | solution.py:219
  123.8 14.9 %shard_map.96 = f32[2,32,128]{2,1,0:T(8,128)} custom-call(f32[8,2,32,128]{3,2,1,0:T(8,128)} %broadcast_multiply_fusion.send_ref), custom_call_target="tpu_custom_call" | custom-call | tf_op jit(solution)/shard_map/pallas_call | solution.py:148
  138.7 1.4 copy.65
  (7 shorter events, 0.1 us)
Async XLA Ops:
  0.6 1.1 copy-start
  1.7 2.0 %copy-start.3 = (f32[2,256,128]{2,1,0:T(8,128)S(1)}, f32[2,256,128]{2,1,0:T(8,128)}, u32[]{:S(2)}) copy-start(f32[2,256,128]{2,1,0:T(8,128)} %param.11) | copy-start | bytes 786436
  3.7 1.0 copy-start.2
  65.6 43.8 %copy-start.1 = (f32[1024,128]{1,0:T(8,128)S(1)}, f32[1024,128]{1,0:T(8,128)}, u32[]{:S(2)}) copy-start(f32[1024,128]{1,0:T(8,128)} %shard_map.94) | copy-start | bytes 1572868
  121.1 0.7 copy-start.4
  121.1 0.7 copy-start.5

commit v7 on v6

--- a/solution.py
+++ b/solution.py
@@ -29,73 +29,109 @@
     return steps
 
 
-def allreduce_kernel(steps, x_ref, o_ref, acc, recv, gathered, send_sem, recv_sem):
+def allreduce_kernel(digits, x_ref, o_ref, acc, recv, exchange, gathered, send_sem, recv_sem):
     index = {"gx": lax.axis_index("gx"), "af": lax.axis_index("af")}
 
-    def partner(axis, bit):
-        own = index[axis]
-        side = (own // bit) % 2
-        other = own + bit - 2 * bit * side
-        device = (other, index["af"]) if axis == "gx" else (index["gx"], other)
-        return device, side
+    def bits_of(digit):
+        return [(index[axis] // bit) % 2 for axis, bit in digit]
+
+    def member(digit):
+        own = bits_of(digit)
+        return own[0] + 2 * own[1]
+
+    def device(digit, d):
+        values = dict(index)
+        for t, ((axis, bit), own) in enumerate(zip(digit, bits_of(digit))):
+            flip = (d >> t) & 1
+            values[axis] = values[axis] + bit * flip * (1 - 2 * own)
+        return (values["gx"], values["af"])
 
     barrier = pltpu.get_barrier_semaphore()
-    for axis, bit in steps:
-        pl.semaphore_signal(barrier, inc=1, device_id=partner(axis, bit)[0], device_id_type=MESH)
-    pl.semaphore_wait(barrier, len(steps))
-
-    def send(n, device, source, target):
+    for digit in digits:
+        for d in (1, 2, 3):
+            pl.semaphore_signal(barrier, inc=1, device_id=device(digit, d), device_id_type=MESH)
+    pl.semaphore_wait(barrier, 3 * len(digits))
+
+    counter = [0]
+
+    def start(device_id, source, target):
+        n = counter[0]
+        counter[0] += 1
         copy = pltpu.make_async_remote_copy(
             src_ref=source,
             dst_ref=target,
             send_sem=send_sem.at[n],
             recv_sem=recv_sem.at[n],
-            device_id=device,
+            device_id=device_id,
             device_id_type=MESH,
         )
         copy.start()
-        copy.wait()
+        return copy
+
+    def flipped(me, d):
+        low, high = me % 2, me // 2
+        low = low + (d & 1) * (1 - 2 * low)
+        high = high + ((d >> 1) & 1) * (1 - 2 * high)
+        return low + 2 * high
 
     acc[...] = x_ref[...]
     offset, length, slot = 0, acc.shape[0], 0
     parents = []
-    for n, (axis, bit) in enumerate(steps[:-1]):
-        device, side = partner(axis, bit)
-        half = length // 2
-        give = pl.multiple_of(offset + half * (1 - side), 8)
-        keep = pl.multiple_of(offset + half * side, 8)
-        send(n, device, acc.at[pl.ds(give, half)], recv.at[pl.ds(slot, half)])
-        acc[pl.ds(keep, half), :] = acc[pl.ds(keep, half), :] + recv[pl.ds(slot, half), :]
+    for digit in digits[:-1]:
+        me = member(digit)
+        quarter = length // 4
+        copies = []
+        for d in (1, 2, 3):
+            give = pl.multiple_of(offset + flipped(me, d) * quarter, 8)
+            target = recv.at[pl.ds(slot + (d - 1) * quarter, quarter)]
+            copies.append(start(device(digit, d), acc.at[pl.ds(give, quarter)], target))
+        for copy in copies:
+            copy.wait()
+        keep = pl.multiple_of(offset + me * quarter, 8)
+        total = acc[pl.ds(keep, quarter), :]
+        for d in (1, 2, 3):
+            total = total + recv[pl.ds(slot + (d - 1) * quarter, quarter), :]
+        acc[pl.ds(keep, quarter), :] = total
         parents.append((offset, length))
-        offset, length, slot = keep, half, slot + half
-    n = len(steps) - 1
-    device, side = partner(*steps[-1])
-    send(n, device, acc.at[pl.ds(offset, length)], recv.at[pl.ds(slot, length)])
-    gathered[pl.ds(offset, length), :] = (
-        acc[pl.ds(offset, length), :] + recv[pl.ds(slot, length), :]
-    )
-    for (axis, bit), (parent_offset, parent_length) in zip(reversed(steps[:-1]), reversed(parents)):
-        n += 1
-        device, side = partner(axis, bit)
-        send(n, device, gathered.at[pl.ds(offset, length)], gathered.at[pl.ds(offset, length)])
+        offset, length, slot = keep, quarter, slot + 3 * quarter
+
+    last = digits[-1]
+    me = member(last)
+    segment = acc.at[pl.ds(offset, length)]
+    copies = [start(device(last, d), segment, exchange.at[me]) for d in (1, 2, 3)]
+    exchange[me] = acc[pl.ds(offset, length), :]
+    for copy in copies:
+        copy.wait()
+    gathered[pl.ds(offset, length), :] = ((exchange[0] + exchange[1]) + exchange[2]) + exchange[3]
+
+    for digit, (parent_offset, parent_length) in zip(reversed(digits[:-1]), reversed(parents)):
+        part = gathered.at[pl.ds(offset, length)]
+        copies = [start(device(digit, d), part, part) for d in (1, 2, 3)]
+        for copy in copies:
+            copy.wait()
         offset, length = parent_offset, parent_length
     o_ref[...] = gathered[...]
 
 
 def allreduce_all(x):
     steps = partner_list(lax.axis_size("gx"), lax.axis_size("af"))
-    assert x.shape[0] % (8 << (len(steps) - 1)) == 0
+    assert len(steps) % 2 == 0
+    digits = [steps[t:t + 2] for t in range(0, len(steps), 2)]
+    last_rows = x.shape[0] // 4 ** (len(digits) - 1)
+    assert last_rows % 8 == 0
+    copies = 3 * (2 * len(digits) - 1)
     return pl.pallas_call(
-        functools.partial(allreduce_kernel, steps),
+        functools.partial(allreduce_kernel, digits),
         out_shape=jax.ShapeDtypeStruct(x.shape, x.dtype),
         in_specs=[pl.BlockSpec(memory_space=pltpu.VMEM)],
         out_specs=pl.BlockSpec(memory_space=pltpu.VMEM),
         scratch_shapes=[
             pltpu.VMEM(x.shape, x.dtype),
             pltpu.VMEM(x.shape, x.dtype),
+            pltpu.VMEM((4, last_rows) + x.shape[1:], x.dtype),
             pltpu.VMEM(x.shape, x.dtype),
-            pltpu.SemaphoreType.DMA((2 * len(steps) - 1,)),
-            pltpu.SemaphoreType.DMA((2 * len(steps) - 1,)),
+            pltpu.SemaphoreType.DMA((copies,)),
+            pltpu.SemaphoreType.DMA((copies,)),
         ],
         compiler_params=pltpu.CompilerParams(collective_id=0, has_side_effects=True),
     )(x)

time: 141 us -> 127 us (0.901)
  Pallas kernels: 79.9 us -> 66.4 us
    pallas_call x1, Pallas kernels: 56.9 us -> 42.8 us  [allreduce_all(): pl.pallas_call(functools.partial(allreduce_kernel, digits), out_shape=jax...]
where the time goes in v7:
time: 127 us
  Pallas kernels  66.4 us (52%)
  other arithmetic  46.1 us (36%)
  matrix products  8.08 us (6%)
  local copies, waits for them, and re-layouts  5.14 us (4%)
    pallas_call x1, Pallas kernels, allreduce_all(): pl.pallas_call(functools.partial(allreduce_kernel, digits), out_shape=jax...  42.8 us
    another operation x4, other arithmetic, body(): lower_factors = jnp.linalg.cholesky(grams)  23.8 us
    pallas_call x2, Pallas kernels, group_sum(): pl.pallas_call(functools.partial(group_kernel, kind, cycle), out_shape=ja...  23.6 us
    another operation x3, other arithmetic, body(): jax.scipy.linalg.solve_triangular(lower_factors, ranges.transpose(0, 2, 1...  19.8 us
    unnamed x14, local copies, waits for them, and re-layouts  2.81 us

profile of v7, /device:TPU:32, one launch (start us, length us, event | category | flops | bytes accessed | tf_op | source)
XLA Modules:
  0.0 126.6 jit_solution(18163996481368866238)
XLA Ops:
  0.6 0.0 copy-start
  0.6 0.8 fusion.28
  1.4 0.3 copy-done
  1.7 0.0 copy-start.3
  1.7 2.0 %fusion.1 = f32[256,512]{0,1:T(8,128)S(1)} fusion(f32[2,128,512]{2,1,0:T(8,128)S(1)} %copy-done, f32[256,2]{0,1:T(2,128)S(1)} %get-tuple-element.7, f32[128,256]{1,0:T(8,128)} %param.9), kind=kOutput, calls=%fused_computation.2 | convolution fusion | flops 403046400 | bytes 1181696 | tf_op jit(solution)/shard_map/pjl,jk->plk/dot_general | solution.py:212
  3.7 0.0 copy-done.3
  3.7 0.0 copy-start.2
  3.7 0.6 fusion.10
  4.3 0.4 copy-done.2
  4.8 0.6 fusion.3
  5.4 0.3 convolution_dynamic-update-slice_fusion
  5.7 0.8 pad_maximum_fusion.x_ref
  6.5 42.8 %shard_map.94 = f32[1024,128]{1,0:T(8,128)} custom-call(f32[1024,128]{1,0:T(8,128)} %pad_maximum_fusion.x_ref), custom_call_target="tpu_custom_call" | custom-call | tf_op jit(solution)/shard_map/pallas_call | solution.py:123
  49.3 2.2 %fusion.29 = f32[2,128,128]{2,1,0:T(8,128)S(1)} fusion(f32[2,512,128]{2,1,0:T(8,128)} %bitcast.71), kind=kOutput, calls=%fused_computation.48 | convolution fusion | flops 201326592 | bytes 655360 | tf_op jit(solution)/shard_map/nji,njk->nik/dot_general | solution.py:224
  51.5 0.0 copy-start.1
  51.5 0.1 copy.25
  51.6 23.6 %custom-call.8 = f32[2,128,128]{2,1,0:T(8,128)S(1)} custom-call(f32[2,128,128]{2,1,0:T(8,128)S(1)} %fusion.9), custom_call_target="Cholesky" | custom-call | tf_op jit(solution)/shard_map/jit(cholesky)/cholesky | solution.py:225
  75.3 0.1 compare_reduce_fusion
  75.5 0.1 select_bitcast_fusion
  75.6 19.7 %custom-call.9 = f32[2,1,128,128]{2,3,1,0:T(8,128)S(1)} custom-call(f32[2,1,128,128]{3,2,1,0:T(8,128)S(1)} %select_bitcast_fusion), custom_call_target="InvertDiagBlocksLowerTriangular" | custom-call | tf_op jit(solution)/shard_map/jit(_solve_triangular)/vmap()/triangular_solve | solution.py:226
  95.3 0.0 copy-done.1
  95.3 0.6 fusion.7
  95.9 0.6 fusion.21
  96.5 0.6 fusion.22
  97.1 0.6 fusion.16
  97.7 1.2 convolution_bitcast_fusion.2.send_ref
  98.9 8.8 %shard_map.95 = f32[2,32,128]{2,1,0:T(8,128)} custom-call(f32[4,2,32,128]{3,2,1,0:T(8,128)} %convolution_bitcast_fusion.2.send_ref), custom_call_target="tpu_custom_call" | custom-call | tf_op jit(solution)/shard_map/pallas_call | solution.py:184
  107.7 0.0 copy-start.4
  107.7 0.0 copy-start.5
  107.7 0.7 copy-done.4
  108.4 0.0 copy-done.5
  108.4 0.1 constant_dynamic-slice_fusion.1
  108.5 0.1 copy.28
  108.6 0.1 copy.27
  108.7 0.1 fusion.19
  108.8 0.1 copy.29
  108.9 1.5 %broadcast_multiply_fusion.send_ref = f32[8,2,32,128]{3,2,1,0:T(8,128)} fusion(f32[2,32,128]{2,1,0:T(8,128)} %shard_map.95, f32[8,2]{1,0:T(8,128)S(1)} %copy.29), kind=kLoop, calls=%fused_computation.20 | loop fusion | flops 65536 | bytes 294976 | tf_op jit(solution)/shard_map/mul | solution.py:255
  110.4 14.8 %shard_map.96 = f32[2,32,128]{2,1,0:T(8,128)} custom-call(f32[8,2,32,128]{3,2,1,0:T(8,128)} %broadcast_multiply_fusion.send_ref), custom_call_target="tpu_custom_call" | custom-call | tf_op jit(solution)/shard_map/pallas_call | solution.py:184
  125.2 1.4 %copy.65 = f32[2,32,128]{2,1,0:T(8,128)} copy(f32[2,32,128]{2,1,0:T(8,128)} %shard_map.96) | data formatting | bytes 65536
  (7 shorter events, 0.1 us)
Async XLA Ops:
  0.6 1.1 copy-start
  1.7 2.0 %copy-start.3 = (f32[2,256,128]{2,1,0:T(8,128)S(1)}, f32[2,256,128]{2,1,0:T(8,128)}, u32[]{:S(2)}) copy-start(f32[2,256,128]{2,1,0:T(8,128)} %param.11) | copy-start | bytes 786436
  3.7 1.0 copy-start.2
  51.5 43.8 %copy-start.1 = (f32[1024,128]{1,0:T(8,128)S(1)}, f32[1024,128]{1,0:T(8,128)}, u32[]{:S(2)}) copy-start(f32[1024,128]{1,0:T(8,128)} %shard_map.94) | copy-start | bytes 1572868
  107.7 0.7 copy-start.4
  107.7 0.7 copy-start.5

commit v8 on v7

--- a/solution.py
+++ b/solution.py
@@ -137,6 +137,42 @@
     )(x)
 
 
+def panel_kernel(*refs):
+    count = len(refs) // 2
+    inputs, outputs = refs[:count], refs[count:]
+    for source, target in zip(inputs, outputs):
+        target[...] = source[...]
+    rank = outputs[0].shape[0]
+
+    def step(j, carry):
+        for ref in outputs:
+            width = ref.shape[1]
+            row = ref[pl.ds(j, 1), :]
+            lanes = lax.broadcasted_iota(jnp.int32, (1, width), 1)
+            pivot = jnp.sum(jnp.where(lanes == j, row, 0.0), axis=1, keepdims=True)
+            root = jnp.sqrt(pivot)
+            column = jnp.where(lanes < j, 0.0, row / root)
+            square = ref[:, pl.ds(0, rank)]
+            cols = lax.broadcasted_iota(jnp.int32, (rank, rank), 1)
+            upper = jnp.sum(jnp.where(cols == j, square, 0.0), axis=1, keepdims=True)
+            below = lax.broadcasted_iota(jnp.int32, (rank, 1), 0) > j
+            scale = jnp.where(below, upper / root, 0.0)
+            ref[...] = ref[...] - scale * column
+            ref[pl.ds(j, 1), :] = column
+        return carry
+
+    lax.fori_loop(0, rank, step, 0)
+
+
+def factor_panels(*panels):
+    return pl.pallas_call(
+        panel_kernel,
+        out_shape=[jax.ShapeDtypeStruct(p.shape, p.dtype) for p in panels],
+        in_specs=[pl.BlockSpec(memory_space=pltpu.VMEM)] * len(panels),
+        out_specs=[pl.BlockSpec(memory_space=pltpu.VMEM)] * len(panels),
+    )(*panels)
+
+
 def group_kernel(kind, cycle, send_ref, o_ref, recv, send_sem, recv_sem):
     g = lax.axis_index("gx")
     a = lax.axis_index("af")
@@ -222,20 +258,20 @@
 
     ranges = both.reshape(2, full_rows, rank_cols)
     grams = jnp.einsum("nji,njk->nik", ranges, ranges, precision=precise)
-    lower_factors = jnp.linalg.cholesky(grams)
-    factors = jax.scipy.linalg.solve_triangular(
-        lower_factors, ranges.transpose(0, 2, 1), lower=True
-    ).transpose(0, 2, 1)
-    factor_second_all, factor_third_all = factors[0], factors[1]
+    own_second = lax.dynamic_slice_in_dim(ranges[0], af_index * rows, rows, 0)
+    panel_third, panel_second = factor_panels(
+        jnp.concatenate([grams[1], ranges[1].T], axis=1),
+        jnp.concatenate([grams[0], own_second.T], axis=1),
+    )
+    factor_third_all = panel_third[:, rank_cols:].T
+    basis_second = panel_second[:, rank_cols:].T
 
     out_second = full_rows // (gx_size * af_size)
-    factor_second = lax.dynamic_slice_in_dim(
-        factor_second_all, (af_index * gx_size + gx_index) * out_second, out_second, 0
-    )
+    assert rows == gx_size * out_second
+    factor_second = lax.dynamic_slice_in_dim(basis_second, gx_index * out_second, out_second, 0)
     factor_third = lax.dynamic_slice_in_dim(
         factor_third_all, (gx_index * af_size + af_index) * out_second, out_second, 0
     )
-    basis_second = lax.dynamic_slice_in_dim(factor_second_all, af_index * rows, rows, 0)
     left_side = jnp.einsum("jr,pjl->prl", basis_second, scalar_field, precision=precise)
     projected = jnp.einsum("prl,ls->prs", left_side, factor_third_all, precision=precise)
     cycle = BLOCK // planes

time: 127 us -> 106 us (0.83)
  other arithmetic: 46.1 us -> 3.19 us
  Pallas kernels: 66.4 us -> 87.2 us
  local copies, waits for them, and re-layouts: 5.14 us -> 7.56 us
  matrix products: 8.08 us -> 6.57 us
    another operation x7 -> x0, other arithmetic: 43.6 us -> none  [the longest x4 23.8 us: body(): lower_factors = jnp.linalg.cholesky(grams)]
    pallas_call x0 -> x1, Pallas kernels: none -> 20.8 us  [factor_panels(): pl.pallas_call(panel_kernel, out_shape=[jax.ShapeDtypeStruct(p.shape, p.d...]
    unnamed x14 -> x28, local copies, waits for them, and re-layouts: 2.81 us -> 5.27 us
    concatenate x0 -> x2, other arithmetic: none -> 1.41 us  [the longest x1 0.74 us: body(): jnp.concatenate([grams[1], ranges[1].T], axis=1)]
where the time goes in v8:
time: 106 us; the launch traced here: 105 us
  Pallas kernels  87.2 us (82%)
  local copies, waits for them, and re-layouts  7.56 us (7%)
  matrix products  6.57 us (6%)
  other arithmetic  3.19 us (3%)
    pallas_call x1, Pallas kernels, allreduce_all(): pl.pallas_call(functools.partial(allreduce_kernel, digits), out_shape=jax...  42.8 us
    pallas_call x2, Pallas kernels, group_sum(): pl.pallas_call(functools.partial(group_kernel, kind, cycle), out_shape=ja...  23.6 us
    pallas_call x1, Pallas kernels, factor_panels(): pl.pallas_call(panel_kernel, out_shape=[jax.ShapeDtypeStruct(p.shape, p.d...  20.8 us
    unnamed x28, local copies, waits for them, and re-layouts  5.27 us

profile of v8, /device:TPU:32, one launch (start us, length us, event | category | flops | bytes accessed | tf_op | source)
XLA Modules:
  0.0 105.4 jit_solution(447171230273656599)
XLA Ops:
  0.6 0.0 copy-start
  0.6 0.0 copy-start.8
  0.7 0.7 copy-done.8
  1.4 0.3 copy-done
  1.7 1.6 %fusion.3 = f32[256,128]{0,1:T(8,128)S(1)} fusion(f32[2,128,512]{2,1,0:T(8,128)S(1)} %copy-done, f32[512,256]{1,0:T(8,128)} %param.10, f32[256,2]{0,1:T(2,128)S(1)} %get-tuple-element.23), kind=kOutput, calls=%fused_computation.6 | convolution fusion | flops 402751488 | bytes 1181696 | tf_op jit(solution)/shard_map/pjl,lk->pjk/dot_general | solution.py:244
  3.3 0.0 copy-start.3
  3.4 0.9 copy-done.3
  4.3 0.0 copy-start.4
  4.3 0.3 convolution_dynamic-update-slice_fusion
  4.6 0.6 copy-done.4
  5.2 1.0 fusion.1
  6.2 0.6 fusion.7
  6.8 0.8 pad_maximum_fusion.x_ref
  7.7 42.8 %shard_map.94 = f32[1024,128]{1,0:T(8,128)} custom-call(f32[1024,128]{1,0:T(8,128)} %pad_maximum_fusion.x_ref), custom_call_target="tpu_custom_call" | custom-call | tf_op jit(solution)/shard_map/pallas_call | solution.py:123
  50.5 0.0 copy-start.1
  50.5 1.1 %fusion.20 = (f32[512,128]{1,0:T(8,128)S(1)}, f32[512,128]{1,0:T(8,128)S(1)}) fusion(f32[1024,128]{1,0:T(8,128)} %shard_map.94), kind=kLoop, calls=%fused_computation.39 | loop fusion | bytes 1048576 | tf_op jit(solution)/shard_map/slice | solution.py:261
  51.6 0.1 copy.64
  51.7 0.0 copy-done.1
  51.7 1.0 fusion.22
  52.8 0.7 pad_maximum_fusion.2.refs_1_
  53.4 0.1 copy.62
  53.6 0.7 pad_maximum_fusion.1.refs_0_
  54.3 20.8 %shard_map.95 = (f32[128,640]{1,0:T(8,128)}, f32[128,256]{1,0:T(8,128)}) custom-call(f32[128,640]{1,0:T(8,128)} %pad_maximum_fusion.1.refs_0_, f32[128,256]{1,0:T(8,128)} %pad_maximum_fusion.2.refs_1_), custom_call_target="tpu_custom_call" | custom-call | tf_op jit(solution)/shard_map/pallas_call | solution.py:168
  75.1 0.0 copy-start.2
  75.1 1.5 %convolution_bitcast_fusion.1 = f32[2,128,512]{2,1,0:T(8,128)S(1)} fusion(f32[2,128,512]{2,1,0:T(8,128)S(1)} %copy-done, f32[128,256]{1,0:T(8,128)} %get-tuple-element.5), kind=kOutput, calls=%fused_computation.3 | convolution fusion | flops 201326592 | bytes 1114112 | tf_op jit(solution)/shard_map/jr,pjl->prl/dot_general | solution.py:275
  76.5 0.0 copy-done.2
  76.6 0.6 fusion.5
  77.1 0.7 copy.72
  77.8 0.0 copy-start.9
  77.8 0.0 copy-start.10
  77.8 8.8 %shard_map.96 = f32[2,32,128]{2,1,0:T(8,128)} custom-call(f32[4,2,32,128]{3,2,1,0:T(8,128)} %bitcast.68), custom_call_target="tpu_custom_call" | custom-call | tf_op jit(solution)/shard_map/pallas_call | solution.py:220
  86.6 0.0 copy-start.5
  86.7 0.0 copy-done.9
  86.7 0.0 copy-done.10
  86.7 0.1 constant_dynamic-slice_fusion.1
  86.8 0.1 copy.35
  86.8 0.1 copy.36
  86.9 0.1 fusion.14
  87.0 0.1 copy.37
  87.1 0.3 copy-done.5
  87.4 0.8 broadcast_multiply_fusion.send_ref
  88.2 14.8 %shard_map.97 = f32[2,32,128]{2,1,0:T(8,128)} custom-call(f32[8,2,32,128]{3,2,1,0:T(8,128)} %broadcast_multiply_fusion.send_ref), custom_call_target="tpu_custom_call" | custom-call | tf_op jit(solution)/shard_map/pallas_call | solution.py:220
  103.0 0.0 copy-start.6
  103.0 0.1 dynamic-slice_bitcast_fusion
  103.1 0.6 copy.40
  103.8 0.2 copy-done.6
  103.9 0.1 dynamic-slice_bitcast_fusion.1
  104.0 0.0 copy-start.7
  104.0 0.6 copy.39
  104.7 0.1 copy-done.7
  104.8 0.6 copy.75
  (7 shorter events, 0.1 us)
Async XLA Ops:
  0.6 1.1 %copy-start = (f32[2,128,512]{2,1,0:T(8,128)S(1)}, f32[2,128,512]{2,1,0:T(8,128)}, u32[]{:S(2)}) copy-start(f32[2,128,512]{2,1,0:T(8,128)} %param.7) | copy-start | bytes 1572868
  0.6 0.7 copy-start.8
  3.3 1.0 copy-start.3
  4.3 0.9 copy-start.4
  50.5 1.3 %copy-start.1 = (f32[1024,128]{1,0:T(8,128)S(1)}, f32[1024,128]{1,0:T(8,128)}, u32[]{:S(2)}) copy-start(f32[1024,128]{1,0:T(8,128)} %shard_map.94) | copy-start | bytes 1572868
  75.1 1.5 %copy-start.2 = (f32[128,640]{1,0:T(8,128)S(1)}, f32[128,640]{1,0:T(8,128)}, u32[]{:S(2)}) copy-start(f32[128,640]{1,0:T(8,128)} %get-tuple-element.6) | copy-start | bytes 983044
  77.8 8.9 %copy-start.9 = (s32[128,2]{0,1:T(2,128)S(1)}, s32[128,2]{0,1:T(2,128)}, u32[]{:S(2)}) copy-start(s32[128,2]{0,1:T(2,128)} %param.12) | copy-start | bytes 3076
  77.8 8.9 %copy-start.10 = (s32[128,2]{0,1:T(2,128)S(1)}, s32[128,2]{0,1:T(2,128)}, u32[]{:S(2)}) copy-start(s32[128,2]{0,1:T(2,128)} %param.13) | copy-start | bytes 3076
  86.6 0.8 copy-start.5
  103.0 0.9 copy-start.6
  104.0 0.8 copy-start.7

commit v9 on v8

--- a/solution.py
+++ b/solution.py
@@ -145,19 +145,29 @@
     rank = outputs[0].shape[0]
 
     def step(j, carry):
+        columns, roots = [], []
         for ref in outputs:
             width = ref.shape[1]
             row = ref[pl.ds(j, 1), :]
             lanes = lax.broadcasted_iota(jnp.int32, (1, width), 1)
             pivot = jnp.sum(jnp.where(lanes == j, row, 0.0), axis=1, keepdims=True)
             root = jnp.sqrt(pivot)
-            column = jnp.where(lanes < j, 0.0, row / root)
-            square = ref[:, pl.ds(0, rank)]
-            cols = lax.broadcasted_iota(jnp.int32, (rank, rank), 1)
-            upper = jnp.sum(jnp.where(cols == j, square, 0.0), axis=1, keepdims=True)
-            below = lax.broadcasted_iota(jnp.int32, (rank, 1), 0) > j
-            scale = jnp.where(below, upper / root, 0.0)
-            ref[...] = ref[...] - scale * column
+            columns.append(jnp.where(lanes < j, 0.0, row / root))
+            roots.append(root)
+
+        def chunk(i, inner):
+            rows = pl.ds(pl.multiple_of(i * 8, 8), 8)
+            below = lax.broadcasted_iota(jnp.int32, (8, 1), 0) + i * 8 > j
+            cols = lax.broadcasted_iota(jnp.int32, (8, rank), 1)
+            for ref, column, root in zip(outputs, columns, roots):
+                block = ref[rows, :]
+                upper = jnp.sum(jnp.where(cols == j, block[:, :rank], 0.0), axis=1, keepdims=True)
+                scale = jnp.where(below, upper / root, 0.0)
+                ref[rows, :] = block - scale * column
+            return inner
+
+        lax.fori_loop(j // 8, rank // 8, chunk, 0)
+        for ref, column in zip(outputs, columns):
             ref[pl.ds(j, 1), :] = column
         return carry
 

time: 106 us -> 194 us (1.83)
  Pallas kernels: 87.2 us -> 175 us
    pallas_call x1, Pallas kernels: 20.8 us -> 109 us  [factor_panels(): pl.pallas_call(panel_kernel, out_shape=[jax.ShapeDtypeStruct(p.shape, p.d...]
where the time goes in v9:
time: 194 us; the launch traced here: 193 us
  Pallas kernels  175 us (90%)
  local copies, waits for them, and re-layouts  7.56 us (4%)
  matrix products  6.57 us (3%)
  other arithmetic  3.19 us (2%)
    pallas_call x1, Pallas kernels, factor_panels(): pl.pallas_call(panel_kernel, out_shape=[jax.ShapeDtypeStruct(p.shape, p.d...  109 us
    pallas_call x1, Pallas kernels, allreduce_all(): pl.pallas_call(functools.partial(allreduce_kernel, digits), out_shape=jax...  42.8 us
    pallas_call x2, Pallas kernels, group_sum(): pl.pallas_call(functools.partial(group_kernel, kind, cycle), out_shape=ja...  23.7 us
    unnamed x28, local copies, waits for them, and re-layouts  5.27 us

profile of v9, /device:TPU:32, one launch (start us, length us, event | category | flops | bytes accessed | tf_op | source)
XLA Modules:
  0.0 193.2 jit_solution(7987921575404510349)
XLA Ops:
  0.6 0.0 copy-start
  0.6 0.0 copy-start.8
  0.7 0.7 copy-done.8
  1.4 0.3 copy-done
  1.7 1.6 fusion.3
  3.3 0.0 copy-start.3
  3.4 0.9 copy-done.3
  4.3 0.0 copy-start.4
  4.3 0.3 convolution_dynamic-update-slice_fusion
  4.6 0.6 copy-done.4
  5.2 1.0 fusion.1
  6.2 0.6 fusion.7
  6.8 0.8 pad_maximum_fusion.x_ref
  7.7 42.8 %shard_map.94 = f32[1024,128]{1,0:T(8,128)} custom-call(f32[1024,128]{1,0:T(8,128)} %pad_maximum_fusion.x_ref), custom_call_target="tpu_custom_call" | custom-call | tf_op jit(solution)/shard_map/pallas_call | solution.py:123
  50.5 0.0 copy-start.1
  50.5 1.1 fusion.20
  51.6 0.1 copy.64
  51.7 0.0 copy-done.1
  51.7 1.0 fusion.22
  52.8 0.7 pad_maximum_fusion.2.refs_1_
  53.4 0.1 copy.62
  53.6 0.7 pad_maximum_fusion.1.refs_0_
  54.3 108.6 %shard_map.95 = (f32[128,640]{1,0:T(8,128)}, f32[128,256]{1,0:T(8,128)}) custom-call(f32[128,640]{1,0:T(8,128)} %pad_maximum_fusion.1.refs_0_, f32[128,256]{1,0:T(8,128)} %pad_maximum_fusion.2.refs_1_), custom_call_target="tpu_custom_call" | custom-call | tf_op jit(solution)/shard_map/pallas_call | solution.py:178
  162.9 0.0 copy-start.2
  162.9 1.5 convolution_bitcast_fusion.1
  164.3 0.0 copy-done.2
  164.4 0.6 fusion.5
  164.9 0.7 copy.72
  165.6 0.0 copy-start.9
  165.6 0.0 copy-start.10
  165.6 8.8 %shard_map.96 = f32[2,32,128]{2,1,0:T(8,128)} custom-call(f32[4,2,32,128]{3,2,1,0:T(8,128)} %bitcast.68), custom_call_target="tpu_custom_call" | custom-call | tf_op jit(solution)/shard_map/pallas_call | solution.py:230
  174.4 0.0 copy-start.5
  174.5 0.0 copy-done.9
  174.5 0.0 copy-done.10
  174.5 0.1 constant_dynamic-slice_fusion.1
  174.5 0.1 copy.35
  174.6 0.1 copy.36
  174.7 0.1 fusion.14
  174.8 0.1 copy.37
  174.9 0.3 copy-done.5
  175.2 0.8 broadcast_multiply_fusion.send_ref
  176.0 14.8 %shard_map.97 = f32[2,32,128]{2,1,0:T(8,128)} custom-call(f32[8,2,32,128]{3,2,1,0:T(8,128)} %broadcast_multiply_fusion.send_ref), custom_call_target="tpu_custom_call" | custom-call | tf_op jit(solution)/shard_map/pallas_call | solution.py:230
  190.8 0.0 copy-start.6
  190.9 0.1 dynamic-slice_bitcast_fusion
  191.0 0.6 copy.40
  191.6 0.2 copy-done.6
  191.8 0.1 dynamic-slice_bitcast_fusion.1
  191.8 0.0 copy-start.7
  191.8 0.6 copy.39
  192.5 0.1 copy-done.7
  192.6 0.6 copy.75
  (7 shorter events, 0.1 us)
Async XLA Ops:
  0.6 1.1 copy-start
  0.6 0.7 copy-start.8
  3.3 1.0 copy-start.3
  4.3 0.9 copy-start.4
  50.5 1.3 copy-start.1
  162.9 1.5 copy-start.2
  165.6 8.9 %copy-start.9 = (s32[128,2]{0,1:T(2,128)S(1)}, s32[128,2]{0,1:T(2,128)}, u32[]{:S(2)}) copy-start(s32[128,2]{0,1:T(2,128)} %param.12) | copy-start | bytes 3076
  165.6 8.9 %copy-start.10 = (s32[128,2]{0,1:T(2,128)S(1)}, s32[128,2]{0,1:T(2,128)}, u32[]{:S(2)}) copy-start(s32[128,2]{0,1:T(2,128)} %param.13) | copy-start | bytes 3076
  174.4 0.8 copy-start.5
  190.8 0.9 copy-start.6
  191.8 0.8 copy-start.7

commit v10 on v8

--- a/solution.py
+++ b/solution.py
@@ -144,7 +144,7 @@
         target[...] = source[...]
     rank = outputs[0].shape[0]
 
-    def step(j, carry):
+    def step(first, j, carry):
         for ref in outputs:
             width = ref.shape[1]
             row = ref[pl.ds(j, 1), :]
@@ -152,16 +152,19 @@
             pivot = jnp.sum(jnp.where(lanes == j, row, 0.0), axis=1, keepdims=True)
             root = jnp.sqrt(pivot)
             column = jnp.where(lanes < j, 0.0, row / root)
-            square = ref[:, pl.ds(0, rank)]
-            cols = lax.broadcasted_iota(jnp.int32, (rank, rank), 1)
-            upper = jnp.sum(jnp.where(cols == j, square, 0.0), axis=1, keepdims=True)
-            below = lax.broadcasted_iota(jnp.int32, (rank, 1), 0) > j
+            count = rank - first
+            block = ref[pl.ds(first, count), :]
+            cols = lax.broadcasted_iota(jnp.int32, (count, rank), 1)
+            upper = jnp.sum(jnp.where(cols == j, block[:, :rank], 0.0), axis=1, keepdims=True)
+            below = lax.broadcasted_iota(jnp.int32, (count, 1), 0) + first > j
             scale = jnp.where(below, upper / root, 0.0)
-            ref[...] = ref[...] - scale * column
+            ref[pl.ds(first, count), :] = block - scale * column
             ref[pl.ds(j, 1), :] = column
         return carry
 
-    lax.fori_loop(0, rank, step, 0)
+    span = 16
+    for first in range(0, rank, span):
+        lax.fori_loop(first, first + span, functools.partial(step, first), 0)
 
 
 def factor_panels(*panels):

time: 106 us -> 104 us (0.981)
  Pallas kernels: 87.2 us -> 85.1 us
    pallas_call x1, Pallas kernels: 20.8 us -> 18.6 us  [factor_panels(): pl.pallas_call(panel_kernel, out_shape=[jax.ShapeDtypeStruct(p.shape, p.d...]
where the time goes in v10:
time: 104 us; the launch traced here: 103 us
  Pallas kernels  85.1 us (82%)
  local copies, waits for them, and re-layouts  7.56 us (7%)
  matrix products  6.57 us (6%)
  other arithmetic  3.19 us (3%)
    pallas_call x1, Pallas kernels, allreduce_all(): pl.pallas_call(functools.partial(allreduce_kernel, digits), out_shape=jax...  42.8 us
    pallas_call x2, Pallas kernels, group_sum(): pl.pallas_call(functools.partial(group_kernel, kind, cycle), out_shape=ja...  23.6 us
    pallas_call x1, Pallas kernels, factor_panels(): pl.pallas_call(panel_kernel, out_shape=[jax.ShapeDtypeStruct(p.shape, p.d...  18.6 us
    unnamed x28, local copies, waits for them, and re-layouts  5.27 us

profile of v10, /device:TPU:32, one launch (start us, length us, event | category | flops | bytes accessed | tf_op | source)
XLA Modules:
  0.0 103.3 jit_solution(10862233807771319953)
XLA Ops:
  0.6 0.0 copy-start
  0.6 0.0 copy-start.8
  0.7 0.7 copy-done.8
  1.4 0.3 copy-done
  1.7 1.6 %fusion.3 = f32[256,128]{0,1:T(8,128)S(1)} fusion(f32[2,128,512]{2,1,0:T(8,128)S(1)} %copy-done, f32[512,256]{1,0:T(8,128)} %param.10, f32[256,2]{0,1:T(2,128)S(1)} %get-tuple-element.23), kind=kOutput, calls=%fused_computation.6 | convolution fusion | flops 402751488 | bytes 1181696 | tf_op jit(solution)/shard_map/pjl,lk->pjk/dot_general | solution.py:247
  3.3 0.0 copy-start.3
  3.4 0.9 copy-done.3
  4.3 0.0 copy-start.4
  4.3 0.3 convolution_dynamic-update-slice_fusion
  4.6 0.6 copy-done.4
  5.2 1.0 fusion.1
  6.2 0.6 fusion.7
  6.8 0.8 pad_maximum_fusion.x_ref
  7.7 42.8 %shard_map.94 = f32[1024,128]{1,0:T(8,128)} custom-call(f32[1024,128]{1,0:T(8,128)} %pad_maximum_fusion.x_ref), custom_call_target="tpu_custom_call" | custom-call | tf_op jit(solution)/shard_map/pallas_call | solution.py:123
  50.5 0.0 copy-start.1
  50.5 1.1 %fusion.20 = (f32[512,128]{1,0:T(8,128)S(1)}, f32[512,128]{1,0:T(8,128)S(1)}) fusion(f32[1024,128]{1,0:T(8,128)} %shard_map.94), kind=kLoop, calls=%fused_computation.39 | loop fusion | bytes 1048576 | tf_op jit(solution)/shard_map/slice | solution.py:264
  51.6 0.1 copy.64
  51.7 0.0 copy-done.1
  51.7 1.0 fusion.22
  52.8 0.7 pad_maximum_fusion.2.refs_1_
  53.4 0.1 copy.62
  53.6 0.7 pad_maximum_fusion.1.refs_0_
  54.3 18.6 %shard_map.95 = (f32[128,640]{1,0:T(8,128)}, f32[128,256]{1,0:T(8,128)}) custom-call(f32[128,640]{1,0:T(8,128)} %pad_maximum_fusion.1.refs_0_, f32[128,256]{1,0:T(8,128)} %pad_maximum_fusion.2.refs_1_), custom_call_target="tpu_custom_call" | custom-call | tf_op jit(solution)/shard_map/pallas_call | solution.py:171
  72.9 0.0 copy-start.2
  72.9 1.5 %convolution_bitcast_fusion.1 = f32[2,128,512]{2,1,0:T(8,128)S(1)} fusion(f32[2,128,512]{2,1,0:T(8,128)S(1)} %copy-done, f32[128,256]{1,0:T(8,128)} %get-tuple-element.5), kind=kOutput, calls=%fused_computation.3 | convolution fusion | flops 201326592 | bytes 1114112 | tf_op jit(solution)/shard_map/jr,pjl->prl/dot_general | solution.py:278
  74.4 0.0 copy-done.2
  74.4 0.6 fusion.5
  75.0 0.7 copy.72
  75.7 0.0 copy-start.9
  75.7 0.0 copy-start.10
  75.7 8.8 %shard_map.96 = f32[2,32,128]{2,1,0:T(8,128)} custom-call(f32[4,2,32,128]{3,2,1,0:T(8,128)} %bitcast.68), custom_call_target="tpu_custom_call" | custom-call | tf_op jit(solution)/shard_map/pallas_call | solution.py:223
  84.5 0.0 copy-start.5
  84.5 0.0 copy-done.9
  84.5 0.0 copy-done.10
  84.5 0.1 constant_dynamic-slice_fusion.1
  84.6 0.1 copy.35
  84.7 0.1 copy.36
  84.8 0.1 fusion.14
  84.9 0.1 copy.37
  85.0 0.3 copy-done.5
  85.3 0.8 broadcast_multiply_fusion.send_ref
  86.0 14.8 %shard_map.97 = f32[2,32,128]{2,1,0:T(8,128)} custom-call(f32[8,2,32,128]{3,2,1,0:T(8,128)} %broadcast_multiply_fusion.send_ref), custom_call_target="tpu_custom_call" | custom-call | tf_op jit(solution)/shard_map/pallas_call | solution.py:223
  100.9 0.0 copy-start.6
  100.9 0.1 dynamic-slice_bitcast_fusion
  101.0 0.6 copy.40
  101.7 0.2 copy-done.6
  101.8 0.1 dynamic-slice_bitcast_fusion.1
  101.9 0.0 copy-start.7
  101.9 0.6 copy.39
  102.5 0.1 copy-done.7
  102.7 0.6 copy.75
  (7 shorter events, 0.1 us)
Async XLA Ops:
  0.6 1.1 %copy-start = (f32[2,128,512]{2,1,0:T(8,128)S(1)}, f32[2,128,512]{2,1,0:T(8,128)}, u32[]{:S(2)}) copy-start(f32[2,128,512]{2,1,0:T(8,128)} %param.7) | copy-start | bytes 1572868
  0.6 0.7 copy-start.8
  3.3 1.0 copy-start.3
  4.3 0.9 copy-start.4
  50.5 1.3 %copy-start.1 = (f32[1024,128]{1,0:T(8,128)S(1)}, f32[1024,128]{1,0:T(8,128)}, u32[]{:S(2)}) copy-start(f32[1024,128]{1,0:T(8,128)} %shard_map.94) | copy-start | bytes 1572868
  72.9 1.5 %copy-start.2 = (f32[128,640]{1,0:T(8,128)S(1)}, f32[128,640]{1,0:T(8,128)}, u32[]{:S(2)}) copy-start(f32[128,640]{1,0:T(8,128)} %get-tuple-element.6) | copy-start | bytes 983044
  75.7 8.8 %copy-start.9 = (s32[128,2]{0,1:T(2,128)S(1)}, s32[128,2]{0,1:T(2,128)}, u32[]{:S(2)}) copy-start(s32[128,2]{0,1:T(2,128)} %param.12) | copy-start | bytes 3076
  75.7 8.8 %copy-start.10 = (s32[128,2]{0,1:T(2,128)S(1)}, s32[128,2]{0,1:T(2,128)}, u32[]{:S(2)}) copy-start(s32[128,2]{0,1:T(2,128)} %param.13) | copy-start | bytes 3076
  84.5 0.8 copy-start.5
  100.9 0.9 copy-start.6
  101.9 0.8 copy-start.7

commit v11 on v10

--- a/solution.py
+++ b/solution.py
@@ -176,62 +176,75 @@
     )(*panels)
 
 
-def group_kernel(kind, cycle, send_ref, o_ref, recv, send_sem, recv_sem):
+def core_kernel(cycle, pieces_ref, weights_ref, o_ref, first, staged, second, send_sem, recv_sem):
     g = lax.axis_index("gx")
     a = lax.axis_index("af")
-    size = send_ref.shape[0]
-    if kind == "af":
-        me = a
-
-        def device(j):
-            return (g, j)
-    else:
-        me = g // cycle
-
-        def device(j):
-            return (j * cycle + g % cycle, a)
-
-    members = [(me + d) % size for d in range(1, size)]
+    quarters, blocks = pieces_ref.shape[0], weights_ref.shape[0]
+    k = g // cycle
+    c = g % cycle
+    peers = [(a + d) % quarters for d in range(1, quarters)]
+    owners = [(k + d) % blocks for d in range(1, blocks)]
+
+    def peer(j):
+        return (g, j)
+
+    def owner(j):
+        return (j * cycle + c, a)
+
     barrier = pltpu.get_barrier_semaphore()
-    for j in members:
-        pl.semaphore_signal(barrier, inc=1, device_id=device(j), device_id_type=MESH)
-    pl.semaphore_wait(barrier, len(members))
-
-    copies = []
-    for n, j in enumerate(members):
+    for device in [peer(j) for j in peers] + [owner(j) for j in owners]:
+        pl.semaphore_signal(barrier, inc=1, device_id=device, device_id_type=MESH)
+    pl.semaphore_wait(barrier, len(peers) + len(owners))
+
+    def start(n, source, target, device):
         copy = pltpu.make_async_remote_copy(
-            src_ref=send_ref.at[j],
-            dst_ref=recv.at[n],
+            src_ref=source,
+            dst_ref=target,
             send_sem=send_sem.at[n],
             recv_sem=recv_sem.at[n],
-            device_id=device(j),
+            device_id=device,
             device_id_type=MESH,
         )
         copy.start()
-        copies.append(copy)
+        return copy
+
+    copies = [start(n, pieces_ref.at[j], first.at[n], peer(j)) for n, j in enumerate(peers)]
     for copy in copies:
         copy.wait()
-    total = send_ref[me]
-    for n in range(len(members)):
-        total = total + recv[n]
-    o_ref[...] = total
-
-
-def group_sum(pieces, kind, cycle, collective_id):
-    size = pieces.shape[0]
+    total = pieces_ref[a]
+    for n in range(len(peers)):
+        total = total + first[n]
+    for j in range(blocks):
+        staged[j] = weights_ref[j] * total
+    base = len(peers)
+    copies = [
+        start(base + n, staged.at[j], second.at[n], owner(j)) for n, j in enumerate(owners)
+    ]
+    for copy in copies:
+        copy.wait()
+    result = staged[k]
+    for n in range(len(owners)):
+        result = result + second[n]
+    o_ref[...] = result
+
+
+def core_exchange(pieces, weights, cycle):
+    quarters, blocks = pieces.shape[0], weights.shape[0]
     piece = pieces.shape[1:]
     return pl.pallas_call(
-        functools.partial(group_kernel, kind, cycle),
+        functools.partial(core_kernel, cycle),
         out_shape=jax.ShapeDtypeStruct(piece, pieces.dtype),
-        in_specs=[pl.BlockSpec(memory_space=pltpu.VMEM)],
+        in_specs=[pl.BlockSpec(memory_space=pltpu.VMEM)] * 2,
         out_specs=pl.BlockSpec(memory_space=pltpu.VMEM),
         scratch_shapes=[
-            pltpu.VMEM((size - 1,) + piece, pieces.dtype),
-            pltpu.SemaphoreType.DMA((size - 1,)),
-            pltpu.SemaphoreType.DMA((size - 1,)),
+            pltpu.VMEM((quarters - 1,) + piece, pieces.dtype),
+            pltpu.VMEM((blocks,) + piece, pieces.dtype),
+            pltpu.VMEM((blocks - 1,) + piece, pieces.dtype),
+            pltpu.SemaphoreType.DMA((quarters + blocks - 2,)),
+            pltpu.SemaphoreType.DMA((quarters + blocks - 2,)),
         ],
-        compiler_params=pltpu.CompilerParams(collective_id=collective_id, has_side_effects=True),
-    )(pieces)
+        compiler_params=pltpu.CompilerParams(collective_id=1, has_side_effects=True),
+    )(pieces, weights)
 
 
 def body(
@@ -290,9 +303,8 @@
     )
     slab = rank_cols // af_size
     pieces = projected.reshape(planes, af_size, slab, rank_cols).transpose(1, 0, 2, 3)
-    summed = group_sum(pieces, "af", cycle, 1)
-    contributions = weights[:, :, None, None] * summed[None]
-    core_sketch = group_sum(contributions, "gx", cycle, 2)
+    lane_weights = jnp.broadcast_to(weights[:, :, None, None], (groups, planes, 1, rank_cols))
+    core_sketch = core_exchange(pieces, lane_weights, cycle)
     return (factor_second, factor_third, core_sketch)
 
 

time: 104 us -> 101 us (0.971)
  Pallas kernels: 85.1 us -> 81.7 us
  local copies, waits for them, and re-layouts: 7.56 us -> 8.65 us
    pallas_call x2 -> x1, Pallas kernels: 23.6 us -> 20.3 us  [core_exchange(): pl.pallas_call(functools.partial(core_kernel, cycle), out_shape=jax.Shape...]
    unnamed x28 -> x26, local copies, waits for them, and re-layouts: 5.27 us -> 5.67 us
where the time goes in v11:
time: 101 us; the launch traced here: 100 us
  Pallas kernels  81.7 us (81%)
  local copies, waits for them, and re-layouts  8.65 us (9%)
  matrix products  6.56 us (6%)
  other arithmetic  2.41 us (2%)
    pallas_call x1, Pallas kernels, allreduce_all(): pl.pallas_call(functools.partial(allreduce_kernel, digits), out_shape=jax...  42.8 us
    pallas_call x1, Pallas kernels, core_exchange(): pl.pallas_call(functools.partial(core_kernel, cycle), out_shape=jax.Shape...  20.3 us
    pallas_call x1, Pallas kernels, factor_panels(): pl.pallas_call(panel_kernel, out_shape=[jax.ShapeDtypeStruct(p.shape, p.d...  18.6 us
    unnamed x26, local copies, waits for them, and re-layouts  5.67 us

profile of v11, /device:TPU:32, one launch (start us, length us, event | category | flops | bytes accessed | tf_op | source)
XLA Modules:
  0.0 100.2 jit_solution(14240331517434215332)
XLA Ops:
  0.6 0.0 copy-start
  0.6 0.0 copy-start.7
  0.7 0.7 copy-done.7
  1.4 0.3 copy-done
  1.7 1.6 %fusion.3 = f32[256,128]{0,1:T(8,128)S(1)} fusion(f32[2,128,512]{2,1,0:T(8,128)S(1)} %copy-done, f32[512,256]{1,0:T(8,128)} %param.10, f32[256,2]{0,1:T(2,128)S(1)} %get-tuple-element.23), kind=kOutput, calls=%fused_computation.6 | convolution fusion | flops 402751488 | bytes 1181696 | tf_op jit(solution)/shard_map/pjl,lk->pjk/dot_general | solution.py:260
  3.3 0.0 copy-start.3
  3.4 0.9 copy-done.3
  4.3 0.0 copy-start.4
  4.3 0.3 convolution_dynamic-update-slice_fusion
  4.6 0.6 copy-done.4
  5.2 1.0 %fusion.1 = f32[256,512]{0,1:T(8,128)S(1)} fusion(f32[2,128,512]{2,1,0:T(8,128)S(1)} %copy-done, f32[256,2]{0,1:T(2,128)S(1)} %get-tuple-element.22, f32[128,256]{1,0:T(8,128)S(1)} %copy-done.4), kind=kOutput, calls=%fused_computation.2 | convolution fusion | flops 403046400 | bytes 1181696 | tf_op jit(solution)/shard_map/pjl,jk->plk/dot_general | solution.py:264
  6.2 0.6 fusion.7
  6.8 0.8 pad_maximum_fusion.x_ref
  7.6 42.8 %shard_map.94 = f32[1024,128]{1,0:T(8,128)} custom-call(f32[1024,128]{1,0:T(8,128)} %pad_maximum_fusion.x_ref), custom_call_target="tpu_custom_call" | custom-call | tf_op jit(solution)/shard_map/pallas_call | solution.py:123
  50.4 0.0 copy-start.1
  50.4 1.1 %fusion.20 = (f32[512,128]{1,0:T(8,128)S(1)}, f32[512,128]{1,0:T(8,128)S(1)}) fusion(f32[1024,128]{1,0:T(8,128)} %shard_map.94), kind=kLoop, calls=%fused_computation.38 | loop fusion | bytes 1048576 | tf_op jit(solution)/shard_map/slice | solution.py:277
  51.6 0.1 copy.64
  51.7 0.0 copy-done.1
  51.7 1.0 %fusion.22 = f32[2,128,128]{2,1,0:T(8,128)S(1)} fusion(f32[2,512,128]{2,1,0:T(8,128)S(1)} %bitcast.65), kind=kOutput, calls=%fused_computation.40 | convolution fusion | flops 201326592 | bytes 655360 | tf_op jit(solution)/shard_map/nji,njk->nik/dot_general | solution.py:276
  52.7 0.7 pad_maximum_fusion.2.refs_1_
  53.4 0.1 copy.62
  53.5 0.7 pad_maximum_fusion.1.refs_0_
  54.3 18.6 %shard_map.95 = (f32[128,640]{1,0:T(8,128)}, f32[128,256]{1,0:T(8,128)}) custom-call(f32[128,640]{1,0:T(8,128)} %pad_maximum_fusion.1.refs_0_, f32[128,256]{1,0:T(8,128)} %pad_maximum_fusion.2.refs_1_), custom_call_target="tpu_custom_call" | custom-call | tf_op jit(solution)/shard_map/pallas_call | solution.py:171
  72.9 0.0 copy-start.2
  72.9 1.5 %convolution_bitcast_fusion.1 = f32[2,128,512]{2,1,0:T(8,128)S(1)} fusion(f32[2,128,512]{2,1,0:T(8,128)S(1)} %copy-done, f32[128,256]{1,0:T(8,128)} %get-tuple-element.5), kind=kOutput, calls=%fused_computation.3 | convolution fusion | flops 201326592 | bytes 1114112 | tf_op jit(solution)/shard_map/jr,pjl->prl/dot_general | solution.py:291
  74.4 0.0 copy-done.2
  74.4 0.6 fusion.5
  75.0 0.7 copy.72
  75.6 0.0 copy-start.8
  75.7 0.0 copy-start.9
  75.7 0.7 copy-done.8
  76.3 0.0 copy-done.9
  76.3 0.1 constant_dynamic-slice_fusion.1
  76.4 0.1 copy.36
  76.5 0.1 copy.37
  76.6 0.1 fusion.14
  76.7 0.1 copy.38
  76.8 0.7 broadcast_in_dim.27.weights_ref
  77.5 20.3 %shard_map.96 = f32[2,32,128]{2,1,0:T(8,128)} custom-call(f32[4,2,32,128]{3,2,1,0:T(8,128)} %bitcast.68, f32[8,2,1,128]{3,2,1,0:T(1,128)} %broadcast_in_dim.27.weights_ref), custom_call_target="tpu_custom_call" | custom-call | tf_op jit(solution)/shard_map/pallas_call | solution.py:234
  97.8 0.0 copy-start.5
  97.8 0.1 dynamic-slice_bitcast_fusion
  97.9 0.6 copy.40
  98.5 0.2 copy-done.5
  98.7 0.1 dynamic-slice_bitcast_fusion.1
  98.8 0.0 copy-start.6
  98.8 0.6 copy.39
  99.4 0.1 copy-done.6
  99.5 0.6 copy.75
  (7 shorter events, 0.1 us)
Async XLA Ops:
  0.6 1.1 %copy-start = (f32[2,128,512]{2,1,0:T(8,128)S(1)}, f32[2,128,512]{2,1,0:T(8,128)}, u32[]{:S(2)}) copy-start(f32[2,128,512]{2,1,0:T(8,128)} %param.7) | copy-start | bytes 1572868
  0.6 0.7 copy-start.7
  3.3 1.0 copy-start.3
  4.3 0.9 copy-start.4
  50.4 1.3 %copy-start.1 = (f32[1024,128]{1,0:T(8,128)S(1)}, f32[1024,128]{1,0:T(8,128)}, u32[]{:S(2)}) copy-start(f32[1024,128]{1,0:T(8,128)} %shard_map.94) | copy-start | bytes 1572868
  72.9 1.5 %copy-start.2 = (f32[128,640]{1,0:T(8,128)S(1)}, f32[128,640]{1,0:T(8,128)}, u32[]{:S(2)}) copy-start(f32[128,640]{1,0:T(8,128)} %get-tuple-element.6) | copy-start | bytes 983044
  75.6 0.7 copy-start.8
  75.7 0.7 copy-start.9
  97.8 0.9 copy-start.5
  98.8 0.8 copy-start.6

commit v12 on v11

--- a/solution.py
+++ b/solution.py
@@ -36,21 +36,27 @@
         return [(index[axis] // bit) % 2 for axis, bit in digit]
 
     def member(digit):
-        own = bits_of(digit)
-        return own[0] + 2 * own[1]
+        return sum(own * 2**t for t, own in enumerate(bits_of(digit)))
+
+    def flipped(digit, d):
+        return sum(
+            (own + ((d >> t) & 1) * (1 - 2 * own)) * 2**t for t, own in enumerate(bits_of(digit))
+        )
 
     def device(digit, d):
         values = dict(index)
         for t, ((axis, bit), own) in enumerate(zip(digit, bits_of(digit))):
-            flip = (d >> t) & 1
-            values[axis] = values[axis] + bit * flip * (1 - 2 * own)
+            values[axis] = values[axis] + bit * ((d >> t) & 1) * (1 - 2 * own)
         return (values["gx"], values["af"])
+
+    def others(digit):
+        return range(1, 2 ** len(digit))
 
     barrier = pltpu.get_barrier_semaphore()
     for digit in digits:
-        for d in (1, 2, 3):
+        for d in others(digit):
             pl.semaphore_signal(barrier, inc=1, device_id=device(digit, d), device_id_type=MESH)
-    pl.semaphore_wait(barrier, 3 * len(digits))
+    pl.semaphore_wait(barrier, sum(len(others(digit)) for digit in digits))
 
     counter = [0]
 
@@ -68,45 +74,42 @@
         copy.start()
         return copy
 
-    def flipped(me, d):
-        low, high = me % 2, me // 2
-        low = low + (d & 1) * (1 - 2 * low)
-        high = high + ((d >> 1) & 1) * (1 - 2 * high)
-        return low + 2 * high
-
     acc[...] = x_ref[...]
     offset, length, slot = 0, acc.shape[0], 0
     parents = []
     for digit in digits[:-1]:
         me = member(digit)
-        quarter = length // 4
+        part = length // 2 ** len(digit)
         copies = []
-        for d in (1, 2, 3):
-            give = pl.multiple_of(offset + flipped(me, d) * quarter, 8)
-            target = recv.at[pl.ds(slot + (d - 1) * quarter, quarter)]
-            copies.append(start(device(digit, d), acc.at[pl.ds(give, quarter)], target))
+        for d in others(digit):
+            give = pl.multiple_of(offset + flipped(digit, d) * part, 8)
+            target = recv.at[pl.ds(slot + (d - 1) * part, part)]
+            copies.append(start(device(digit, d), acc.at[pl.ds(give, part)], target))
         for copy in copies:
             copy.wait()
-        keep = pl.multiple_of(offset + me * quarter, 8)
-        total = acc[pl.ds(keep, quarter), :]
-        for d in (1, 2, 3):
-            total = total + recv[pl.ds(slot + (d - 1) * quarter, quarter), :]
-        acc[pl.ds(keep, quarter), :] = total
+        keep = pl.multiple_of(offset + me * part, 8)
+        total = acc[pl.ds(keep, part), :]
+        for d in others(digit):
+            total = total + recv[pl.ds(slot + (d - 1) * part, part), :]
+        acc[pl.ds(keep, part), :] = total
         parents.append((offset, length))
-        offset, length, slot = keep, quarter, slot + 3 * quarter
+        offset, length, slot = keep, part, slot + len(others(digit)) * part
 
     last = digits[-1]
     me = member(last)
     segment = acc.at[pl.ds(offset, length)]
-    copies = [start(device(last, d), segment, exchange.at[me]) for d in (1, 2, 3)]
+    copies = [start(device(last, d), segment, exchange.at[me]) for d in others(last)]
     exchange[me] = acc[pl.ds(offset, length), :]
     for copy in copies:
         copy.wait()
-    gathered[pl.ds(offset, length), :] = ((exchange[0] + exchange[1]) + exchange[2]) + exchange[3]
+    total = exchange[0]
+    for q in range(1, 2 ** len(last)):
+        total = total + exchange[q]
+    gathered[pl.ds(offset, length), :] = total
 
     for digit, (parent_offset, parent_length) in zip(reversed(digits[:-1]), reversed(parents)):
         part = gathered.at[pl.ds(offset, length)]
-        copies = [start(device(digit, d), part, part) for d in (1, 2, 3)]
+        copies = [start(device(digit, d), part, part) for d in others(digit)]
         for copy in copies:
             copy.wait()
         offset, length = parent_offset, parent_length
@@ -115,11 +118,12 @@
 
 def allreduce_all(x):
     steps = partner_list(lax.axis_size("gx"), lax.axis_size("af"))
-    assert len(steps) % 2 == 0
-    digits = [steps[t:t + 2] for t in range(0, len(steps), 2)]
-    last_rows = x.shape[0] // 4 ** (len(digits) - 1)
+    digits = [steps[t:t + 3] for t in range(0, len(steps), 3)]
+    last_rows = x.shape[0]
+    for digit in digits[:-1]:
+        last_rows //= 2 ** len(digit)
     assert last_rows % 8 == 0
-    copies = 3 * (2 * len(digits) - 1)
+    copies = sum(2 * (2 ** len(digit) - 1) for digit in digits[:-1]) + 2 ** len(digits[-1]) - 1
     return pl.pallas_call(
         functools.partial(allreduce_kernel, digits),
         out_shape=jax.ShapeDtypeStruct(x.shape, x.dtype),
@@ -128,7 +132,7 @@
         scratch_shapes=[
             pltpu.VMEM(x.shape, x.dtype),
             pltpu.VMEM(x.shape, x.dtype),
-            pltpu.VMEM((4, last_rows) + x.shape[1:], x.dtype),
+            pltpu.VMEM((2 ** len(digits[-1]), last_rows) + x.shape[1:], x.dtype),
             pltpu.VMEM(x.shape, x.dtype),
             pltpu.SemaphoreType.DMA((copies,)),
             pltpu.SemaphoreType.DMA((copies,)),

time: 101 us -> 97.2 us (0.962)
  Pallas kernels: 81.7 us -> 78.3 us
    pallas_call x1, Pallas kernels: 42.8 us -> 39.5 us  [allreduce_all(): pl.pallas_call(functools.partial(allreduce_kernel, digits), out_shape=jax...]
where the time goes in v12:
time: 97.2 us; the launch traced here: 96.8 us
  Pallas kernels  78.3 us (81%)
  local copies, waits for them, and re-layouts  8.65 us (9%)
  matrix products  6.57 us (7%)
  other arithmetic  2.41 us (2%)
    pallas_call x1, Pallas kernels, allreduce_all(): pl.pallas_call(functools.partial(allreduce_kernel, digits), out_shape=jax...  39.5 us
    pallas_call x1, Pallas kernels, core_exchange(): pl.pallas_call(functools.partial(core_kernel, cycle), out_shape=jax.Shape...  20.2 us
    pallas_call x1, Pallas kernels, factor_panels(): pl.pallas_call(panel_kernel, out_shape=[jax.ShapeDtypeStruct(p.shape, p.d...  18.6 us
    unnamed x26, local copies, waits for them, and re-layouts  5.67 us

profile of v12, /device:TPU:32, one launch (start us, length us, event | category | flops | bytes accessed | tf_op | source)
XLA Modules:
  0.0 96.8 jit_solution(16112604122830089790)
XLA Ops:
  0.6 0.0 copy-start
  0.6 0.0 copy-start.7
  0.7 0.7 copy-done.7
  1.4 0.3 copy-done
  1.7 1.6 %fusion.3 = f32[256,128]{0,1:T(8,128)S(1)} fusion(f32[2,128,512]{2,1,0:T(8,128)S(1)} %copy-done, f32[512,256]{1,0:T(8,128)} %param.10, f32[256,2]{0,1:T(2,128)S(1)} %get-tuple-element.23), kind=kOutput, calls=%fused_computation.6 | convolution fusion | flops 402751488 | bytes 1181696 | tf_op jit(solution)/shard_map/pjl,lk->pjk/dot_general | solution.py:264
  3.3 0.0 copy-start.3
  3.4 0.9 copy-done.3
  4.3 0.0 copy-start.4
  4.3 0.3 convolution_dynamic-update-slice_fusion
  4.6 0.6 copy-done.4
  5.2 1.0 %fusion.1 = f32[256,512]{0,1:T(8,128)S(1)} fusion(f32[2,128,512]{2,1,0:T(8,128)S(1)} %copy-done, f32[256,2]{0,1:T(2,128)S(1)} %get-tuple-element.22, f32[128,256]{1,0:T(8,128)S(1)} %copy-done.4), kind=kOutput, calls=%fused_computation.2 | convolution fusion | flops 403046400 | bytes 1181696 | tf_op jit(solution)/shard_map/pjl,jk->plk/dot_general | solution.py:268
  6.2 0.6 fusion.7
  6.8 0.8 pad_maximum_fusion.x_ref
  7.6 39.5 %shard_map.94 = f32[1024,128]{1,0:T(8,128)} custom-call(f32[1024,128]{1,0:T(8,128)} %pad_maximum_fusion.x_ref), custom_call_target="tpu_custom_call" | custom-call | tf_op jit(solution)/shard_map/pallas_call | solution.py:127
  47.1 0.0 copy-start.1
  47.2 1.1 %fusion.20 = (f32[512,128]{1,0:T(8,128)S(1)}, f32[512,128]{1,0:T(8,128)S(1)}) fusion(f32[1024,128]{1,0:T(8,128)} %shard_map.94), kind=kLoop, calls=%fused_computation.38 | loop fusion | bytes 1048576 | tf_op jit(solution)/shard_map/slice | solution.py:281
  48.3 0.1 copy.64
  48.4 0.0 copy-done.1
  48.4 1.0 %fusion.22 = f32[2,128,128]{2,1,0:T(8,128)S(1)} fusion(f32[2,512,128]{2,1,0:T(8,128)S(1)} %bitcast.65), kind=kOutput, calls=%fused_computation.40 | convolution fusion | flops 201326592 | bytes 655360 | tf_op jit(solution)/shard_map/nji,njk->nik/dot_general | solution.py:280
  49.4 0.7 pad_maximum_fusion.2.refs_1_
  50.1 0.1 copy.62
  50.3 0.7 pad_maximum_fusion.1.refs_0_
  51.0 18.6 %shard_map.95 = (f32[128,640]{1,0:T(8,128)}, f32[128,256]{1,0:T(8,128)}) custom-call(f32[128,640]{1,0:T(8,128)} %pad_maximum_fusion.1.refs_0_, f32[128,256]{1,0:T(8,128)} %pad_maximum_fusion.2.refs_1_), custom_call_target="tpu_custom_call" | custom-call | tf_op jit(solution)/shard_map/pallas_call | solution.py:175
  69.6 0.0 copy-start.2
  69.6 1.5 %convolution_bitcast_fusion.1 = f32[2,128,512]{2,1,0:T(8,128)S(1)} fusion(f32[2,128,512]{2,1,0:T(8,128)S(1)} %copy-done, f32[128,256]{1,0:T(8,128)} %get-tuple-element.5), kind=kOutput, calls=%fused_computation.3 | convolution fusion | flops 201326592 | bytes 1114112 | tf_op jit(solution)/shard_map/jr,pjl->prl/dot_general | solution.py:295
  71.1 0.0 copy-done.2
  71.1 0.6 fusion.5
  71.7 0.7 copy.72
  72.4 0.0 copy-start.8
  72.4 0.0 copy-start.9
  72.4 0.7 copy-done.8
  73.0 0.0 copy-done.9
  73.1 0.1 constant_dynamic-slice_fusion.1
  73.1 0.1 copy.36
  73.2 0.1 copy.37
  73.3 0.1 fusion.14
  73.4 0.1 copy.38
  73.5 0.7 broadcast_in_dim.27.weights_ref
  74.2 20.2 %shard_map.96 = f32[2,32,128]{2,1,0:T(8,128)} custom-call(f32[4,2,32,128]{3,2,1,0:T(8,128)} %bitcast.68, f32[8,2,1,128]{3,2,1,0:T(1,128)} %broadcast_in_dim.27.weights_ref), custom_call_target="tpu_custom_call" | custom-call | tf_op jit(solution)/shard_map/pallas_call | solution.py:238
  94.4 0.0 copy-start.5
  94.5 0.1 dynamic-slice_bitcast_fusion
  94.6 0.6 copy.40
  95.2 0.2 copy-done.5
  95.4 0.1 dynamic-slice_bitcast_fusion.1
  95.4 0.0 copy-start.6
  95.4 0.6 copy.39
  96.1 0.1 copy-done.6
  96.2 0.6 copy.75
  (7 shorter events, 0.1 us)
Async XLA Ops:
  0.6 1.1 %copy-start = (f32[2,128,512]{2,1,0:T(8,128)S(1)}, f32[2,128,512]{2,1,0:T(8,128)}, u32[]{:S(2)}) copy-start(f32[2,128,512]{2,1,0:T(8,128)} %param.7) | copy-start | bytes 1572868
  0.6 0.7 copy-start.7
  3.3 1.0 copy-start.3
  4.3 0.9 copy-start.4
  47.1 1.3 %copy-start.1 = (f32[1024,128]{1,0:T(8,128)S(1)}, f32[1024,128]{1,0:T(8,128)}, u32[]{:S(2)}) copy-start(f32[1024,128]{1,0:T(8,128)} %shard_map.94) | copy-start | bytes 1572868
  69.6 1.5 %copy-start.2 = (f32[128,640]{1,0:T(8,128)S(1)}, f32[128,640]{1,0:T(8,128)}, u32[]{:S(2)}) copy-start(f32[128,640]{1,0:T(8,128)} %get-tuple-element.6) | copy-start | bytes 983044
  72.4 0.7 copy-start.8
  72.4 0.7 copy-start.9
  94.4 0.9 copy-start.5
  95.4 0.8 copy-start.6

commit v13 on v12

--- a/solution.py
+++ b/solution.py
@@ -153,22 +153,25 @@
             width = ref.shape[1]
             row = ref[pl.ds(j, 1), :]
             lanes = lax.broadcasted_iota(jnp.int32, (1, width), 1)
-            pivot = jnp.sum(jnp.where(lanes == j, row, 0.0), axis=1, keepdims=True)
-            root = jnp.sqrt(pivot)
-            column = jnp.where(lanes < j, 0.0, row / root)
+            square_lanes = lax.broadcasted_iota(jnp.int32, (1, rank), 1)
+            pivot = jnp.sum(
+                jnp.where(square_lanes == j, row[:, :rank], 0.0), axis=1, keepdims=True
+            )
+            inverse = 1.0 / jnp.sqrt(pivot)
+            column = jnp.where(lanes < j, 0.0, row * inverse)
             count = rank - first
             block = ref[pl.ds(first, count), :]
             cols = lax.broadcasted_iota(jnp.int32, (count, rank), 1)
             upper = jnp.sum(jnp.where(cols == j, block[:, :rank], 0.0), axis=1, keepdims=True)
             below = lax.broadcasted_iota(jnp.int32, (count, 1), 0) + first > j
-            scale = jnp.where(below, upper / root, 0.0)
+            scale = jnp.where(below, upper * inverse, 0.0)
             ref[pl.ds(first, count), :] = block - scale * column
             ref[pl.ds(j, 1), :] = column
         return carry
 
     span = 16
     for first in range(0, rank, span):
-        lax.fori_loop(first, first + span, functools.partial(step, first), 0)
+        lax.fori_loop(first, first + span, functools.partial(step, first), 0, unroll=2)
 
 
 def factor_panels(*panels):

time: 97.2 us -> 96.7 us (level)
  no operation moved by 1% of the time
where the time goes in v13:
time: 96.7 us; the launch traced here: 96.3 us
  Pallas kernels  77.8 us (80%)
  local copies, waits for them, and re-layouts  8.65 us (9%)
  matrix products  6.56 us (7%)
  other arithmetic  2.41 us (2%)
    pallas_call x1, Pallas kernels, allreduce_all(): pl.pallas_call(functools.partial(allreduce_kernel, digits), out_shape=jax...  39.5 us
    pallas_call x1, Pallas kernels, core_exchange(): pl.pallas_call(functools.partial(core_kernel, cycle), out_shape=jax.Shape...  20.2 us
    pallas_call x1, Pallas kernels, factor_panels(): pl.pallas_call(panel_kernel, out_shape=[jax.ShapeDtypeStruct(p.shape, p.d...  18.1 us
    unnamed x26, local copies, waits for them, and re-layouts  5.67 us

profile of v13, /device:TPU:32, one launch (start us, length us, event | category | flops | bytes accessed | tf_op | source)
XLA Modules:
  0.0 96.3 jit_solution(4070073502356892183)
XLA Ops:
  0.6 0.0 copy-start
  0.6 0.0 copy-start.7
  0.7 0.7 copy-done.7
  1.4 0.3 copy-done
  1.7 1.6 %fusion.3 = f32[256,128]{0,1:T(8,128)S(1)} fusion(f32[2,128,512]{2,1,0:T(8,128)S(1)} %copy-done, f32[512,256]{1,0:T(8,128)} %param.10, f32[256,2]{0,1:T(2,128)S(1)} %get-tuple-element.23), kind=kOutput, calls=%fused_computation.6 | convolution fusion | flops 402751488 | bytes 1181696 | tf_op jit(solution)/shard_map/pjl,lk->pjk/dot_general | solution.py:267
  3.3 0.0 copy-start.3
  3.4 0.9 copy-done.3
  4.3 0.0 copy-start.4
  4.3 0.3 convolution_dynamic-update-slice_fusion
  4.6 0.6 copy-done.4
  5.2 1.0 %fusion.1 = f32[256,512]{0,1:T(8,128)S(1)} fusion(f32[2,128,512]{2,1,0:T(8,128)S(1)} %copy-done, f32[256,2]{0,1:T(2,128)S(1)} %get-tuple-element.22, f32[128,256]{1,0:T(8,128)S(1)} %copy-done.4), kind=kOutput, calls=%fused_computation.2 | convolution fusion | flops 403046400 | bytes 1181696 | tf_op jit(solution)/shard_map/pjl,jk->plk/dot_general | solution.py:271
  6.2 0.6 fusion.7
  6.8 0.8 pad_maximum_fusion.x_ref
  7.6 39.5 %shard_map.94 = f32[1024,128]{1,0:T(8,128)} custom-call(f32[1024,128]{1,0:T(8,128)} %pad_maximum_fusion.x_ref), custom_call_target="tpu_custom_call" | custom-call | tf_op jit(solution)/shard_map/pallas_call | solution.py:127
  47.1 0.0 copy-start.1
  47.2 1.1 %fusion.20 = (f32[512,128]{1,0:T(8,128)S(1)}, f32[512,128]{1,0:T(8,128)S(1)}) fusion(f32[1024,128]{1,0:T(8,128)} %shard_map.94), kind=kLoop, calls=%fused_computation.38 | loop fusion | bytes 1048576 | tf_op jit(solution)/shard_map/slice | solution.py:284
  48.3 0.1 copy.64
  48.4 0.0 copy-done.1
  48.4 1.0 %fusion.22 = f32[2,128,128]{2,1,0:T(8,128)S(1)} fusion(f32[2,512,128]{2,1,0:T(8,128)S(1)} %bitcast.65), kind=kOutput, calls=%fused_computation.40 | convolution fusion | flops 201326592 | bytes 655360 | tf_op jit(solution)/shard_map/nji,njk->nik/dot_general | solution.py:283
  49.4 0.7 pad_maximum_fusion.2.refs_1_
  50.1 0.1 copy.62
  50.3 0.7 pad_maximum_fusion.1.refs_0_
  51.0 18.1 %shard_map.95 = (f32[128,640]{1,0:T(8,128)}, f32[128,256]{1,0:T(8,128)}) custom-call(f32[128,640]{1,0:T(8,128)} %pad_maximum_fusion.1.refs_0_, f32[128,256]{1,0:T(8,128)} %pad_maximum_fusion.2.refs_1_), custom_call_target="tpu_custom_call" | custom-call | tf_op jit(solution)/shard_map/pallas_call | solution.py:178
  69.1 0.0 copy-start.2
  69.1 1.5 %convolution_bitcast_fusion.1 = f32[2,128,512]{2,1,0:T(8,128)S(1)} fusion(f32[2,128,512]{2,1,0:T(8,128)S(1)} %copy-done, f32[128,256]{1,0:T(8,128)} %get-tuple-element.5), kind=kOutput, calls=%fused_computation.3 | convolution fusion | flops 201326592 | bytes 1114112 | tf_op jit(solution)/shard_map/jr,pjl->prl/dot_general | solution.py:298
  70.6 0.0 copy-done.2
  70.6 0.6 fusion.5
  71.1 0.7 copy.72
  71.8 0.0 copy-start.8
  71.8 0.0 copy-start.9
  71.8 0.7 copy-done.8
  72.5 0.0 copy-done.9
  72.5 0.1 constant_dynamic-slice_fusion.1
  72.6 0.1 copy.36
  72.7 0.1 copy.37
  72.8 0.1 fusion.14
  72.9 0.1 copy.38
  72.9 0.7 broadcast_in_dim.27.weights_ref
  73.6 20.2 %shard_map.96 = f32[2,32,128]{2,1,0:T(8,128)} custom-call(f32[4,2,32,128]{3,2,1,0:T(8,128)} %bitcast.68, f32[8,2,1,128]{3,2,1,0:T(1,128)} %broadcast_in_dim.27.weights_ref), custom_call_target="tpu_custom_call" | custom-call | tf_op jit(solution)/shard_map/pallas_call | solution.py:241
  93.9 0.0 copy-start.5
  93.9 0.1 dynamic-slice_bitcast_fusion
  94.0 0.6 copy.40
  94.6 0.2 copy-done.5
  94.8 0.1 dynamic-slice_bitcast_fusion.1
  94.9 0.0 copy-start.6
  94.9 0.6 copy.39
  95.5 0.1 copy-done.6
  95.6 0.6 copy.75
  (7 shorter events, 0.1 us)
Async XLA Ops:
  0.6 1.1 %copy-start = (f32[2,128,512]{2,1,0:T(8,128)S(1)}, f32[2,128,512]{2,1,0:T(8,128)}, u32[]{:S(2)}) copy-start(f32[2,128,512]{2,1,0:T(8,128)} %param.7) | copy-start | bytes 1572868
  0.6 0.7 copy-start.7
  3.3 1.0 copy-start.3
  4.3 0.9 copy-start.4
  47.1 1.3 %copy-start.1 = (f32[1024,128]{1,0:T(8,128)S(1)}, f32[1024,128]{1,0:T(8,128)}, u32[]{:S(2)}) copy-start(f32[1024,128]{1,0:T(8,128)} %shard_map.94) | copy-start | bytes 1572868
  69.1 1.5 %copy-start.2 = (f32[128,640]{1,0:T(8,128)S(1)}, f32[128,640]{1,0:T(8,128)}, u32[]{:S(2)}) copy-start(f32[128,640]{1,0:T(8,128)} %get-tuple-element.6) | copy-start | bytes 983044
  71.8 0.7 copy-start.8
  71.8 0.7 copy-start.9
  93.9 0.9 copy-start.5
  94.9 0.8 copy-start.6

commit v14 on v13

--- a/solution.py
+++ b/solution.py
@@ -141,12 +141,19 @@
     )(x)
 
 
-def panel_kernel(*refs):
-    count = len(refs) // 2
-    inputs, outputs = refs[:count], refs[count:]
-    for source, target in zip(inputs, outputs):
-        target[...] = source[...]
-    rank = outputs[0].shape[0]
+def panel_kernel(both_ref, third_ref, second_ref):
+    outputs = (third_ref, second_ref)
+    rank = third_ref.shape[0]
+    half = both_ref.shape[0] // 2
+    own_rows = second_ref.shape[1] - rank
+    for target, ranged in ((third_ref, both_ref[half:, :]), (second_ref, both_ref[:half, :])):
+        flipped = ranged.T
+        target[:, :rank] = jnp.dot(
+            flipped, ranged, precision=lax.Precision.HIGHEST, preferred_element_type=jnp.float32
+        )
+    third_ref[:, rank:] = both_ref[half:, :].T
+    start = pl.multiple_of(lax.axis_index("af") * own_rows, 8)
+    second_ref[:, rank:] = both_ref[pl.ds(start, own_rows), :].T
 
     def step(first, j, carry):
         for ref in outputs:
@@ -174,13 +181,18 @@
         lax.fori_loop(first, first + span, functools.partial(step, first), 0, unroll=2)
 
 
-def factor_panels(*panels):
+def factor_panels(both, rows):
+    rank = both.shape[1]
+    half = both.shape[0] // 2
     return pl.pallas_call(
         panel_kernel,
-        out_shape=[jax.ShapeDtypeStruct(p.shape, p.dtype) for p in panels],
-        in_specs=[pl.BlockSpec(memory_space=pltpu.VMEM)] * len(panels),
-        out_specs=[pl.BlockSpec(memory_space=pltpu.VMEM)] * len(panels),
-    )(*panels)
+        out_shape=[
+            jax.ShapeDtypeStruct((rank, rank + half), both.dtype),
+            jax.ShapeDtypeStruct((rank, rank + rows), both.dtype),
+        ],
+        in_specs=[pl.BlockSpec(memory_space=pltpu.VMEM)],
+        out_specs=[pl.BlockSpec(memory_space=pltpu.VMEM)] * 2,
+    )(both)
 
 
 def core_kernel(cycle, pieces_ref, weights_ref, o_ref, first, staged, second, send_sem, recv_sem):
@@ -279,13 +291,7 @@
     )
     both = allreduce_all(jnp.concatenate([range_second, range_third], axis=0))
 
-    ranges = both.reshape(2, full_rows, rank_cols)
-    grams = jnp.einsum("nji,njk->nik", ranges, ranges, precision=precise)
-    own_second = lax.dynamic_slice_in_dim(ranges[0], af_index * rows, rows, 0)
-    panel_third, panel_second = factor_panels(
-        jnp.concatenate([grams[1], ranges[1].T], axis=1),
-        jnp.concatenate([grams[0], own_second.T], axis=1),
-    )
+    panel_third, panel_second = factor_panels(both, rows)
     factor_third_all = panel_third[:, rank_cols:].T
     basis_second = panel_second[:, rank_cols:].T
 

time: 96.7 us -> 92.9 us (0.961)
  matrix products: 6.56 us -> 4.59 us
  other arithmetic: 2.41 us -> 0.99 us
    concatenate x2 -> x0, other arithmetic: 1.42 us -> none  [the longest x1 0.75 us: body(): jnp.concatenate([grams[1], ranges[1].T], axis=1)]
    unnamed x26 -> x18, local copies, waits for them, and re-layouts: 5.67 us -> 4.26 us
    slice x1 -> x0, local copies, waits for them, and re-layouts: 1.12 us -> none  [body(): own_second = lax.dynamic_slice_in_dim(ranges[0], af_index * rows, rows, 0)]
    dot_general x1, matrix products: 1.64 us -> 0.59 us  [body(): jnp.einsum('pjl,lk->pjk', scalar_field, third_sketch, precision=precise)]
    dot_general x1 -> x0, matrix products: 1.02 us -> none  [body(): grams = jnp.einsum('nji,njk->nik', ranges, ranges, precision=precise)]
    dot_general x1, matrix products: 1.02 us -> 2 us  [body(): jnp.einsum('pjl,jk->plk', scalar_field, second_sketch, precision=precise)]
where the time goes in v14:
time: 92.9 us; the launch traced here: 92.5 us
  Pallas kernels  78.4 us (84%)
  local copies, waits for them, and re-layouts  7.73 us (8%)
  matrix products  4.59 us (5%)
  other arithmetic  0.99 us (1%)
    pallas_call x1, Pallas kernels, allreduce_all(): pl.pallas_call(functools.partial(allreduce_kernel, digits), out_shape=jax...  39.5 us
    pallas_call x1, Pallas kernels, core_exchange(): pl.pallas_call(functools.partial(core_kernel, cycle), out_shape=jax.Shape...  20.2 us
    pallas_call x1, Pallas kernels, factor_panels(): pl.pallas_call(panel_kernel, out_shape=[jax.ShapeDtypeStruct((rank, rank...  18.7 us
    unnamed x18, local copies, waits for them, and re-layouts  4.26 us
    dot_general x1, matrix products, body(): jnp.einsum('pjl,jk->plk', scalar_field, second_sketch, precision=precise)  2 us

profile of v14, /device:TPU:32, one launch (start us, length us, event | category | flops | bytes accessed | tf_op | source)
XLA Modules:
  0.0 92.5 jit_solution(979581113830654599)
XLA Ops:
  0.6 0.0 copy-start
  0.6 0.8 fusion.20
  1.4 0.3 copy-done
  1.7 0.0 copy-start.3
  1.7 2.0 %fusion.1 = f32[256,512]{0,1:T(8,128)S(1)} fusion(f32[2,128,512]{2,1,0:T(8,128)S(1)} %copy-done, f32[256,2]{0,1:T(2,128)S(1)} %get-tuple-element.18, f32[128,256]{1,0:T(8,128)} %param.9), kind=kOutput, calls=%fused_computation.2 | convolution fusion | flops 403046400 | bytes 1181696 | tf_op jit(solution)/shard_map/pjl,jk->plk/dot_general | solution.py:283
  3.7 0.0 copy-done.3
  3.7 0.0 copy-start.2
  3.7 0.6 fusion.7
  4.3 0.4 copy-done.2
  4.8 0.6 fusion.3
  5.4 0.3 convolution_dynamic-update-slice_fusion
  5.7 0.8 pad_maximum_fusion.x_ref
  6.5 39.5 %shard_map.94.both_ref = f32[1024,128]{1,0:T(8,128)} custom-call(f32[1024,128]{1,0:T(8,128)} %pad_maximum_fusion.x_ref), custom_call_target="tpu_custom_call" | custom-call | tf_op jit(solution)/shard_map/pallas_call | solution.py:127
  46.0 18.7 %shard_map.95 = (f32[128,640]{1,0:T(8,128)}, f32[128,256]{1,0:T(8,128)}) custom-call(f32[1024,128]{1,0:T(8,128)} %shard_map.94.both_ref), custom_call_target="tpu_custom_call" | custom-call | tf_op jit(solution)/shard_map/pallas_call | solution.py:187
  64.7 0.0 copy-start.1
  64.7 0.9 slice.22
  65.6 0.1 dynamic-slice_bitcast_fusion.1
  65.7 0.6 copy.24
  66.4 0.0 copy-done.1
  66.4 0.0 copy-start.4
  66.4 0.1 dynamic-slice_bitcast_fusion
  66.5 0.6 copy.25
  67.1 0.2 copy-done.4
  67.3 0.6 convolution_bitcast_fusion.1
  67.9 0.6 fusion.5
  68.5 0.0 copy-start.6
  68.5 0.7 copy.52
  69.1 0.0 copy-start.5
  69.1 0.0 copy-done.6
  69.1 0.7 copy-done.5
  69.8 0.1 constant_dynamic-slice_fusion.1
  69.9 0.1 copy.22
  70.0 0.1 copy.21
  70.1 0.1 fusion.14
  70.2 0.1 copy.23
  70.3 0.7 broadcast_in_dim.27.weights_ref
  70.9 20.2 %shard_map.96 = f32[2,32,128]{2,1,0:T(8,128)} custom-call(f32[4,2,32,128]{3,2,1,0:T(8,128)} %bitcast.57, f32[8,2,1,128]{3,2,1,0:T(1,128)} %broadcast_in_dim.27.weights_ref), custom_call_target="tpu_custom_call" | custom-call | tf_op jit(solution)/shard_map/pallas_call | solution.py:253
  91.1 1.4 %copy.55 = f32[2,32,128]{2,1,0:T(8,128)} copy(f32[2,32,128]{2,1,0:T(8,128)} %shard_map.96) | data formatting | bytes 65536
  (3 shorter events, 0.0 us)
Async XLA Ops:
  0.6 1.1 %copy-start = (f32[2,128,512]{2,1,0:T(8,128)S(1)}, f32[2,128,512]{2,1,0:T(8,128)}, u32[]{:S(2)}) copy-start(f32[2,128,512]{2,1,0:T(8,128)} %param.7) | copy-start | bytes 1572868
  1.7 2.0 %copy-start.3 = (f32[2,256,128]{2,1,0:T(8,128)S(1)}, f32[2,256,128]{2,1,0:T(8,128)}, u32[]{:S(2)}) copy-start(f32[2,256,128]{2,1,0:T(8,128)} %param.11) | copy-start | bytes 786436
  3.7 1.0 %copy-start.2 = (f32[512,256]{1,0:T(8,128)S(1)}, f32[512,256]{1,0:T(8,128)}, u32[]{:S(2)}) copy-start(f32[512,256]{1,0:T(8,128)} %param.10) | copy-start | bytes 1572868
  64.7 1.6 %copy-start.1 = (f32[128,640]{1,0:T(8,128)S(1)}, f32[128,640]{1,0:T(8,128)}, u32[]{:S(2)}) copy-start(f32[128,640]{1,0:T(8,128)} %get-tuple-element.6) | copy-start | bytes 983044
  66.4 0.9 copy-start.4
  68.5 0.7 copy-start.6
  69.1 0.7 copy-start.5

commit v15 on v14

--- a/solution.py
+++ b/solution.py
@@ -195,10 +195,26 @@
     )(both)
 
 
-def core_kernel(cycle, pieces_ref, weights_ref, o_ref, first, staged, second, send_sem, recv_sem):
+def core_kernel(
+    cycle, field_ref, left_ref, right_ref, weights_ref, o_ref,
+    pieces_ref, first, staged, second, send_sem, recv_sem,
+):
     g = lax.axis_index("gx")
     a = lax.axis_index("af")
-    quarters, blocks = pieces_ref.shape[0], weights_ref.shape[0]
+    quarters, planes, slab = pieces_ref.shape[:3]
+    blocks = weights_ref.shape[0]
+    rank = right_ref.shape[0]
+    for p in range(planes):
+        left = jnp.dot(
+            left_ref[:, rank:], field_ref[p],
+            precision=lax.Precision.HIGHEST, preferred_element_type=jnp.float32,
+        )
+        projected = lax.dot_general(
+            left, right_ref[:, rank:], (((1,), (1,)), ((), ())),
+            precision=lax.Precision.HIGHEST, preferred_element_type=jnp.float32,
+        )
+        for q in range(quarters):
+            pieces_ref[q, p] = projected[q * slab:(q + 1) * slab, :]
     k = g // cycle
     c = g % cycle
     peers = [(a + d) % quarters for d in range(1, quarters)]
@@ -247,23 +263,26 @@
     o_ref[...] = result
 
 
-def core_exchange(pieces, weights, cycle):
-    quarters, blocks = pieces.shape[0], weights.shape[0]
-    piece = pieces.shape[1:]
+def core_exchange(field, left, right, weights, cycle, quarters):
+    planes, rank = field.shape[0], right.shape[0]
+    blocks = weights.shape[0]
+    piece = (planes, rank // quarters, rank)
+    dtype = field.dtype
     return pl.pallas_call(
         functools.partial(core_kernel, cycle),
-        out_shape=jax.ShapeDtypeStruct(piece, pieces.dtype),
-        in_specs=[pl.BlockSpec(memory_space=pltpu.VMEM)] * 2,
+        out_shape=jax.ShapeDtypeStruct(piece, dtype),
+        in_specs=[pl.BlockSpec(memory_space=pltpu.VMEM)] * 4,
         out_specs=pl.BlockSpec(memory_space=pltpu.VMEM),
         scratch_shapes=[
-            pltpu.VMEM((quarters - 1,) + piece, pieces.dtype),
-            pltpu.VMEM((blocks,) + piece, pieces.dtype),
-            pltpu.VMEM((blocks - 1,) + piece, pieces.dtype),
+            pltpu.VMEM((quarters,) + piece, dtype),
+            pltpu.VMEM((quarters - 1,) + piece, dtype),
+            pltpu.VMEM((blocks,) + piece, dtype),
+            pltpu.VMEM((blocks - 1,) + piece, dtype),
             pltpu.SemaphoreType.DMA((quarters + blocks - 2,)),
             pltpu.SemaphoreType.DMA((quarters + blocks - 2,)),
         ],
         compiler_params=pltpu.CompilerParams(collective_id=1, has_side_effects=True),
-    )(pieces, weights)
+    )(field, left, right, weights)
 
 
 def body(
@@ -301,8 +320,6 @@
     factor_third = lax.dynamic_slice_in_dim(
         factor_third_all, (gx_index * af_size + af_index) * out_second, out_second, 0
     )
-    left_side = jnp.einsum("jr,pjl->prl", basis_second, scalar_field, precision=precise)
-    projected = jnp.einsum("prl,ls->prs", left_side, factor_third_all, precision=precise)
     cycle = BLOCK // planes
     groups = gx_size // cycle
     assert planes * gx_size == BLOCKS * BLOCK and groups == BLOCKS
@@ -314,10 +331,10 @@
         jnp.where(own_targets[None, :, :] == block_ids[:, None, None], sign_values[None, :, :], 0.0),
         axis=2,
     )
-    slab = rank_cols // af_size
-    pieces = projected.reshape(planes, af_size, slab, rank_cols).transpose(1, 0, 2, 3)
     lane_weights = jnp.broadcast_to(weights[:, :, None, None], (groups, planes, 1, rank_cols))
-    core_sketch = core_exchange(pieces, lane_weights, cycle)
+    core_sketch = core_exchange(
+        scalar_field, panel_second, panel_third, lane_weights, cycle, af_size
+    )
     return (factor_second, factor_third, core_sketch)
 
 

time: 92.9 us -> 91.7 us (0.987)
  local copies, waits for them, and re-layouts: 7.73 us -> 5.98 us
  Pallas kernels: 78.4 us -> 80 us
  matrix products: 4.59 us -> 3.61 us
    pallas_call x1, Pallas kernels: 20.2 us -> 21.8 us  [core_exchange(): pl.pallas_call(functools.partial(core_kernel, cycle), out_shape=jax.Shape...]
    dot_general x2 -> x0, matrix products: 1.15 us -> none  [the longest x1 0.58 us: body(): jnp.einsum('jr,pjl->prl', basis_second, scalar_field, precision=precise)]
    unnamed x18 -> x16, local copies, waits for them, and re-layouts: 4.26 us -> 3.16 us
where the time goes in v15:
time: 91.7 us; the launch traced here: 91.3 us
  Pallas kernels  80 us (87%)
  local copies, waits for them, and re-layouts  5.98 us (7%)
  matrix products  3.61 us (4%)
  other arithmetic  0.99 us (1%)
    pallas_call x1, Pallas kernels, allreduce_all(): pl.pallas_call(functools.partial(allreduce_kernel, digits), out_shape=jax...  39.5 us
    pallas_call x1, Pallas kernels, core_exchange(): pl.pallas_call(functools.partial(core_kernel, cycle), out_shape=jax.Shape...  21.8 us
    pallas_call x1, Pallas kernels, factor_panels(): pl.pallas_call(panel_kernel, out_shape=[jax.ShapeDtypeStruct((rank, rank...  18.7 us
    unnamed x16, local copies, waits for them, and re-layouts  3.16 us
    dot_general x1, matrix products, body(): jnp.einsum('pjl,jk->plk', scalar_field, second_sketch, precision=precise)  2.16 us

profile of v15, /device:TPU:32, one launch (start us, length us, event | category | flops | bytes accessed | tf_op | source)
XLA Modules:
  0.0 91.3 jit_solution(11606085332930831506)
XLA Ops:
  0.6 0.0 copy-start
  0.6 0.8 fusion.15
  1.4 0.0 copy-start.3
  1.4 2.2 %fusion.1 = f32[256,512]{0,1:T(8,128)S(1)} fusion(f32[2,128,512]{2,1,0:T(8,128)} %field_ref.1, f32[256,2]{0,1:T(2,128)S(1)} %get-tuple-element.18, f32[128,256]{1,0:T(8,128)} %param.9), kind=kOutput, calls=%fused_computation.2 | convolution fusion | flops 403046400 | bytes 1181696 | tf_op jit(solution)/shard_map/pjl,jk->plk/dot_general | solution.py:302
  3.6 0.0 copy-done.3
  3.6 0.0 copy-start.1
  3.6 0.6 fusion.5
  4.2 0.0 copy-done
  4.2 0.4 copy-done.1
  4.6 0.6 fusion.3
  5.3 0.3 convolution_dynamic-update-slice_fusion
  5.6 0.8 pad_maximum_fusion.x_ref
  6.4 39.5 %shard_map.94.both_ref = f32[1024,128]{1,0:T(8,128)} custom-call(f32[1024,128]{1,0:T(8,128)} %pad_maximum_fusion.x_ref), custom_call_target="tpu_custom_call" | custom-call | tf_op jit(solution)/shard_map/pallas_call | solution.py:127
  45.9 18.7 %shard_map.95 = (f32[128,640]{1,0:T(8,128)}, f32[128,256]{1,0:T(8,128)}) custom-call(f32[1024,128]{1,0:T(8,128)} %shard_map.94.both_ref), custom_call_target="tpu_custom_call" | custom-call | tf_op jit(solution)/shard_map/pallas_call | solution.py:187
  64.6 0.0 copy-start.2
  64.6 0.9 slice.22
  65.5 0.1 dynamic-slice_bitcast_fusion.1
  65.6 0.6 copy.22
  66.2 0.0 copy-done.2
  66.2 0.1 dynamic-slice_bitcast_fusion
  66.3 0.0 copy-start.4
  66.3 0.0 copy-start.5
  66.4 0.6 copy.23
  67.0 0.0 copy-done.4
  67.0 0.0 copy-done.5
  67.0 0.1 constant_dynamic-slice_fusion.1
  67.1 0.1 copy.20
  67.2 0.1 copy.19
  67.3 0.1 fusion.11
  67.4 0.1 copy.21
  67.5 0.7 broadcast_in_dim.27.weights_ref
  68.2 21.8 %shard_map.96 = f32[2,32,128]{2,1,0:T(8,128)} custom-call(f32[2,128,512]{2,1,0:T(8,128)} %field_ref.1, f32[128,256]{1,0:T(8,128)} %get-tuple-element.5.left_ref, f32[128,640]{1,0:T(8,128)} %get-tuple-element.6.right_ref, f32[8,2,1,128]{3,2,1,0:T(1,128)} %broadcast_in_dim.27.weights_ref), custom_call_target="tpu_custom_call" | custom-call | tf_op jit(solution)/shard_map/pallas_call | solution.py:271
  89.9 1.4 %copy.51 = f32[2,32,128]{2,1,0:T(8,128)} copy(f32[2,32,128]{2,1,0:T(8,128)} %shard_map.96) | data formatting | bytes 65536
  (3 shorter events, 0.0 us)
Async XLA Ops:
  0.6 3.6 %copy-start = (f32[512,256]{1,0:T(8,128)S(1)}, f32[512,256]{1,0:T(8,128)}, u32[]{:S(2)}) copy-start(f32[512,256]{1,0:T(8,128)} %param.10) | copy-start | bytes 1572868
  1.4 2.2 %copy-start.3 = (f32[2,256,128]{2,1,0:T(8,128)S(1)}, f32[2,256,128]{2,1,0:T(8,128)}, u32[]{:S(2)}) copy-start(f32[2,256,128]{2,1,0:T(8,128)} %param.11) | copy-start | bytes 786436
  3.6 1.0 %copy-start.1 = (f32[2,128,512]{2,1,0:T(8,128)S(1)}, f32[2,128,512]{2,1,0:T(8,128)}, u32[]{:S(2)}) copy-start(f32[2,128,512]{2,1,0:T(8,128)} %field_ref.1) | copy-start | bytes 1572868
  64.6 1.6 %copy-start.2 = (f32[128,640]{1,0:T(8,128)S(1)}, f32[128,640]{1,0:T(8,128)}, u32[]{:S(2)}) copy-start(f32[128,640]{1,0:T(8,128)} %get-tuple-element.6.right_ref) | copy-start | bytes 983044
  66.3 0.7 copy-start.4
  66.3 0.7 copy-start.5

commit v16 on v15

--- a/solution.py
+++ b/solution.py
@@ -196,13 +196,12 @@
 
 
 def core_kernel(
-    cycle, field_ref, left_ref, right_ref, weights_ref, o_ref,
+    cycle, blocks, field_ref, left_ref, right_ref, targets_ref, signs_ref, o_ref,
     pieces_ref, first, staged, second, send_sem, recv_sem,
 ):
     g = lax.axis_index("gx")
     a = lax.axis_index("af")
     quarters, planes, slab = pieces_ref.shape[:3]
-    blocks = weights_ref.shape[0]
     rank = right_ref.shape[0]
     for p in range(planes):
         left = jnp.dot(
@@ -249,8 +248,14 @@
     total = pieces_ref[a]
     for n in range(len(peers)):
         total = total + first[n]
-    for j in range(blocks):
-        staged[j] = weights_ref[j] * total
+    for p in range(planes):
+        plane = g * planes + p
+        for j in range(blocks):
+            weight = 0
+            for t in range(targets_ref.shape[1]):
+                sign = 2 * signs_ref[plane, t] - 1
+                weight = weight + jnp.where(targets_ref[plane, t] == j, sign, 0)
+            staged[j, p] = weight.astype(jnp.float32) * total[p]
     base = len(peers)
     copies = [
         start(base + n, staged.at[j], second.at[n], owner(j)) for n, j in enumerate(owners)
@@ -263,15 +268,15 @@
     o_ref[...] = result
 
 
-def core_exchange(field, left, right, weights, cycle, quarters):
+def core_exchange(field, left, right, targets, signs, cycle, quarters, blocks):
     planes, rank = field.shape[0], right.shape[0]
-    blocks = weights.shape[0]
     piece = (planes, rank // quarters, rank)
     dtype = field.dtype
     return pl.pallas_call(
-        functools.partial(core_kernel, cycle),
+        functools.partial(core_kernel, cycle, blocks),
         out_shape=jax.ShapeDtypeStruct(piece, dtype),
-        in_specs=[pl.BlockSpec(memory_space=pltpu.VMEM)] * 4,
+        in_specs=[pl.BlockSpec(memory_space=pltpu.VMEM)] * 3
+        + [pl.BlockSpec(memory_space=pltpu.SMEM)] * 2,
         out_specs=pl.BlockSpec(memory_space=pltpu.VMEM),
         scratch_shapes=[
             pltpu.VMEM((quarters,) + piece, dtype),
@@ -282,7 +287,7 @@
             pltpu.SemaphoreType.DMA((quarters + blocks - 2,)),
         ],
         compiler_params=pltpu.CompilerParams(collective_id=1, has_side_effects=True),
-    )(field, left, right, weights)
+    )(field, left, right, targets, signs)
 
 
 def body(
@@ -323,17 +328,8 @@
     cycle = BLOCK // planes
     groups = gx_size // cycle
     assert planes * gx_size == BLOCKS * BLOCK and groups == BLOCKS
-    own_targets = lax.dynamic_slice_in_dim(plane_targets, gx_index * planes, planes, 0)
-    own_signs = lax.dynamic_slice_in_dim(plane_signs, gx_index * planes, planes, 0)
-    sign_values = (2 * own_signs - 1).astype(jnp.float32)
-    block_ids = jnp.arange(groups, dtype=jnp.int32)
-    weights = jnp.sum(
-        jnp.where(own_targets[None, :, :] == block_ids[:, None, None], sign_values[None, :, :], 0.0),
-        axis=2,
-    )
-    lane_weights = jnp.broadcast_to(weights[:, :, None, None], (groups, planes, 1, rank_cols))
     core_sketch = core_exchange(
-        scalar_field, panel_second, panel_third, lane_weights, cycle, af_size
+        scalar_field, panel_second, panel_third, plane_targets, plane_signs, cycle, af_size, groups
     )
     return (factor_second, factor_third, core_sketch)
 

time: 91.7 us -> 93.7 us (1.022)
  Pallas kernels: 80 us -> 81.8 us
    unnamed x16 -> x26, local copies, waits for them, and re-layouts: 3.16 us -> 6.07 us
    pallas_call x1, Pallas kernels: 21.8 us -> 23.6 us  [core_exchange(): pl.pallas_call(functools.partial(core_kernel, cycle, blocks), out_shape=j...]
    dot_general x1, matrix products: 2.16 us -> 1.02 us  [body(): jnp.einsum('pjl,jk->plk', scalar_field, second_sketch, precision=precise)]
    dot_general x1, matrix products: 0.59 us -> 1.69 us  [body(): jnp.einsum('pjl,lk->pjk', scalar_field, third_sketch, precision=precise)]
where the time goes in v16:
time: 93.7 us; the launch traced here: 93.2 us
  Pallas kernels  81.8 us (87%)
  local copies, waits for them, and re-layouts  6.29 us (7%)
  matrix products  3.57 us (4%)
    pallas_call x1, Pallas kernels, allreduce_all(): pl.pallas_call(functools.partial(allreduce_kernel, digits), out_shape=jax...  39.5 us
    pallas_call x1, Pallas kernels, core_exchange(): pl.pallas_call(functools.partial(core_kernel, cycle, blocks), out_shape=j...  23.6 us
    pallas_call x1, Pallas kernels, factor_panels(): pl.pallas_call(panel_kernel, out_shape=[jax.ShapeDtypeStruct((rank, rank...  18.7 us
    unnamed x26, local copies, waits for them, and re-layouts  6.07 us

profile of v16, /device:TPU:32, one launch (start us, length us, event | category | flops | bytes accessed | tf_op | source)
XLA Modules:
  0.0 93.2 jit_solution(16611898479493584667)
XLA Ops:
  0.6 0.0 copy-start
  0.6 0.0 copy-start.7
  0.7 0.7 copy-done.7
  1.4 0.3 copy-done
  1.7 0.0 copy-start.4
  1.7 0.0 copy-start.5
  1.7 1.7 %fusion.3 = f32[256,128]{0,1:T(8,128)S(1)} fusion(f32[2,128,512]{2,1,0:T(8,128)} %field_ref.1, f32[512,256]{1,0:T(8,128)S(1)} %copy-done, f32[256,2]{0,1:T(2,128)S(1)} %get-tuple-element.16), kind=kOutput, calls=%fused_computation.5 | convolution fusion | flops 402751488 | bytes 1181696 | tf_op jit(solution)/shard_map/pjl,lk->pjk/dot_general | solution.py:303
  3.4 0.0 copy-start.1
  3.4 0.0 copy-done.4
  3.4 0.3 convolution_dynamic-update-slice_fusion
  3.7 0.0 copy-done.5
  3.7 0.7 copy-done.1
  4.4 1.0 %fusion.1 = f32[256,512]{0,1:T(8,128)S(1)} fusion(f32[2,128,512]{2,1,0:T(8,128)S(1)} %copy-done.1, f32[256,2]{0,1:T(2,128)S(1)} %get-tuple-element.15, f32[128,256]{1,0:T(8,128)S(1)} %copy-done.5), kind=kOutput, calls=%fused_computation.2 | convolution fusion | flops 403046400 | bytes 1181696 | tf_op jit(solution)/shard_map/pjl,jk->plk/dot_general | solution.py:307
  5.5 0.6 fusion.5
  6.1 0.8 pad_maximum_fusion.x_ref
  6.9 39.5 %shard_map.94.both_ref = f32[1024,128]{1,0:T(8,128)} custom-call(f32[1024,128]{1,0:T(8,128)} %pad_maximum_fusion.x_ref), custom_call_target="tpu_custom_call" | custom-call | tf_op jit(solution)/shard_map/pallas_call | solution.py:127
  46.4 18.7 %shard_map.95 = (f32[128,640]{1,0:T(8,128)}, f32[128,256]{1,0:T(8,128)}) custom-call(f32[1024,128]{1,0:T(8,128)} %shard_map.94.both_ref), custom_call_target="tpu_custom_call" | custom-call | tf_op jit(solution)/shard_map/pallas_call | solution.py:187
  65.1 0.0 copy-start.8
  65.1 0.7 copy-done.8
  65.8 0.0 copy-start.9
  65.8 0.7 copy.14.targets_ref
  66.5 0.0 copy-done.9
  66.5 0.7 copy.15.signs_ref
  67.2 0.0 copy-start.2
  67.2 23.6 %shard_map.96 = f32[2,32,128]{2,1,0:T(8,128)} custom-call(f32[2,128,512]{2,1,0:T(8,128)} %field_ref.1, f32[128,256]{1,0:T(8,128)} %get-tuple-element.5.left_ref, f32[128,640]{1,0:T(8,128)} %get-tuple-element.6.right_ref, s32[128,2]{1,0:T(8,128)} %copy.14.targets_ref, s32[128,2]{1,0:T(8,128)} %copy.15.signs_ref), custom_call_target="tpu_custom_call" | custom-call | tf_op jit(solution)/shard_map/pallas_call | solution.py:275
  90.8 0.0 copy-done.2
  90.9 0.0 copy-start.3
  90.9 0.1 dynamic-slice_bitcast_fusion
  91.0 0.6 copy.17
  91.6 0.2 copy-done.3
  91.8 0.1 dynamic-slice_bitcast_fusion.1
  91.8 0.0 copy-start.6
  91.9 0.6 copy.16
  92.5 0.1 copy-done.6
  92.6 0.6 copy.44
  (5 shorter events, 0.1 us)
Async XLA Ops:
  0.6 1.1 %copy-start = (f32[512,256]{1,0:T(8,128)S(1)}, f32[512,256]{1,0:T(8,128)}, u32[]{:S(2)}) copy-start(f32[512,256]{1,0:T(8,128)} %param.10) | copy-start | bytes 1572868
  0.6 0.7 copy-start.7
  1.7 1.7 %copy-start.4 = (f32[2,256,128]{2,1,0:T(8,128)S(1)}, f32[2,256,128]{2,1,0:T(8,128)}, u32[]{:S(2)}) copy-start(f32[2,256,128]{2,1,0:T(8,128)} %param.11) | copy-start | bytes 786436
  1.7 2.0 %copy-start.5 = (f32[128,256]{1,0:T(8,128)S(1)}, f32[128,256]{1,0:T(8,128)}, u32[]{:S(2)}) copy-start(f32[128,256]{1,0:T(8,128)} %param.9) | copy-start | bytes 393220
  3.4 1.0 %copy-start.1 = (f32[2,128,512]{2,1,0:T(8,128)S(1)}, f32[2,128,512]{2,1,0:T(8,128)}, u32[]{:S(2)}) copy-start(f32[2,128,512]{2,1,0:T(8,128)} %field_ref.1) | copy-start | bytes 1572868
  65.1 0.7 copy-start.8
  65.8 0.7 copy-start.9
  67.2 23.6 %copy-start.2 = (f32[128,640]{1,0:T(8,128)S(1)}, f32[128,640]{1,0:T(8,128)}, u32[]{:S(2)}) copy-start(f32[128,640]{1,0:T(8,128)} %get-tuple-element.6.right_ref) | copy-start | bytes 983044
  90.9 0.9 copy-start.3
  91.8 0.8 copy-start.6

commit v17 on v15

--- a/solution.py
+++ b/solution.py
@@ -29,7 +29,7 @@
     return steps
 
 
-def allreduce_kernel(digits, x_ref, o_ref, acc, recv, exchange, gathered, send_sem, recv_sem):
+def allreduce_kernel(digits, block_ref, third_ref, o_ref, acc, recv, exchange, gathered, send_sem, recv_sem):
     index = {"gx": lax.axis_index("gx"), "af": lax.axis_index("af")}
 
     def bits_of(digit):
@@ -74,7 +74,11 @@
         copy.start()
         return copy
 
-    acc[...] = x_ref[...]
+    half = third_ref.shape[0]
+    block_rows = block_ref.shape[0]
+    acc[pl.ds(0, half), :] = jnp.zeros((half,) + acc.shape[1:], acc.dtype)
+    acc[pl.ds(pl.multiple_of(index["af"] * block_rows, 8), block_rows), :] = block_ref[...]
+    acc[pl.ds(half, half), :] = third_ref[...]
     offset, length, slot = 0, acc.shape[0], 0
     parents = []
     for digit in digits[:-1]:
@@ -116,7 +120,8 @@
     o_ref[...] = gathered[...]
 
 
-def allreduce_all(x):
+def allreduce_all(block, third):
+    x = jax.ShapeDtypeStruct((2 * third.shape[0],) + third.shape[1:], third.dtype)
     steps = partner_list(lax.axis_size("gx"), lax.axis_size("af"))
     digits = [steps[t:t + 3] for t in range(0, len(steps), 3)]
     last_rows = x.shape[0]
@@ -127,7 +132,7 @@
     return pl.pallas_call(
         functools.partial(allreduce_kernel, digits),
         out_shape=jax.ShapeDtypeStruct(x.shape, x.dtype),
-        in_specs=[pl.BlockSpec(memory_space=pltpu.VMEM)],
+        in_specs=[pl.BlockSpec(memory_space=pltpu.VMEM)] * 2,
         out_specs=pl.BlockSpec(memory_space=pltpu.VMEM),
         scratch_shapes=[
             pltpu.VMEM(x.shape, x.dtype),
@@ -138,7 +143,7 @@
             pltpu.SemaphoreType.DMA((copies,)),
         ],
         compiler_params=pltpu.CompilerParams(collective_id=0, has_side_effects=True),
-    )(x)
+    )(block, third)
 
 
 def panel_kernel(both_ref, third_ref, second_ref):
@@ -305,10 +310,7 @@
     range_second_block = jnp.dot(partial_second, mixing[0], precision=precise)
     range_third = jnp.dot(partial_third, mixing[1], precision=precise)
     full_rows = rows * af_size
-    range_second = lax.dynamic_update_slice_in_dim(
-        jnp.zeros((full_rows, rank_cols), jnp.float32), range_second_block, af_index * rows, 0
-    )
-    both = allreduce_all(jnp.concatenate([range_second, range_third], axis=0))
+    both = allreduce_all(range_second_block, range_third)
 
     panel_third, panel_second = factor_panels(both, rows)
     factor_third_all = panel_third[:, rank_cols:].T

time: 91.7 us -> 91.9 us (level)
  matrix products: 3.61 us -> 4.92 us
    dot_general x1, matrix products: 2.16 us -> 1.02 us  [body(): jnp.einsum('pjl,jk->plk', scalar_field, second_sketch, precision=precise)]
    dot_general x1, matrix products: 0.59 us -> 1.71 us  [body(): jnp.einsum('pjl,lk->pjk', scalar_field, third_sketch, precision=precise)]
    unnamed x16 -> x18, local copies, waits for them, and re-layouts: 3.16 us -> 3.02 us
where the time goes in v17:
time: 91.9 us; the launch traced here: 91.6 us
  Pallas kernels  80 us (87%)
  local copies, waits for them, and re-layouts  5.82 us (6%)
  matrix products  4.92 us (5%)
    pallas_call x1, Pallas kernels, allreduce_all(): pl.pallas_call(functools.partial(allreduce_kernel, digits), out_shape=jax...  39.4 us
    pallas_call x1, Pallas kernels, core_exchange(): pl.pallas_call(functools.partial(core_kernel, cycle), out_shape=jax.Shape...  21.8 us
    pallas_call x1, Pallas kernels, factor_panels(): pl.pallas_call(panel_kernel, out_shape=[jax.ShapeDtypeStruct((rank, rank...  18.7 us
    unnamed x18, local copies, waits for them, and re-layouts  3.02 us

profile of v17, /device:TPU:32, one launch (start us, length us, event | category | flops | bytes accessed | tf_op | source)
XLA Modules:
  0.0 91.6 jit_solution(5445617956419809622)
XLA Ops:
  0.6 0.0 copy-start
  0.6 0.8 fusion.13
  1.4 0.3 copy-done
  1.7 0.0 copy-start.3
  1.7 0.0 copy-start.1
  1.7 1.7 %fusion.3 = f32[256,128]{0,1:T(8,128)S(1)} fusion(f32[2,128,512]{2,1,0:T(8,128)} %field_ref.1, f32[512,256]{1,0:T(8,128)S(1)} %copy-done, f32[256,2]{0,1:T(2,128)S(1)} %get-tuple-element.19), kind=kOutput, calls=%fused_computation.5 | convolution fusion | flops 402751488 | bytes 1181696 | tf_op jit(solution)/shard_map/pjl,lk->pjk/dot_general | solution.py:303
  3.4 0.0 copy-done.3
  3.4 0.0 copy-start.4
  3.5 0.9 fusion.8.block_ref
  4.4 0.0 copy-done.1
  4.4 0.0 copy-done.4
  4.4 1.0 %fusion.1 = f32[256,512]{0,1:T(8,128)S(1)} fusion(f32[2,128,512]{2,1,0:T(8,128)S(1)} %copy-done.1, f32[256,2]{0,1:T(2,128)S(1)} %get-tuple-element.18, f32[128,256]{1,0:T(8,128)S(1)} %copy-done.4), kind=kOutput, calls=%fused_computation.2 | convolution fusion | flops 403046400 | bytes 1181696 | tf_op jit(solution)/shard_map/pjl,jk->plk/dot_general | solution.py:307
  5.4 1.3 %fusion.5.third_ref = f32[512,128]{1,0:T(8,128)} fusion(f32[256,512]{0,1:T(8,128)S(1)} %fusion.1, f32[2,256,128]{2,1,0:T(8,128)S(1)} %copy-done.3), kind=kOutput, calls=%fused_computation.7 | convolution fusion | flops 201326592 | bytes 917504 | tf_op jit(solution)/shard_map/dot_general | solution.py:311
  6.7 39.4 %shard_map.94.both_ref = f32[1024,128]{1,0:T(8,128)} custom-call(f32[128,128]{1,0:T(8,128)} %fusion.8.block_ref, f32[512,128]{1,0:T(8,128)} %fusion.5.third_ref), custom_call_target="tpu_custom_call" | custom-call | tf_op jit(solution)/shard_map/pallas_call | solution.py:132
  46.1 18.7 %shard_map.95 = (f32[128,640]{1,0:T(8,128)}, f32[128,256]{1,0:T(8,128)}) custom-call(f32[1024,128]{1,0:T(8,128)} %shard_map.94.both_ref), custom_call_target="tpu_custom_call" | custom-call | tf_op jit(solution)/shard_map/pallas_call | solution.py:192
  64.8 0.0 copy-start.2
  64.9 0.9 slice.22
  65.7 0.1 dynamic-slice_bitcast_fusion.1
  65.8 0.6 copy.22
  66.5 0.0 copy-done.2
  66.5 0.1 dynamic-slice_bitcast_fusion
  66.6 0.0 copy-start.5
  66.6 0.0 copy-start.6
  66.6 0.6 copy.23
  67.3 0.0 copy-done.5
  67.3 0.0 copy-done.6
  67.3 0.1 add_convert_fusion
  67.4 0.1 copy.20
  67.5 0.1 copy.19
  67.6 0.1 fusion.12
  67.6 0.1 copy.21
  67.7 0.7 broadcast_in_dim.23.weights_ref
  68.4 21.8 %shard_map.96 = f32[2,32,128]{2,1,0:T(8,128)} custom-call(f32[2,128,512]{2,1,0:T(8,128)} %field_ref.1, f32[128,256]{1,0:T(8,128)} %get-tuple-element.5.left_ref, f32[128,640]{1,0:T(8,128)} %get-tuple-element.6.right_ref, f32[8,2,1,128]{3,2,1,0:T(1,128)} %broadcast_in_dim.23.weights_ref), custom_call_target="tpu_custom_call" | custom-call | tf_op jit(solution)/shard_map/pallas_call | solution.py:276
  90.2 1.4 %copy.50 = f32[2,32,128]{2,1,0:T(8,128)} copy(f32[2,32,128]{2,1,0:T(8,128)} %shard_map.96) | data formatting | bytes 65536
  (2 shorter events, 0.0 us)
Async XLA Ops:
  0.6 1.1 %copy-start = (f32[512,256]{1,0:T(8,128)S(1)}, f32[512,256]{1,0:T(8,128)}, u32[]{:S(2)}) copy-start(f32[512,256]{1,0:T(8,128)} %param.10) | copy-start | bytes 1572868
  1.7 1.7 %copy-start.3 = (f32[2,256,128]{2,1,0:T(8,128)S(1)}, f32[2,256,128]{2,1,0:T(8,128)}, u32[]{:S(2)}) copy-start(f32[2,256,128]{2,1,0:T(8,128)} %param.11) | copy-start | bytes 786436
  1.7 2.7 %copy-start.1 = (f32[2,128,512]{2,1,0:T(8,128)S(1)}, f32[2,128,512]{2,1,0:T(8,128)}, u32[]{:S(2)}) copy-start(f32[2,128,512]{2,1,0:T(8,128)} %field_ref.1) | copy-start | bytes 1572868
  3.4 0.9 %copy-start.4 = (f32[128,256]{1,0:T(8,128)S(1)}, f32[128,256]{1,0:T(8,128)}, u32[]{:S(2)}) copy-start(f32[128,256]{1,0:T(8,128)} %param.9) | copy-start | bytes 393220
  64.8 1.6 %copy-start.2 = (f32[128,640]{1,0:T(8,128)S(1)}, f32[128,640]{1,0:T(8,128)}, u32[]{:S(2)}) copy-start(f32[128,640]{1,0:T(8,128)} %get-tuple-element.6.right_ref) | copy-start | bytes 983044
  66.6 0.7 copy-start.5
  66.6 0.7 copy-start.6

commit v18 on v15

--- a/solution.py
+++ b/solution.py
@@ -17,7 +17,7 @@
 
 
 def partner_list(gx_size, af_size):
-    preferred = [("gx", 1), ("gx", 2), ("gx", 16), ("af", 1), ("gx", 4), ("gx", 32), ("af", 2), ("gx", 8)]
+    preferred = [("gx", 1), ("gx", 2), ("af", 1), ("gx", 16), ("gx", 4), ("af", 2), ("gx", 32), ("gx", 8)]
     sizes = {"gx": gx_size, "af": af_size}
     steps = [(axis, bit) for axis, bit in preferred if bit < sizes[axis]]
     for axis in ("gx", "af"):

time: 91.7 us -> 91.3 us (level)
  no operation moved by 1% of the time
where the time goes in v18:
time: 91.3 us; the launch traced here: 90.5 us
  Pallas kernels  79.1 us (87%)
  local copies, waits for them, and re-layouts  5.98 us (7%)
  matrix products  3.61 us (4%)
  other arithmetic  0.99 us (1%)
    pallas_call x1, Pallas kernels, allreduce_all(): pl.pallas_call(functools.partial(allreduce_kernel, digits), out_shape=jax...  39.4 us
    pallas_call x1, Pallas kernels, core_exchange(): pl.pallas_call(functools.partial(core_kernel, cycle), out_shape=jax.Shape...  21 us
    pallas_call x1, Pallas kernels, factor_panels(): pl.pallas_call(panel_kernel, out_shape=[jax.ShapeDtypeStruct((rank, rank...  18.7 us
    unnamed x16, local copies, waits for them, and re-layouts  3.16 us
    dot_general x1, matrix products, body(): jnp.einsum('pjl,jk->plk', scalar_field, second_sketch, precision=precise)  2.16 us

profile of v18, /device:TPU:32, one launch (start us, length us, event | category | flops | bytes accessed | tf_op | source)
XLA Modules:
  0.0 90.5 jit_solution(14305605157963199661)
XLA Ops:
  0.6 0.0 copy-start
  0.6 0.8 fusion.15
  1.4 0.0 copy-start.3
  1.4 2.2 %fusion.1 = f32[256,512]{0,1:T(8,128)S(1)} fusion(f32[2,128,512]{2,1,0:T(8,128)} %field_ref.1, f32[256,2]{0,1:T(2,128)S(1)} %get-tuple-element.18, f32[128,256]{1,0:T(8,128)} %param.9), kind=kOutput, calls=%fused_computation.2 | convolution fusion | flops 403046400 | bytes 1181696 | tf_op jit(solution)/shard_map/pjl,jk->plk/dot_general | solution.py:302
  3.6 0.0 copy-done.3
  3.6 0.0 copy-start.1
  3.6 0.6 fusion.5
  4.2 0.0 copy-done
  4.2 0.4 copy-done.1
  4.6 0.6 fusion.3
  5.3 0.3 convolution_dynamic-update-slice_fusion
  5.6 0.8 pad_maximum_fusion.x_ref
  6.4 39.4 %shard_map.94.both_ref = f32[1024,128]{1,0:T(8,128)} custom-call(f32[1024,128]{1,0:T(8,128)} %pad_maximum_fusion.x_ref), custom_call_target="tpu_custom_call" | custom-call | tf_op jit(solution)/shard_map/pallas_call | solution.py:127
  45.8 18.7 %shard_map.95 = (f32[128,640]{1,0:T(8,128)}, f32[128,256]{1,0:T(8,128)}) custom-call(f32[1024,128]{1,0:T(8,128)} %shard_map.94.both_ref), custom_call_target="tpu_custom_call" | custom-call | tf_op jit(solution)/shard_map/pallas_call | solution.py:187
  64.6 0.0 copy-start.2
  64.6 0.9 slice.22
  65.4 0.1 dynamic-slice_bitcast_fusion.1
  65.5 0.6 copy.22
  66.2 0.0 copy-done.2
  66.2 0.1 dynamic-slice_bitcast_fusion
  66.3 0.0 copy-start.4
  66.3 0.0 copy-start.5
  66.3 0.6 copy.23
  67.0 0.0 copy-done.4
  67.0 0.0 copy-done.5
  67.0 0.1 constant_dynamic-slice_fusion.1
  67.1 0.1 copy.20
  67.2 0.1 copy.19
  67.3 0.1 fusion.11
  67.4 0.1 copy.21
  67.4 0.7 broadcast_in_dim.27.weights_ref
  68.1 21.0 %shard_map.96 = f32[2,32,128]{2,1,0:T(8,128)} custom-call(f32[2,128,512]{2,1,0:T(8,128)} %field_ref.1, f32[128,256]{1,0:T(8,128)} %get-tuple-element.5.left_ref, f32[128,640]{1,0:T(8,128)} %get-tuple-element.6.right_ref, f32[8,2,1,128]{3,2,1,0:T(1,128)} %broadcast_in_dim.27.weights_ref), custom_call_target="tpu_custom_call" | custom-call | tf_op jit(solution)/shard_map/pallas_call | solution.py:271
  89.1 1.4 %copy.51 = f32[2,32,128]{2,1,0:T(8,128)} copy(f32[2,32,128]{2,1,0:T(8,128)} %shard_map.96) | data formatting | bytes 65536
  (3 shorter events, 0.0 us)
Async XLA Ops:
  0.6 3.6 %copy-start = (f32[512,256]{1,0:T(8,128)S(1)}, f32[512,256]{1,0:T(8,128)}, u32[]{:S(2)}) copy-start(f32[512,256]{1,0:T(8,128)} %param.10) | copy-start | bytes 1572868
  1.4 2.2 %copy-start.3 = (f32[2,256,128]{2,1,0:T(8,128)S(1)}, f32[2,256,128]{2,1,0:T(8,128)}, u32[]{:S(2)}) copy-start(f32[2,256,128]{2,1,0:T(8,128)} %param.11) | copy-start | bytes 786436
  3.6 1.0 %copy-start.1 = (f32[2,128,512]{2,1,0:T(8,128)S(1)}, f32[2,128,512]{2,1,0:T(8,128)}, u32[]{:S(2)}) copy-start(f32[2,128,512]{2,1,0:T(8,128)} %field_ref.1) | copy-start | bytes 1572868
  64.6 1.6 %copy-start.2 = (f32[128,640]{1,0:T(8,128)S(1)}, f32[128,640]{1,0:T(8,128)}, u32[]{:S(2)}) copy-start(f32[128,640]{1,0:T(8,128)} %get-tuple-element.6.right_ref) | copy-start | bytes 983044
  66.3 0.7 copy-start.4
  66.3 0.7 copy-start.5

commit v19 on v18

--- a/solution.py
+++ b/solution.py
@@ -311,15 +311,14 @@
     both = allreduce_all(jnp.concatenate([range_second, range_third], axis=0))
 
     panel_third, panel_second = factor_panels(both, rows)
-    factor_third_all = panel_third[:, rank_cols:].T
-    basis_second = panel_second[:, rank_cols:].T
-
     out_second = full_rows // (gx_size * af_size)
     assert rows == gx_size * out_second
-    factor_second = lax.dynamic_slice_in_dim(basis_second, gx_index * out_second, out_second, 0)
+    factor_second = lax.dynamic_slice_in_dim(
+        panel_second, rank_cols + gx_index * out_second, out_second, 1
+    ).T
     factor_third = lax.dynamic_slice_in_dim(
-        factor_third_all, (gx_index * af_size + af_index) * out_second, out_second, 0
-    )
+        panel_third, rank_cols + (gx_index * af_size + af_index) * out_second, out_second, 1
+    ).T
     cycle = BLOCK // planes
     groups = gx_size // cycle
     assert planes * gx_size == BLOCKS * BLOCK and groups == BLOCKS

time: 91.3 us -> 92.7 us (1.015)
  local copies, waits for them, and re-layouts: 5.98 us -> 7.38 us
    transpose x0 -> x2, local copies, waits for them, and re-layouts: none -> 1.83 us  [the longest x1 0.91 us: body(): factor_second = lax.dynamic_slice_in_dim(panel_second, rank_cols + gx_ind...]
    unnamed x16 -> x14, local copies, waits for them, and re-layouts: 3.16 us -> 3.81 us
where the time goes in v19:
time: 92.7 us; the launch traced here: 91.9 us
  Pallas kernels  79.2 us (85%)
  local copies, waits for them, and re-layouts  7.38 us (8%)
  matrix products  3.61 us (4%)
  other arithmetic  1.01 us (1%)
    pallas_call x1, Pallas kernels, allreduce_all(): pl.pallas_call(functools.partial(allreduce_kernel, digits), out_shape=jax...  39.5 us
    pallas_call x1, Pallas kernels, core_exchange(): pl.pallas_call(functools.partial(core_kernel, cycle), out_shape=jax.Shape...  21 us
    pallas_call x1, Pallas kernels, factor_panels(): pl.pallas_call(panel_kernel, out_shape=[jax.ShapeDtypeStruct((rank, rank...  18.7 us
    unnamed x14, local copies, waits for them, and re-layouts  3.81 us
    dot_general x1, matrix products, body(): jnp.einsum('pjl,jk->plk', scalar_field, second_sketch, precision=precise)  2.16 us

profile of v19, /device:TPU:32, one launch (start us, length us, event | category | flops | bytes accessed | tf_op | source)
XLA Modules:
  0.0 91.9 jit_solution(9733605637763463413)
XLA Ops:
  0.6 0.0 copy-start
  0.6 0.8 fusion.15
  1.4 0.0 copy-start.2
  1.4 2.2 %fusion.1 = f32[256,512]{0,1:T(8,128)S(1)} fusion(f32[2,128,512]{2,1,0:T(8,128)} %field_ref.1, f32[256,2]{0,1:T(2,128)S(1)} %get-tuple-element.18, f32[128,256]{1,0:T(8,128)} %param.9), kind=kOutput, calls=%fused_computation.2 | convolution fusion | flops 403046400 | bytes 1181696 | tf_op jit(solution)/shard_map/pjl,jk->plk/dot_general | solution.py:302
  3.6 0.0 copy-done.2
  3.6 0.0 copy-start.1
  3.6 0.6 fusion.5
  4.2 0.0 copy-done
  4.2 0.4 copy-done.1
  4.6 0.6 fusion.3
  5.3 0.3 convolution_dynamic-update-slice_fusion
  5.6 0.8 pad_maximum_fusion.x_ref
  6.4 39.5 %shard_map.94.both_ref = f32[1024,128]{1,0:T(8,128)} custom-call(f32[1024,128]{1,0:T(8,128)} %pad_maximum_fusion.x_ref), custom_call_target="tpu_custom_call" | custom-call | tf_op jit(solution)/shard_map/pallas_call | solution.py:127
  45.9 18.7 %shard_map.95 = (f32[128,640]{1,0:T(8,128)}, f32[128,256]{1,0:T(8,128)}) custom-call(f32[1024,128]{1,0:T(8,128)} %shard_map.94.both_ref), custom_call_target="tpu_custom_call" | custom-call | tf_op jit(solution)/shard_map/pallas_call | solution.py:187
  64.6 0.9 dynamic-slice_bitcast_fusion.1
  65.5 0.6 copy.22
  66.1 0.9 dynamic-slice_bitcast_fusion
  67.1 0.6 copy.23
  67.7 0.0 copy-start.3
  67.7 0.0 copy-start.4
  67.7 0.7 copy-done.3
  68.4 0.0 copy-done.4
  68.4 0.1 constant_dynamic-slice_fusion.1
  68.5 0.1 copy.20
  68.6 0.1 copy.19
  68.7 0.1 fusion.11
  68.8 0.1 copy.21
  68.8 0.7 broadcast_in_dim.27.weights_ref
  69.5 21.0 %shard_map.96 = f32[2,32,128]{2,1,0:T(8,128)} custom-call(f32[2,128,512]{2,1,0:T(8,128)} %field_ref.1, f32[128,256]{1,0:T(8,128)} %get-tuple-element.5.left_ref, f32[128,640]{1,0:T(8,128)} %get-tuple-element.6.right_ref, f32[8,2,1,128]{3,2,1,0:T(1,128)} %broadcast_in_dim.27.weights_ref), custom_call_target="tpu_custom_call" | custom-call | tf_op jit(solution)/shard_map/pallas_call | solution.py:271
  90.5 1.4 %copy.51 = f32[2,32,128]{2,1,0:T(8,128)} copy(f32[2,32,128]{2,1,0:T(8,128)} %shard_map.96) | data formatting | bytes 65536
  (2 shorter events, 0.0 us)
Async XLA Ops:
  0.6 3.6 %copy-start = (f32[512,256]{1,0:T(8,128)S(1)}, f32[512,256]{1,0:T(8,128)}, u32[]{:S(2)}) copy-start(f32[512,256]{1,0:T(8,128)} %param.10) | copy-start | bytes 1572868
  1.4 2.2 %copy-start.2 = (f32[2,256,128]{2,1,0:T(8,128)S(1)}, f32[2,256,128]{2,1,0:T(8,128)}, u32[]{:S(2)}) copy-start(f32[2,256,128]{2,1,0:T(8,128)} %param.11) | copy-start | bytes 786436
  3.6 1.0 %copy-start.1 = (f32[2,128,512]{2,1,0:T(8,128)S(1)}, f32[2,128,512]{2,1,0:T(8,128)}, u32[]{:S(2)}) copy-start(f32[2,128,512]{2,1,0:T(8,128)} %field_ref.1) | copy-start | bytes 1572868
  67.7 0.7 copy-start.3
  67.7 0.7 copy-start.4

commit v20 on v18

--- a/solution.py
+++ b/solution.py
@@ -178,7 +178,7 @@
 
     span = 16
     for first in range(0, rank, span):
-        lax.fori_loop(first, first + span, functools.partial(step, first), 0, unroll=2)
+        lax.fori_loop(first, first + span, functools.partial(step, first), 0, unroll=4)
 
 
 def factor_panels(both, rows):

time: 91.3 us -> 91.1 us (level)
  no operation moved by 1% of the time
where the time goes in v20:
time: 91.1 us; the launch traced here: 90.3 us
  Pallas kernels  79 us (87%)
  local copies, waits for them, and re-layouts  5.98 us (7%)
  matrix products  3.61 us (4%)
  other arithmetic  0.99 us (1%)
    pallas_call x1, Pallas kernels, allreduce_all(): pl.pallas_call(functools.partial(allreduce_kernel, digits), out_shape=jax...  39.4 us
    pallas_call x1, Pallas kernels, core_exchange(): pl.pallas_call(functools.partial(core_kernel, cycle), out_shape=jax.Shape...  21 us
    pallas_call x1, Pallas kernels, factor_panels(): pl.pallas_call(panel_kernel, out_shape=[jax.ShapeDtypeStruct((rank, rank...  18.6 us
    unnamed x16, local copies, waits for them, and re-layouts  3.16 us
    dot_general x1, matrix products, body(): jnp.einsum('pjl,jk->plk', scalar_field, second_sketch, precision=precise)  2.16 us

profile of v20, /device:TPU:32, one launch (start us, length us, event | category | flops | bytes accessed | tf_op | source)
XLA Modules:
  0.0 90.3 jit_solution(17141124630380556527)
XLA Ops:
  0.6 0.0 copy-start
  0.6 0.8 fusion.15
  1.4 0.0 copy-start.3
  1.4 2.2 %fusion.1 = f32[256,512]{0,1:T(8,128)S(1)} fusion(f32[2,128,512]{2,1,0:T(8,128)} %field_ref.1, f32[256,2]{0,1:T(2,128)S(1)} %get-tuple-element.18, f32[128,256]{1,0:T(8,128)} %param.9), kind=kOutput, calls=%fused_computation.2 | convolution fusion | flops 403046400 | bytes 1181696 | tf_op jit(solution)/shard_map/pjl,jk->plk/dot_general | solution.py:302
  3.6 0.0 copy-done.3
  3.6 0.0 copy-start.1
  3.6 0.6 fusion.5
  4.2 0.0 copy-done
  4.2 0.4 copy-done.1
  4.6 0.6 fusion.3
  5.3 0.3 convolution_dynamic-update-slice_fusion
  5.6 0.8 pad_maximum_fusion.x_ref
  6.4 39.4 %shard_map.94.both_ref = f32[1024,128]{1,0:T(8,128)} custom-call(f32[1024,128]{1,0:T(8,128)} %pad_maximum_fusion.x_ref), custom_call_target="tpu_custom_call" | custom-call | tf_op jit(solution)/shard_map/pallas_call | solution.py:127
  45.8 18.6 %shard_map.95 = (f32[128,640]{1,0:T(8,128)}, f32[128,256]{1,0:T(8,128)}) custom-call(f32[1024,128]{1,0:T(8,128)} %shard_map.94.both_ref), custom_call_target="tpu_custom_call" | custom-call | tf_op jit(solution)/shard_map/pallas_call | solution.py:187
  64.4 0.0 copy-start.2
  64.4 0.9 slice.22
  65.3 0.1 dynamic-slice_bitcast_fusion.1
  65.4 0.6 copy.22
  66.0 0.0 copy-done.2
  66.1 0.1 dynamic-slice_bitcast_fusion
  66.2 0.0 copy-start.4
  66.2 0.0 copy-start.5
  66.2 0.6 copy.23
  66.8 0.0 copy-done.4
  66.8 0.0 copy-done.5
  66.9 0.1 constant_dynamic-slice_fusion.1
  66.9 0.1 copy.20
  67.0 0.1 copy.19
  67.1 0.1 fusion.11
  67.2 0.1 copy.21
  67.3 0.7 broadcast_in_dim.27.weights_ref
  68.0 21.0 %shard_map.96 = f32[2,32,128]{2,1,0:T(8,128)} custom-call(f32[2,128,512]{2,1,0:T(8,128)} %field_ref.1, f32[128,256]{1,0:T(8,128)} %get-tuple-element.5.left_ref, f32[128,640]{1,0:T(8,128)} %get-tuple-element.6.right_ref, f32[8,2,1,128]{3,2,1,0:T(1,128)} %broadcast_in_dim.27.weights_ref), custom_call_target="tpu_custom_call" | custom-call | tf_op jit(solution)/shard_map/pallas_call | solution.py:271
  89.0 1.4 %copy.51 = f32[2,32,128]{2,1,0:T(8,128)} copy(f32[2,32,128]{2,1,0:T(8,128)} %shard_map.96) | data formatting | bytes 65536
  (3 shorter events, 0.0 us)
Async XLA Ops:
  0.6 3.6 %copy-start = (f32[512,256]{1,0:T(8,128)S(1)}, f32[512,256]{1,0:T(8,128)}, u32[]{:S(2)}) copy-start(f32[512,256]{1,0:T(8,128)} %param.10) | copy-start | bytes 1572868
  1.4 2.2 %copy-start.3 = (f32[2,256,128]{2,1,0:T(8,128)S(1)}, f32[2,256,128]{2,1,0:T(8,128)}, u32[]{:S(2)}) copy-start(f32[2,256,128]{2,1,0:T(8,128)} %param.11) | copy-start | bytes 786436
  3.6 1.0 %copy-start.1 = (f32[2,128,512]{2,1,0:T(8,128)S(1)}, f32[2,128,512]{2,1,0:T(8,128)}, u32[]{:S(2)}) copy-start(f32[2,128,512]{2,1,0:T(8,128)} %field_ref.1) | copy-start | bytes 1572868
  64.4 1.6 %copy-start.2 = (f32[128,640]{1,0:T(8,128)S(1)}, f32[128,640]{1,0:T(8,128)}, u32[]{:S(2)}) copy-start(f32[128,640]{1,0:T(8,128)} %get-tuple-element.6.right_ref) | copy-start | bytes 983044
  66.2 0.7 copy-start.4
  66.2 0.7 copy-start.5

commit v21 on v20

--- a/solution.py
+++ b/solution.py
@@ -29,7 +29,7 @@
     return steps
 
 
-def allreduce_kernel(digits, x_ref, o_ref, acc, recv, exchange, gathered, send_sem, recv_sem):
+def allreduce_kernel(digits, x_ref, third_ref, second_ref, acc, recv, exchange, gathered, send_sem, recv_sem):
     index = {"gx": lax.axis_index("gx"), "af": lax.axis_index("af")}
 
     def bits_of(digit):
@@ -113,10 +113,12 @@
         for copy in copies:
             copy.wait()
         offset, length = parent_offset, parent_length
-    o_ref[...] = gathered[...]
-
-
-def allreduce_all(x):
+    panel_kernel(gathered, third_ref, second_ref)
+
+
+def allreduce_all(x, rows):
+    rank = x.shape[1]
+    half = x.shape[0] // 2
     steps = partner_list(lax.axis_size("gx"), lax.axis_size("af"))
     digits = [steps[t:t + 3] for t in range(0, len(steps), 3)]
     last_rows = x.shape[0]
@@ -126,9 +128,12 @@
     copies = sum(2 * (2 ** len(digit) - 1) for digit in digits[:-1]) + 2 ** len(digits[-1]) - 1
     return pl.pallas_call(
         functools.partial(allreduce_kernel, digits),
-        out_shape=jax.ShapeDtypeStruct(x.shape, x.dtype),
+        out_shape=[
+            jax.ShapeDtypeStruct((rank, rank + half), x.dtype),
+            jax.ShapeDtypeStruct((rank, rank + rows), x.dtype),
+        ],
         in_specs=[pl.BlockSpec(memory_space=pltpu.VMEM)],
-        out_specs=pl.BlockSpec(memory_space=pltpu.VMEM),
+        out_specs=[pl.BlockSpec(memory_space=pltpu.VMEM)] * 2,
         scratch_shapes=[
             pltpu.VMEM(x.shape, x.dtype),
             pltpu.VMEM(x.shape, x.dtype),
@@ -181,20 +186,6 @@
         lax.fori_loop(first, first + span, functools.partial(step, first), 0, unroll=4)
 
 
-def factor_panels(both, rows):
-    rank = both.shape[1]
-    half = both.shape[0] // 2
-    return pl.pallas_call(
-        panel_kernel,
-        out_shape=[
-            jax.ShapeDtypeStruct((rank, rank + half), both.dtype),
-            jax.ShapeDtypeStruct((rank, rank + rows), both.dtype),
-        ],
-        in_specs=[pl.BlockSpec(memory_space=pltpu.VMEM)],
-        out_specs=[pl.BlockSpec(memory_space=pltpu.VMEM)] * 2,
-    )(both)
-
-
 def core_kernel(
     cycle, field_ref, left_ref, right_ref, weights_ref, o_ref,
     pieces_ref, first, staged, second, send_sem, recv_sem,
@@ -308,9 +299,9 @@
     range_second = lax.dynamic_update_slice_in_dim(
         jnp.zeros((full_rows, rank_cols), jnp.float32), range_second_block, af_index * rows, 0
     )
-    both = allreduce_all(jnp.concatenate([range_second, range_third], axis=0))
-
-    panel_third, panel_second = factor_panels(both, rows)
+    panel_third, panel_second = allreduce_all(
+        jnp.concatenate([range_second, range_third], axis=0), rows
+    )
     factor_third_all = panel_third[:, rank_cols:].T
     basis_second = panel_second[:, rank_cols:].T
 

time: 91.1 us -> 89.2 us (0.979)
  Pallas kernels: 79 us -> 77.2 us
    pallas_call x2 -> x1, Pallas kernels: 58 us -> 56.2 us  [allreduce_all(): pl.pallas_call(functools.partial(allreduce_kernel, digits), out_shape=[ja...]
where the time goes in v21:
time: 89.2 us; the launch traced here: 88.5 us
  Pallas kernels  77.2 us (87%)
  local copies, waits for them, and re-layouts  5.98 us (7%)
  matrix products  3.61 us (4%)
  other arithmetic  0.98 us (1%)
    pallas_call x1, Pallas kernels, allreduce_all(): pl.pallas_call(functools.partial(allreduce_kernel, digits), out_shape=[ja...  56.2 us
    pallas_call x1, Pallas kernels, core_exchange(): pl.pallas_call(functools.partial(core_kernel, cycle), out_shape=jax.Shape...  21 us
    unnamed x16, local copies, waits for them, and re-layouts  3.16 us
    dot_general x1, matrix products, body(): jnp.einsum('pjl,jk->plk', scalar_field, second_sketch, precision=precise)  2.16 us

profile of v21, /device:TPU:32, one launch (start us, length us, event | category | flops | bytes accessed | tf_op | source)
XLA Modules:
  0.0 88.5 jit_solution(12762931633453152987)
XLA Ops:
  0.6 0.0 copy-start
  0.6 0.8 fusion.15
  1.4 0.0 copy-start.3
  1.4 2.2 %fusion.1 = f32[256,512]{0,1:T(8,128)S(1)} fusion(f32[2,128,512]{2,1,0:T(8,128)} %field_ref.1, f32[256,2]{0,1:T(2,128)S(1)} %get-tuple-element.18, f32[128,256]{1,0:T(8,128)} %param.9), kind=kOutput, calls=%fused_computation.2 | convolution fusion | flops 403046400 | bytes 1181696 | tf_op jit(solution)/shard_map/pjl,jk->plk/dot_general | solution.py:293
  3.6 0.0 copy-done.3
  3.6 0.0 copy-start.1
  3.6 0.6 fusion.5
  4.2 0.0 copy-done
  4.2 0.4 copy-done.1
  4.6 0.6 fusion.3
  5.3 0.3 convolution_dynamic-update-slice_fusion
  5.6 0.8 pad_maximum_fusion.x_ref
  6.4 56.2 %shard_map.94 = (f32[128,640]{1,0:T(8,128)}, f32[128,256]{1,0:T(8,128)}) custom-call(f32[1024,128]{1,0:T(8,128)} %pad_maximum_fusion.x_ref), custom_call_target="tpu_custom_call" | custom-call | tf_op jit(solution)/shard_map/pallas_call | solution.py:129
  62.5 0.0 copy-start.2
  62.6 0.9 %slice.22 = f32[128,128]{1,0:T(8,128)S(1)} slice(f32[128,256]{1,0:T(8,128)} %get-tuple-element.5.left_ref), slice={[0:128], [128:256]} | slice | bytes 131072 | tf_op jit(solution)/shard_map/slice | solution.py:306
  63.5 0.1 dynamic-slice_bitcast_fusion.1
  63.5 0.6 copy.22
  64.2 0.0 copy-done.2
  64.2 0.1 dynamic-slice_bitcast_fusion
  64.3 0.0 copy-start.4
  64.3 0.0 copy-start.5
  64.3 0.6 copy.23
  65.0 0.0 copy-done.4
  65.0 0.0 copy-done.5
  65.0 0.1 constant_dynamic-slice_fusion.1
  65.1 0.1 copy.20
  65.2 0.1 copy.19
  65.3 0.1 fusion.11
  65.4 0.1 copy.21
  65.4 0.7 broadcast_in_dim.27.weights_ref
  66.1 21.0 %shard_map.95 = f32[2,32,128]{2,1,0:T(8,128)} custom-call(f32[2,128,512]{2,1,0:T(8,128)} %field_ref.1, f32[128,256]{1,0:T(8,128)} %get-tuple-element.5.left_ref, f32[128,640]{1,0:T(8,128)} %get-tuple-element.6.right_ref, f32[8,2,1,128]{3,2,1,0:T(1,128)} %broadcast_in_dim.27.weights_ref), custom_call_target="tpu_custom_call" | custom-call | tf_op jit(solution)/shard_map/pallas_call | solution.py:262
  87.1 1.4 %copy.51 = f32[2,32,128]{2,1,0:T(8,128)} copy(f32[2,32,128]{2,1,0:T(8,128)} %shard_map.95) | data formatting | bytes 65536
  (3 shorter events, 0.0 us)
Async XLA Ops:
  0.6 3.6 %copy-start = (f32[512,256]{1,0:T(8,128)S(1)}, f32[512,256]{1,0:T(8,128)}, u32[]{:S(2)}) copy-start(f32[512,256]{1,0:T(8,128)} %param.10) | copy-start | bytes 1572868
  1.4 2.2 %copy-start.3 = (f32[2,256,128]{2,1,0:T(8,128)S(1)}, f32[2,256,128]{2,1,0:T(8,128)}, u32[]{:S(2)}) copy-start(f32[2,256,128]{2,1,0:T(8,128)} %param.11) | copy-start | bytes 786436
  3.6 1.0 %copy-start.1 = (f32[2,128,512]{2,1,0:T(8,128)S(1)}, f32[2,128,512]{2,1,0:T(8,128)}, u32[]{:S(2)}) copy-start(f32[2,128,512]{2,1,0:T(8,128)} %field_ref.1) | copy-start | bytes 1572868
  62.5 1.6 %copy-start.2 = (f32[128,640]{1,0:T(8,128)S(1)}, f32[128,640]{1,0:T(8,128)}, u32[]{:S(2)}) copy-start(f32[128,640]{1,0:T(8,128)} %get-tuple-element.6.right_ref) | copy-start | bytes 983044
  64.3 0.7 copy-start.4
  64.3 0.7 copy-start.5

commit v22 on v21

--- a/solution.py
+++ b/solution.py
@@ -29,7 +29,11 @@
     return steps
 
 
-def allreduce_kernel(digits, x_ref, third_ref, second_ref, acc, recv, exchange, gathered, send_sem, recv_sem):
+def allreduce_kernel(
+    digits, cycle, x_ref, field_ref, weights_ref, third_ref, second_ref, core_ref,
+    acc, recv, exchange, gathered, send_sem, recv_sem,
+    pieces, first, staged, second, core_send, core_recv,
+):
     index = {"gx": lax.axis_index("gx"), "af": lax.axis_index("af")}
 
     def bits_of(digit):
@@ -56,7 +60,13 @@
     for digit in digits:
         for d in others(digit):
             pl.semaphore_signal(barrier, inc=1, device_id=device(digit, d), device_id_type=MESH)
-    pl.semaphore_wait(barrier, sum(len(others(digit)) for digit in digits))
+    quarters, blocks = pieces.shape[0], weights_ref.shape[0]
+    k, c = index["gx"] // cycle, index["gx"] % cycle
+    core_devices = [(index["gx"], (index["af"] + d) % quarters) for d in range(1, quarters)]
+    core_devices += [(((k + d) % blocks) * cycle + c, index["af"]) for d in range(1, blocks)]
+    for core_device in core_devices:
+        pl.semaphore_signal(barrier, inc=1, device_id=core_device, device_id_type=MESH)
+    pl.semaphore_wait(barrier, sum(len(others(digit)) for digit in digits) + len(core_devices))
 
     counter = [0]
 
@@ -114,9 +124,14 @@
             copy.wait()
         offset, length = parent_offset, parent_length
     panel_kernel(gathered, third_ref, second_ref)
-
-
-def allreduce_all(x, rows):
+    core_kernel(
+        cycle, field_ref, second_ref, third_ref, weights_ref, core_ref,
+        pieces, first, staged, second, core_send, core_recv, enter=False,
+    )
+
+
+def allreduce_all(x, rows, field, weights, cycle, quarters):
+    planes, blocks = field.shape[0], weights.shape[0]
     rank = x.shape[1]
     half = x.shape[0] // 2
     steps = partner_list(lax.axis_size("gx"), lax.axis_size("af"))
@@ -126,14 +141,16 @@
         last_rows //= 2 ** len(digit)
     assert last_rows % 8 == 0
     copies = sum(2 * (2 ** len(digit) - 1) for digit in digits[:-1]) + 2 ** len(digits[-1]) - 1
+    piece = (planes, rank // quarters, rank)
     return pl.pallas_call(
-        functools.partial(allreduce_kernel, digits),
+        functools.partial(allreduce_kernel, digits, cycle),
         out_shape=[
             jax.ShapeDtypeStruct((rank, rank + half), x.dtype),
             jax.ShapeDtypeStruct((rank, rank + rows), x.dtype),
+            jax.ShapeDtypeStruct(piece, x.dtype),
         ],
-        in_specs=[pl.BlockSpec(memory_space=pltpu.VMEM)],
-        out_specs=[pl.BlockSpec(memory_space=pltpu.VMEM)] * 2,
+        in_specs=[pl.BlockSpec(memory_space=pltpu.VMEM)] * 3,
+        out_specs=[pl.BlockSpec(memory_space=pltpu.VMEM)] * 3,
         scratch_shapes=[
             pltpu.VMEM(x.shape, x.dtype),
             pltpu.VMEM(x.shape, x.dtype),
@@ -141,9 +158,15 @@
             pltpu.VMEM(x.shape, x.dtype),
             pltpu.SemaphoreType.DMA((copies,)),
             pltpu.SemaphoreType.DMA((copies,)),
+            pltpu.VMEM((quarters,) + piece, x.dtype),
+            pltpu.VMEM((quarters - 1,) + piece, x.dtype),
+            pltpu.VMEM((blocks,) + piece, x.dtype),
+            pltpu.VMEM((blocks - 1,) + piece, x.dtype),
+            pltpu.SemaphoreType.DMA((quarters + blocks - 2,)),
+            pltpu.SemaphoreType.DMA((quarters + blocks - 2,)),
         ],
         compiler_params=pltpu.CompilerParams(collective_id=0, has_side_effects=True),
-    )(x)
+    )(x, field, weights)
 
 
 def panel_kernel(both_ref, third_ref, second_ref):
@@ -188,7 +211,7 @@
 
 def core_kernel(
     cycle, field_ref, left_ref, right_ref, weights_ref, o_ref,
-    pieces_ref, first, staged, second, send_sem, recv_sem,
+    pieces_ref, first, staged, second, send_sem, recv_sem, enter=True,
 ):
     g = lax.axis_index("gx")
     a = lax.axis_index("af")
@@ -217,10 +240,11 @@
     def owner(j):
         return (j * cycle + c, a)
 
-    barrier = pltpu.get_barrier_semaphore()
-    for device in [peer(j) for j in peers] + [owner(j) for j in owners]:
-        pl.semaphore_signal(barrier, inc=1, device_id=device, device_id_type=MESH)
-    pl.semaphore_wait(barrier, len(peers) + len(owners))
+    if enter:
+        barrier = pltpu.get_barrier_semaphore()
+        for device in [peer(j) for j in peers] + [owner(j) for j in owners]:
+            pl.semaphore_signal(barrier, inc=1, device_id=device, device_id_type=MESH)
+        pl.semaphore_wait(barrier, len(peers) + len(owners))
 
     def start(n, source, target, device):
         copy = pltpu.make_async_remote_copy(
@@ -299,18 +323,6 @@
     range_second = lax.dynamic_update_slice_in_dim(
         jnp.zeros((full_rows, rank_cols), jnp.float32), range_second_block, af_index * rows, 0
     )
-    panel_third, panel_second = allreduce_all(
-        jnp.concatenate([range_second, range_third], axis=0), rows
-    )
-    factor_third_all = panel_third[:, rank_cols:].T
-    basis_second = panel_second[:, rank_cols:].T
-
-    out_second = full_rows // (gx_size * af_size)
-    assert rows == gx_size * out_second
-    factor_second = lax.dynamic_slice_in_dim(basis_second, gx_index * out_second, out_second, 0)
-    factor_third = lax.dynamic_slice_in_dim(
-        factor_third_all, (gx_index * af_size + af_index) * out_second, out_second, 0
-    )
     cycle = BLOCK // planes
     groups = gx_size // cycle
     assert planes * gx_size == BLOCKS * BLOCK and groups == BLOCKS
@@ -323,8 +335,18 @@
         axis=2,
     )
     lane_weights = jnp.broadcast_to(weights[:, :, None, None], (groups, planes, 1, rank_cols))
-    core_sketch = core_exchange(
-        scalar_field, panel_second, panel_third, lane_weights, cycle, af_size
+    panel_third, panel_second, core_sketch = allreduce_all(
+        jnp.concatenate([range_second, range_third], axis=0), rows,
+        scalar_field, lane_weights, cycle, af_size,
+    )
+    factor_third_all = panel_third[:, rank_cols:].T
+    basis_second = panel_second[:, rank_cols:].T
+
+    out_second = full_rows // (gx_size * af_size)
+    assert rows == gx_size * out_second
+    factor_second = lax.dynamic_slice_in_dim(basis_second, gx_index * out_second, out_second, 0)
+    factor_third = lax.dynamic_slice_in_dim(
+        factor_third_all, (gx_index * af_size + af_index) * out_second, out_second, 0
     )
     return (factor_second, factor_third, core_sketch)
 

time: 89.2 us -> 85.4 us (0.957)
  Pallas kernels: 77.2 us -> 73.5 us
    pallas_call x2 -> x1, Pallas kernels: 77.2 us -> 73.5 us  [allreduce_all(): pl.pallas_call(functools.partial(allreduce_kernel, digits, cycle), out_sh...]
    unnamed x16 -> x18, local copies, waits for them, and re-layouts: 3.16 us -> 3.16 us
where the time goes in v22:
time: 85.4 us; the launch traced here: 84.8 us
  Pallas kernels  73.5 us (86%)
  local copies, waits for them, and re-layouts  5.98 us (7%)
  matrix products  3.61 us (4%)
  other arithmetic  0.99 us (1%)
    pallas_call x1, Pallas kernels, allreduce_all(): pl.pallas_call(functools.partial(allreduce_kernel, digits, cycle), out_sh...  73.5 us
    unnamed x18, local copies, waits for them, and re-layouts  3.16 us
    dot_general x1, matrix products, body(): jnp.einsum('pjl,jk->plk', scalar_field, second_sketch, precision=precise)  2.16 us

profile of v22, /device:TPU:32, one launch (start us, length us, event | category | flops | bytes accessed | tf_op | source)
XLA Modules:
  0.0 84.8 jit_solution(12372579941299229334)
XLA Ops:
  0.6 0.0 copy-start
  0.6 0.8 fusion.15
  1.4 0.0 copy-start.2
  1.4 2.2 %fusion.1 = f32[256,512]{0,1:T(8,128)S(1)} fusion(f32[2,128,512]{2,1,0:T(8,128)} %field_ref.1, f32[256,2]{0,1:T(2,128)S(1)} %get-tuple-element.20, f32[128,256]{1,0:T(8,128)} %param.9), kind=kOutput, calls=%fused_computation.2 | convolution fusion | flops 403046400 | bytes 1181696 | tf_op jit(solution)/shard_map/pjl,jk->plk/dot_general | solution.py:317
  3.6 0.0 copy-done.2
  3.6 0.0 copy-start.1
  3.6 0.6 fusion.5
  4.2 0.0 copy-done
  4.2 0.4 copy-done.1
  4.6 0.6 fusion.3
  5.3 0.3 convolution_dynamic-update-slice_fusion
  5.6 0.8 pad_maximum_fusion.x_ref
  6.4 0.0 copy-start.5
  6.4 0.0 copy-start.6
  6.4 0.7 copy-done.5
  7.1 0.0 copy-done.6
  7.1 0.1 constant_dynamic-slice_fusion.1
  7.2 0.1 copy.20
  7.2 0.1 copy.19
  7.3 0.1 fusion.11
  7.4 0.1 copy.21
  7.5 0.7 broadcast_in_dim.27.weights_ref
  8.2 73.5 %shard_map.94 = (f32[128,640]{1,0:T(8,128)}, f32[128,256]{1,0:T(8,128)}, f32[2,32,128]{2,1,0:T(8,128)}) custom-call(f32[1024,128]{1,0:T(8,128)} %pad_maximum_fusion.x_ref, f32[2,128,512]{2,1,0:T(8,128)} %field_ref.1, f32[8,2,1,128]{3,2,1,0:T(1,128)} %broadcast_in_dim.27.weights_ref), custom_call_target="tpu_custom_call" | custom-call | tf_op jit(solution)/shard_map/pallas_call | solution.py:145
  81.7 0.0 copy-start.3
  81.7 0.9 %slice.22 = f32[128,128]{1,0:T(8,128)S(1)} slice(f32[128,256]{1,0:T(8,128)} %get-tuple-element.6), slice={[0:128], [128:256]} | slice | bytes 131072 | tf_op jit(solution)/shard_map/slice | solution.py:343
  82.6 0.1 dynamic-slice_bitcast_fusion.1
  82.7 0.6 copy.22
  83.3 0.0 copy-done.3
  83.4 0.1 dynamic-slice_bitcast_fusion
  83.5 0.0 copy-start.4
  83.5 0.6 copy.23
  84.1 0.1 copy-done.4
  84.2 0.6 copy.51
  (3 shorter events, 0.0 us)
Async XLA Ops:
  0.6 3.6 %copy-start = (f32[512,256]{1,0:T(8,128)S(1)}, f32[512,256]{1,0:T(8,128)}, u32[]{:S(2)}) copy-start(f32[512,256]{1,0:T(8,128)} %param.10) | copy-start | bytes 1572868
  1.4 2.2 %copy-start.2 = (f32[2,256,128]{2,1,0:T(8,128)S(1)}, f32[2,256,128]{2,1,0:T(8,128)}, u32[]{:S(2)}) copy-start(f32[2,256,128]{2,1,0:T(8,128)} %param.11) | copy-start | bytes 786436
  3.6 1.0 %copy-start.1 = (f32[2,128,512]{2,1,0:T(8,128)S(1)}, f32[2,128,512]{2,1,0:T(8,128)}, u32[]{:S(2)}) copy-start(f32[2,128,512]{2,1,0:T(8,128)} %field_ref.1) | copy-start | bytes 1572868
  6.4 0.7 copy-start.5
  6.4 0.7 copy-start.6
  81.7 1.6 %copy-start.3 = (f32[128,640]{1,0:T(8,128)S(1)}, f32[128,640]{1,0:T(8,128)}, u32[]{:S(2)}) copy-start(f32[128,640]{1,0:T(8,128)} %get-tuple-element.7) | copy-start | bytes 983044
  83.5 0.8 copy-start.4
